TPU v7x, 32 devices: a whole 2x2x4 slice. The times are simulated.
32 devices in a mesh: gx: 8 (over z, y), gy: 4 (over x, core).
Axes of the slice: x: 2, y: 2, z: 4, core: 2. Of those that a mesh axis runs over, the one named last changes fastest.
Arguments:
- density: float32 [4, 128, 512], P(None, 'gx', 'gy'), may hold values from 0 to 1
- tile_mask: int32 [16, 64], P('gx', 'gy'), may hold values 0 or 1
- material: int32 [8, 128, 512], P(None, 'gx', 'gy'), may hold values from 0 to 3
- material_table: float32 [3, 4], replicated, may hold values from 1 to 4
- contrast: float32 [3], replicated, may hold values from 1 to 3
- electric: float32 [3, 8, 128, 512], P(None, None, 'gx', 'gy'), may hold values from -6 to 6
- magnetic: float32 [3, 8, 128, 512], P(None, None, 'gx', 'gy'), may hold values from -6 to 6
- forward_fields: bfloat16 [4, 3, 8, 128, 512], P(None, None, None, 'gx', 'gy'), may hold values from -6 to 6
Outputs:
- electric_final: float32 [3, 8, 128, 512], P(None, None, 'gx', 'gy')
- magnetic_final: float32 [3, 8, 128, 512], P(None, None, 'gx', 'gy')
- design_gradient: float32 [4, 128, 512], P(None, 'gx', 'gy')
All inputs are finite; a program needn't handle non-finite values. No bound on the sum of `tile_mask` on one device may be relied on, other than what follows from the above.
Results may differ from a plain program's by a relative error of at most 0.00065.
Values sent between devices are 32-bit elements; how exact they have to be, the bound alone decides.
No kernel may reach another device: no remote copies, remote signals or barrier semaphores. Data moves between devices by JAX's collectives and lax.ppermute only.
A program may use at most 64 MiB of HBM per device.

v0:
```python
import jax
import jax.numpy as jnp
from jax import lax
from jax.sharding import PartitionSpec as P

CY = 128
Z = 8
DZ = 4
STEPS = 4
TILE = 8
MATS = 4


courant = 0.5
sharpness = 4.0
threshold = 0.5


def passed_along(x, axis, by):
    size = lax.axis_size(axis)
    return lax.ppermute(x, axis, [(i, (i + by) % size) for i in range(size)])


def kernel_weights(source, target, count, reach):
    offsets = target[None, :] - source[:, None]
    ahead = jnp.mod(offsets, count).astype(jnp.float32)
    behind = jnp.mod(-offsets, count).astype(jnp.float32)
    return jnp.exp(-ahead / reach) + jnp.exp(-behind / reach)


def project(values):
    bottom = jnp.tanh(sharpness * threshold) + jnp.tanh(sharpness * (1.0 - threshold))
    level = jnp.tanh(sharpness * (values - threshold))
    return (
        (jnp.tanh(sharpness * threshold) + level) / bottom,
        sharpness * (1.0 - level * level) / bottom,
    )


def inverse_permittivity(projected, cell_mask, material, material_table, contrast):
    layered = jnp.repeat(projected, Z // DZ, axis=0)
    design = cell_mask[None] * layered
    result = []
    for channel in range(3):
        background = jnp.zeros(material.shape, jnp.float32)
        for index in range(MATS):
            background = background + jnp.where(
                material == index, material_table[channel, index], 0.0
            )
        result.append(1.0 / (background + design * contrast[channel]))
    return jnp.stack(result)


def ahead_x(values):
    return (values[:, 1:, :] - values[:, :-1, :])[:, :, :-1]


def ahead_y(values):
    return (values[:, :, 1:] - values[:, :, :-1])[:, :-1, :]


def ahead_z(values):
    return (jnp.concatenate([values[1:], jnp.zeros_like(values[:1])], 0) - values)[:, :-1, :-1]


def behind_x(values):
    return (values[:, 1:, :] - values[:, :-1, :])[:, :, 1:]


def behind_y(values):
    return (values[:, :, 1:] - values[:, :, :-1])[:, 1:, :]


def behind_z(values):
    return (values - jnp.concatenate([jnp.zeros_like(values[:1]), values[:-1]], 0))[:, 1:, 1:]


def curl_ahead(field):
    part_x, part_y, part_z = (field[0], field[1], field[2])
    return jnp.stack(
        [
            ahead_y(part_z) - ahead_z(part_y),
            ahead_z(part_x) - ahead_x(part_z),
            ahead_x(part_y) - ahead_y(part_x),
        ]
    )


def curl_behind(field):
    part_x, part_y, part_z = (field[0], field[1], field[2])
    return jnp.stack(
        [
            behind_y(part_z) - behind_z(part_y),
            behind_z(part_x) - behind_x(part_z),
            behind_x(part_y) - behind_y(part_x),
        ]
    )


def upper_frame(field, row_edge, column_edge):
    planes = field.shape[1]
    row_full = jnp.concatenate([jnp.zeros_like(row_edge[:1]), row_edge], 0)
    widened = jnp.concatenate([field, row_full], 2)
    column_full = jnp.stack([column_edge[0], jnp.zeros_like(column_edge[0]), column_edge[1]])
    column_full = jnp.concatenate([column_full, jnp.zeros((3, planes, 1, 1), field.dtype)], 2)
    return jnp.concatenate([widened, column_full], 3)


def lower_frame(field, row_edge, column_edge):
    planes = field.shape[1]
    row_full = jnp.concatenate([jnp.zeros_like(row_edge[:1]), row_edge], 0)
    widened = jnp.concatenate([row_full, field], 2)
    column_full = jnp.stack([column_edge[0], jnp.zeros_like(column_edge[0]), column_edge[1]])
    column_full = jnp.concatenate([jnp.zeros((3, planes, 1, 1), field.dtype), column_full], 2)
    return jnp.concatenate([column_full, widened], 3)


def accumulate(gained, contrast, electric, forward_step):
    return gained + jnp.sum(
        contrast[:, None, None, None] * electric * forward_step.astype(jnp.float32), axis=0
    )


def body(
    density, tile_mask, material, material_table, contrast, electric, magnetic, forward_fields
):
    column_count = density.shape[2]
    row_count = density.shape[1]
    devices_y = lax.axis_size("gy")
    count = column_count * devices_y
    reach = 4.0 * CY
    own_block = lax.axis_index("gy")
    local_index = jnp.arange(column_count, dtype=jnp.int32)
    mine = own_block * column_count + local_index
    panel_piece = lax.all_gather(density, "gy", axis=2, tiled=True)
    span_width = panel_piece.shape[2]
    source = jnp.arange(span_width, dtype=jnp.int32)
    weights = kernel_weights(source, mine, count, reach)
    product = jnp.dot(
        panel_piece.reshape(-1, span_width),
        weights,
        precision=lax.Precision.HIGHEST,
        preferred_element_type=jnp.float32,
    )
    smooth = product.reshape(jnp.zeros(density.shape, jnp.float32).shape)
    norm_total = 2.0 * jnp.sum(
        jnp.exp(-jnp.arange(count, dtype=jnp.int32).astype(jnp.float32) / reach)
    )
    filtered = 0.5 * density + 0.5 * smooth / norm_total
    projected, slope = project(filtered)
    cell_mask = jnp.repeat(jnp.repeat(tile_mask, TILE, 0), TILE, 1).astype(jnp.float32)
    inverse = inverse_permittivity(projected, cell_mask, material, material_table, contrast)
    gained = jnp.zeros(material.shape, jnp.float32)
    for step in range(STEPS):
        next_rows = passed_along(electric[1:, :, :1, :], "gx", -1)
        next_columns = passed_along(electric[0::2, :, :, :1], "gy", -1)
        magnetic = magnetic - courant * curl_ahead(upper_frame(electric, next_rows, next_columns))
        prior_rows = passed_along(magnetic[1:, :, -1:, :], "gx", 1)
        prior_columns = passed_along(magnetic[0::2, :, :, -1:], "gy", 1)
        electric = electric + courant * inverse * curl_behind(
            lower_frame(magnetic, prior_rows, prior_columns)
        )
        gained = accumulate(gained, contrast, electric, forward_fields[step])
    layered = gained.reshape(DZ, Z // DZ, row_count, column_count).sum(axis=1)
    design_gradient = cell_mask[None] * slope * layered
    return (electric, magnetic, design_gradient)


def solution(mesh):
    return jax.shard_map(
        body,
        mesh=mesh,
        in_specs=(
            P(None, "gx", "gy"),
            P("gx", "gy"),
            P(None, "gx", "gy"),
            P(),
            P(),
            P(None, None, "gx", "gy"),
            P(None, None, "gx", "gy"),
            P(None, None, None, "gx", "gy"),
        ),
        out_specs=(P(None, None, "gx", "gy"), P(None, None, "gx", "gy"), P(None, "gx", "gy")),
        check_vma=False,
    )
```

profile of v0, /device:TPU:0, one launch (start us, length us, event | category | flops | bytes accessed | tf_op | source)
XLA Modules:
  0.0 81.1 jit_solution(11006217435610323451)
XLA Ops:
  0.6 1.0 %slice.689 = f32[2,8,16,1]{3,2,1,0:T(8,128)S(1)} slice(f32[3,8,16,128]{3,2,1,0:T(8,128)} %param.13), slice={[0:3:2], [0:8:1], [0:16:1], [0:1:1]} | slice | bytes 2048 | tf_op jit(solution)/shard_map/slice | solution.py:156
  1.8 2.4 %collective-permute-start.1 = (f32[2,8,16,1]{2,1,3,0:T(8,128)S(1)}, f32[2,8,16,1]{2,1,3,0:T(8,128)S(1)}, u32[]{:S(2)}, u32[]{:S(2)}) collective-permute-start(f32[2,8,16,1]{2,1,3,0:T(8,128)S(1)} %copy.276), channel_id=1, source_target_pairs={{0,3},{1,0},{2,1},{3,2},{4,7},{5,4},{6,5},{7,6},{8,11},{9,8},{10,9... | collective-permute-start | bytes 3080 | tf_op jit(solution)/shard_map/ppermute | solution.py:21
  4.3 4.6 %collective-permute-start = (f32[2,8,1,128]{3,1,2,0:T(8,128)S(1)}, f32[2,8,1,128]{3,1,2,0:T(8,128)S(1)}, u32[]{:S(2)}, u32[]{:S(2)}) collective-permute-start(f32[2,8,1,128]{3,1,2,0:T(8,128)S(1)} %slice.892), channel_id=1, source_target_pairs={{0,28},{4,0},{8,4},{12,8},{16,12},{20,16},{24,20},{28,24},{1,29},{... | collective-permute-start | bytes 24584 | tf_op jit(solution)/shard_map/ppermute | solution.py:21
  12.5 5.4 %all_gather.3 = f32[4,16,512]{2,1,0:T(8,128)S(1)} all-gather(f32[4,16,128]{2,1,0:T(8,128)S(1)} %copy-done.3), channel_id=1, replica_groups=mesh['gx'=8,'gy'=4] {'gy'}, dimensions={2}, use_global_device_ids=true | all-gather | bytes 163840 | tf_op jit(solution)/shard_map/all_gather | solution.py:135
  19.9 3.3 %fusion.97 = (f32[8,16,128]{2,1,0:T(8,128)S(1)}, pred[8,16,128]{2,1,0:T(8,128)(4,1)S(1)}, pred[8,16,128]{2,1,0:T(8,128)(4,1)S(1)}, pred[8,16,128]{2,1,0:T(8,128)(4,1)S(1)}, pred[8,16,128]{2,1,0:T(8,128)(4,1)S(1)}) fusion(f32[]{:T(128)} %bitcast.10, f32[4,16,128]{2,1,0:T(8,128)S(1)} %add_multiply_fusion, f32[16,128]{1,0:T(8,128)S(1)} %copy.231, f32[]{:T(128)} %bitcast.3, ...), kind=kLoop, calls=%fused_computation.228 | loop fusion | flops 245760 | bytes 237588 | tf_op jit(solution)/shard_map/div | solution.py:50
  23.2 6.3 %fusion.99 = (f32[8,16,128]{2,1,0:T(8,128)S(1)}, f32[8,16,128]{2,1,0:T(8,128)S(1)}) fusion(pred[8,16,128]{2,1,0:T(8,128)(4,1)S(1)} %get-tuple-element.27, pred[8,16,128]{2,1,0:T(8,128)(4,1)S(1)} %get-tuple-element.26, pred[8,16,128]{2,1,0:T(8,128)(4,1)S(1)} %get-tuple-element.25, pred[8,16,128]{2,1,0:T(8,128)(4,1)S(1)} %get-tuple-element.24, f32[]{:T(128)} %bitcast.16, ...), kind=kLoop, calls=%fused_computation.230 | loop fusion | flops 344064 | bytes 237608 | tf_op jit(solution)/shard_map/div | solution.py:50
  30.3 0.9 %copy-done = f32[3,8,16,128]{3,2,1,0:T(8,128)S(1)} copy-done((f32[3,8,16,128]{3,2,1,0:T(8,128)S(1)}, f32[3,8,16,128]{3,2,1,0:T(8,128)}, u32[]{:S(2)}) %copy-start) | copy-done | bytes 196632
  31.8 4.0 %collective-permute-done.2 = f32[2,8,16,1]{3,1,2,0:T(8,128)S(1)} collective-permute-done((f32[2,8,16,1]{3,1,2,0:T(8,128)S(1)}, f32[2,8,16,1]{3,1,2,0:T(8,128)S(1)}, u32[]{:S(2)}, u32[]{:S(2)}) %collective-permute-start.2) | collective-permute-done | bytes 1056 | tf_op jit(solution)/shard_map/ppermute | solution.py:21
  36.3 1.8 %collective-permute-done.3 = f32[2,8,1,128]{3,1,2,0:T(8,128)S(1)} collective-permute-done((f32[2,8,1,128]{3,1,2,0:T(8,128)S(1)}, f32[2,8,1,128]{3,1,2,0:T(8,128)S(1)}, u32[]{:S(2)}, u32[]{:S(2)}) %collective-permute-start.3) | collective-permute-done | bytes 8224 | tf_op jit(solution)/shard_map/ppermute | solution.py:21
  39.5 2.5 %collective-permute-done.5 = f32[2,8,16,1]{3,1,2,0:T(8,128)S(1)} collective-permute-done((f32[2,8,16,1]{3,1,2,0:T(8,128)S(1)}, f32[2,8,16,1]{3,1,2,0:T(8,128)S(1)}, u32[]{:S(2)}, u32[]{:S(2)}) %collective-permute-start.5) | collective-permute-done | bytes 1056 | tf_op jit(solution)/shard_map/ppermute | solution.py:21
  44.0 4.2 %collective-permute-done.6 = f32[2,8,16,1]{3,1,2,0:T(8,128)S(1)} collective-permute-done((f32[2,8,16,1]{3,1,2,0:T(8,128)S(1)}, f32[2,8,16,1]{3,1,2,0:T(8,128)S(1)}, u32[]{:S(2)}, u32[]{:S(2)}) %collective-permute-start.6) | collective-permute-done | bytes 1056 | tf_op jit(solution)/shard_map/ppermute | solution.py:21
  48.8 1.6 %collective-permute-done.7 = f32[2,8,1,128]{3,1,2,0:T(8,128)S(1)} collective-permute-done((f32[2,8,1,128]{3,1,2,0:T(8,128)S(1)}, f32[2,8,1,128]{3,1,2,0:T(8,128)S(1)}, u32[]{:S(2)}, u32[]{:S(2)}) %collective-permute-start.7) | collective-permute-done | bytes 8224 | tf_op jit(solution)/shard_map/ppermute | solution.py:21
  51.8 0.8 collective-permute-start.8
  52.6 1.7 %collective-permute-done.9 = f32[2,8,16,1]{3,1,2,0:T(8,128)S(1)} collective-permute-done((f32[2,8,16,1]{3,1,2,0:T(8,128)S(1)}, f32[2,8,16,1]{3,1,2,0:T(8,128)S(1)}, u32[]{:S(2)}, u32[]{:S(2)}) %collective-permute-start.9) | collective-permute-done | bytes 1056 | tf_op jit(solution)/shard_map/ppermute | solution.py:21
  56.0 0.9 %collective-permute-start.10 = (f32[2,8,16,1]{3,1,2,0:T(8,128)S(1)}, f32[2,8,16,1]{3,1,2,0:T(8,128)S(1)}, u32[]{:S(2)}, u32[]{:S(2)}) collective-permute-start(f32[2,8,16,1]{3,1,2,0:T(8,128)S(1)} %slice.813), channel_id=1, source_target_pairs={{0,1},{1,2},{2,3},{3,0},{4,5},{5,6},{6,7},{7,4},{8,9},{9,10},{10,1... | collective-permute-start | bytes 3080 | tf_op jit(solution)/shard_map/ppermute | solution.py:21
  56.9 3.6 %collective-permute-done.10 = f32[2,8,16,1]{3,1,2,0:T(8,128)S(1)} collective-permute-done((f32[2,8,16,1]{3,1,2,0:T(8,128)S(1)}, f32[2,8,16,1]{3,1,2,0:T(8,128)S(1)}, u32[]{:S(2)}, u32[]{:S(2)}) %collective-permute-start.10) | collective-permute-done | bytes 1056 | tf_op jit(solution)/shard_map/ppermute | solution.py:21
  61.1 2.2 %collective-permute-done.11 = f32[2,8,1,128]{3,1,2,0:T(8,128)S(1)} collective-permute-done((f32[2,8,1,128]{3,1,2,0:T(8,128)S(1)}, f32[2,8,1,128]{3,1,2,0:T(8,128)S(1)}, u32[]{:S(2)}, u32[]{:S(2)}) %collective-permute-start.11) | collective-permute-done | bytes 8224 | tf_op jit(solution)/shard_map/ppermute | solution.py:21
  64.3 0.8 copy-done.2
  65.1 1.4 %collective-permute-start.12 = (f32[2,8,1,128]{3,1,2,0:T(8,128)S(1)}, f32[2,8,1,128]{3,1,2,0:T(8,128)S(1)}, u32[]{:S(2)}, u32[]{:S(2)}) collective-permute-start(f32[2,8,1,128]{3,1,2,0:T(8,128)S(1)} %slice.1048), channel_id=1, source_target_pairs={{0,28},{4,0},{8,4},{12,8},{16,12},{20,16},{24,20},{28,24},{1,29},{... | collective-permute-start | bytes 24584 | tf_op jit(solution)/shard_map/ppermute | solution.py:21
  67.4 1.5 %collective-permute-done.12 = f32[2,8,1,128]{3,1,2,0:T(8,128)S(1)} collective-permute-done((f32[2,8,1,128]{3,1,2,0:T(8,128)S(1)}, f32[2,8,1,128]{3,1,2,0:T(8,128)S(1)}, u32[]{:S(2)}, u32[]{:S(2)}) %collective-permute-start.12) | collective-permute-done | bytes 8224 | tf_op jit(solution)/shard_map/ppermute | solution.py:21
  69.6 0.7 copy.271
  70.3 3.6 %collective-permute-done.14 = f32[2,8,16,1]{3,1,2,0:T(8,128)S(1)} collective-permute-done((f32[2,8,16,1]{3,1,2,0:T(8,128)S(1)}, f32[2,8,16,1]{3,1,2,0:T(8,128)S(1)}, u32[]{:S(2)}, u32[]{:S(2)}) %collective-permute-start.14) | collective-permute-done | bytes 1056 | tf_op jit(solution)/shard_map/ppermute | solution.py:21
  74.5 2.2 %collective-permute-done.15 = f32[2,8,1,128]{3,1,2,0:T(8,128)S(1)} collective-permute-done((f32[2,8,1,128]{3,1,2,0:T(8,128)S(1)}, f32[2,8,1,128]{3,1,2,0:T(8,128)S(1)}, u32[]{:S(2)}, u32[]{:S(2)}) %collective-permute-start.15) | collective-permute-done | bytes 8224 | tf_op jit(solution)/shard_map/ppermute | solution.py:21
  79.6 0.8 reduce_sum.59
  (196 shorter events, 21.1 us)
Async XLA Ops:
  0.6 3.6 %copy-start.1 = (f32[3,8,16,128]{3,2,1,0:T(8,128)S(1)}, f32[3,8,16,128]{3,2,1,0:T(8,128)}, u32[]{:S(2)}) copy-start(f32[3,8,16,128]{3,2,1,0:T(8,128)} %param.13) | copy-start | bytes 589828
  1.8 27.8 %collective-permute-start.1 = (f32[2,8,16,1]{2,1,3,0:T(8,128)S(1)}, f32[2,8,16,1]{2,1,3,0:T(8,128)S(1)}, u32[]{:S(2)}, u32[]{:S(2)}) collective-permute-start(f32[2,8,16,1]{2,1,3,0:T(8,128)S(1)} %copy.276), channel_id=1, source_target_pairs={{0,3},{1,0},{2,1},{3,2},{4,7},{5,4},{6,5},{7,6},{8,11},{9,8},{10,9... | collective-permute-start | bytes 3080 | tf_op jit(solution)/shard_map/ppermute | solution.py:21
  4.3 25.6 %collective-permute-start = (f32[2,8,1,128]{3,1,2,0:T(8,128)S(1)}, f32[2,8,1,128]{3,1,2,0:T(8,128)S(1)}, u32[]{:S(2)}, u32[]{:S(2)}) collective-permute-start(f32[2,8,1,128]{3,1,2,0:T(8,128)S(1)} %slice.892), channel_id=1, source_target_pairs={{0,28},{4,0},{8,4},{12,8},{16,12},{20,16},{24,20},{28,24},{1,29},{... | collective-permute-start | bytes 24584 | tf_op jit(solution)/shard_map/ppermute | solution.py:21
  9.6 0.7 copy-start.6
  9.6 0.7 copy-start.7
  10.3 0.7 copy-start.5
  11.7 0.8 copy-start.3
  19.1 0.8 %copy-start.4 = (s32[8,16,128]{2,1,0:T(8,128)S(1)}, s32[8,16,128]{2,1,0:T(8,128)}, u32[]{:S(2)}) copy-start(s32[8,16,128]{2,1,0:T(8,128)} %param.10) | copy-start | bytes 196612
  30.2 0.9 %copy-start = (f32[3,8,16,128]{3,2,1,0:T(8,128)S(1)}, f32[3,8,16,128]{3,2,1,0:T(8,128)}, u32[]{:S(2)}) copy-start(f32[3,8,16,128]{3,2,1,0:T(8,128)} %param.14) | copy-start | bytes 589828
  31.3 4.4 %collective-permute-start.2 = (f32[2,8,16,1]{3,1,2,0:T(8,128)S(1)}, f32[2,8,16,1]{3,1,2,0:T(8,128)S(1)}, u32[]{:S(2)}, u32[]{:S(2)}) collective-permute-start(f32[2,8,16,1]{3,1,2,0:T(8,128)S(1)} %slice.713), channel_id=1, source_target_pairs={{0,1},{1,2},{2,3},{3,0},{4,5},{5,6},{6,7},{7,4},{8,9},{9,10},{10,1... | collective-permute-start | bytes 3080 | tf_op jit(solution)/shard_map/ppermute | solution.py:21
  31.8 6.4 %collective-permute-start.3 = (f32[2,8,1,128]{3,1,2,0:T(8,128)S(1)}, f32[2,8,1,128]{3,1,2,0:T(8,128)S(1)}, u32[]{:S(2)}, u32[]{:S(2)}) collective-permute-start(f32[2,8,1,128]{3,1,2,0:T(8,128)S(1)} %slice.920), channel_id=1, source_target_pairs={{0,4},{4,8},{8,12},{12,16},{16,20},{20,24},{24,28},{28,0},{1,5},{5... | collective-permute-start | bytes 24584 | tf_op jit(solution)/shard_map/ppermute | solution.py:21
  39.2 2.9 %collective-permute-start.5 = (f32[2,8,16,1]{3,1,2,0:T(8,128)S(1)}, f32[2,8,16,1]{3,1,2,0:T(8,128)S(1)}, u32[]{:S(2)}, u32[]{:S(2)}) collective-permute-start(f32[2,8,16,1]{3,1,2,0:T(8,128)S(1)} %slice.739), channel_id=1, source_target_pairs={{0,3},{1,0},{2,1},{3,2},{4,7},{5,4},{6,5},{7,6},{8,11},{9,8},{10,9... | collective-permute-start | bytes 3080 | tf_op jit(solution)/shard_map/ppermute | solution.py:21
  39.5 3.7 %collective-permute-start.4 = (f32[2,8,1,128]{3,1,2,0:T(8,128)S(1)}, f32[2,8,1,128]{3,1,2,0:T(8,128)S(1)}, u32[]{:S(2)}, u32[]{:S(2)}) collective-permute-start(f32[2,8,1,128]{3,1,2,0:T(8,128)S(1)} %slice.944), channel_id=1, source_target_pairs={{0,28},{4,0},{8,4},{12,8},{16,12},{20,16},{24,20},{28,24},{1,29},{... | collective-permute-start | bytes 24584 | tf_op jit(solution)/shard_map/ppermute | solution.py:21
  43.8 4.4 %collective-permute-start.6 = (f32[2,8,16,1]{3,1,2,0:T(8,128)S(1)}, f32[2,8,16,1]{3,1,2,0:T(8,128)S(1)}, u32[]{:S(2)}, u32[]{:S(2)}) collective-permute-start(f32[2,8,16,1]{3,1,2,0:T(8,128)S(1)} %slice.763), channel_id=1, source_target_pairs={{0,1},{1,2},{2,3},{3,0},{4,5},{5,6},{6,7},{7,4},{8,9},{9,10},{10,1... | collective-permute-start | bytes 3080 | tf_op jit(solution)/shard_map/ppermute | solution.py:21
  44.0 6.3 %collective-permute-start.7 = (f32[2,8,1,128]{3,1,2,0:T(8,128)S(1)}, f32[2,8,1,128]{3,1,2,0:T(8,128)S(1)}, u32[]{:S(2)}, u32[]{:S(2)}) collective-permute-start(f32[2,8,1,128]{3,1,2,0:T(8,128)S(1)} %slice.972), channel_id=1, source_target_pairs={{0,4},{4,8},{8,12},{12,16},{16,20},{20,24},{24,28},{28,0},{1,5},{5... | collective-permute-start | bytes 24584 | tf_op jit(solution)/shard_map/ppermute | solution.py:21
  51.3 3.0 %collective-permute-start.9 = (f32[2,8,16,1]{3,1,2,0:T(8,128)S(1)}, f32[2,8,16,1]{3,1,2,0:T(8,128)S(1)}, u32[]{:S(2)}, u32[]{:S(2)}) collective-permute-start(f32[2,8,16,1]{3,1,2,0:T(8,128)S(1)} %slice.789), channel_id=1, source_target_pairs={{0,3},{1,0},{2,1},{3,2},{4,7},{5,4},{6,5},{7,6},{8,11},{9,8},{10,9... | collective-permute-start | bytes 3080 | tf_op jit(solution)/shard_map/ppermute | solution.py:21
  51.8 3.7 %collective-permute-start.8 = (f32[2,8,1,128]{3,1,2,0:T(8,128)S(1)}, f32[2,8,1,128]{3,1,2,0:T(8,128)S(1)}, u32[]{:S(2)}, u32[]{:S(2)}) collective-permute-start(f32[2,8,1,128]{3,1,2,0:T(8,128)S(1)} %slice.996), channel_id=1, source_target_pairs={{0,28},{4,0},{8,4},{12,8},{16,12},{20,16},{24,20},{28,24},{1,29},{... | collective-permute-start | bytes 24584 | tf_op jit(solution)/shard_map/ppermute | solution.py:21
  56.0 4.4 %collective-permute-start.10 = (f32[2,8,16,1]{3,1,2,0:T(8,128)S(1)}, f32[2,8,16,1]{3,1,2,0:T(8,128)S(1)}, u32[]{:S(2)}, u32[]{:S(2)}) collective-permute-start(f32[2,8,16,1]{3,1,2,0:T(8,128)S(1)} %slice.813), channel_id=1, source_target_pairs={{0,1},{1,2},{2,3},{3,0},{4,5},{5,6},{6,7},{7,4},{8,9},{9,10},{10,1... | collective-permute-start | bytes 3080 | tf_op jit(solution)/shard_map/ppermute | solution.py:21
  56.9 6.3 %collective-permute-start.11 = (f32[2,8,1,128]{3,1,2,0:T(8,128)S(1)}, f32[2,8,1,128]{3,1,2,0:T(8,128)S(1)}, u32[]{:S(2)}, u32[]{:S(2)}) collective-permute-start(f32[2,8,1,128]{3,1,2,0:T(8,128)S(1)} %slice.1024), channel_id=1, source_target_pairs={{0,4},{4,8},{8,12},{12,16},{16,20},{20,24},{24,28},{28,0},{1,5},{5... | collective-permute-start | bytes 24584 | tf_op jit(solution)/shard_map/ppermute | solution.py:21
  64.1 1.0 %copy-start.2 = (bf16[4,3,8,16,128]{4,3,2,1,0:T(8,128)(2,1)S(1)}, bf16[4,3,8,16,128]{4,3,2,1,0:T(8,128)(2,1)}, u32[]{:S(2)}) copy-start(bf16[4,3,8,16,128]{4,3,2,1,0:T(8,128)(2,1)} %param.15) | copy-start | bytes 1179652
  64.2 2.6 %collective-permute-start.13 = (f32[2,8,16,1]{3,1,2,0:T(8,128)S(1)}, f32[2,8,16,1]{3,1,2,0:T(8,128)S(1)}, u32[]{:S(2)}, u32[]{:S(2)}) collective-permute-start(f32[2,8,16,1]{3,1,2,0:T(8,128)S(1)} %slice.839), channel_id=1, source_target_pairs={{0,3},{1,0},{2,1},{3,2},{4,7},{5,4},{6,5},{7,6},{8,11},{9,8},{10,9... | collective-permute-start | bytes 3080 | tf_op jit(solution)/shard_map/ppermute | solution.py:21
  65.1 3.7 %collective-permute-start.12 = (f32[2,8,1,128]{3,1,2,0:T(8,128)S(1)}, f32[2,8,1,128]{3,1,2,0:T(8,128)S(1)}, u32[]{:S(2)}, u32[]{:S(2)}) collective-permute-start(f32[2,8,1,128]{3,1,2,0:T(8,128)S(1)} %slice.1048), channel_id=1, source_target_pairs={{0,28},{4,0},{8,4},{12,8},{16,12},{20,16},{24,20},{28,24},{1,29},{... | collective-permute-start | bytes 24584 | tf_op jit(solution)/shard_map/ppermute | solution.py:21
  69.5 4.4 %collective-permute-start.14 = (f32[2,8,16,1]{3,1,2,0:T(8,128)S(1)}, f32[2,8,16,1]{3,1,2,0:T(8,128)S(1)}, u32[]{:S(2)}, u32[]{:S(2)}) collective-permute-start(f32[2,8,16,1]{3,1,2,0:T(8,128)S(1)} %slice.863), channel_id=1, source_target_pairs={{0,1},{1,2},{2,3},{3,0},{4,5},{5,6},{6,7},{7,4},{8,9},{9,10},{10,1... | collective-permute-start | bytes 3080 | tf_op jit(solution)/shard_map/ppermute | solution.py:21
  70.3 6.3 %collective-permute-start.15 = (f32[2,8,1,128]{3,1,2,0:T(8,128)S(1)}, f32[2,8,1,128]{3,1,2,0:T(8,128)S(1)}, u32[]{:S(2)}, u32[]{:S(2)}) collective-permute-start(f32[2,8,1,128]{3,1,2,0:T(8,128)S(1)} %slice.1076), channel_id=1, source_target_pairs={{0,4},{4,8},{8,12},{12,16},{16,20},{20,24},{24,28},{28,0},{1,5},{5... | collective-permute-start | bytes 24584 | tf_op jit(solution)/shard_map/ppermute | solution.py:21
where the time goes:
time: 81.6 us; the launch traced here: 81.1 us
  waiting for transfers between devices  30.2 us (37%)
  other arithmetic  15.9 us (19%)
  local copies, waits for them, and re-layouts  15.3 us (19%)
  starting transfers between devices  11.7 us (14%)
  blocking collectives  5.41 us (7%)
  between operations  2.02 us (2%)
    ppermute x16, waiting for transfers between devices, passed_along(): return lax.ppermute(x, axis, [(i, (i + by) % size) for i in range(size)])  30.2 us
    ppermute x16, starting transfers between devices, passed_along(): return lax.ppermute(x, axis, [(i, (i + by) % size) for i in range(size)])  11.7 us
    div x2, other arithmetic, inverse_permittivity(): result.append(1.0 / (background + design * contrast[channel]))  9.6 us
    unnamed x32, local copies, waits for them, and re-layouts  8.42 us
    all_gather x1, blocking collectives, body(): panel_piece = lax.all_gather(density, 'gy', axis=2, tiled=True)  5.41 us
  transfers between devices with their start and end apart: 16, of which 14 were waited for; matrix products, arithmetic and copies ran while one was open for 22% of the time, Pallas kernels for 0%

commit v1 on v0

v1 whole, which is shorter than its diff:
```python
import math

import jax
import jax.numpy as jnp
import numpy as np
from jax import lax
from jax.experimental import pallas as pl
from jax.experimental.pallas import tpu as pltpu
from jax.sharding import PartitionSpec as P

CY = 128
Z = 8
DZ = 4
STEPS = 4
TILE = 8
MATS = 4

courant = 0.5
sharpness = 4.0
threshold = 0.5

ROWS = 24
OWN = 16
SLOT = 64


def in_vmem(x):
    return pltpu.with_memory_space_constraint(x, pltpu.VMEM)


def call(kernel, outs, ins, aliases=None, scratch=()):
    return pl.pallas_call(
        kernel,
        out_shape=outs,
        in_specs=[pl.BlockSpec(memory_space=pltpu.VMEM)] * len(ins),
        out_specs=[pl.BlockSpec(memory_space=pltpu.VMEM)] * len(outs),
        scratch_shapes=list(scratch),
        input_output_aliases=aliases or {},
        compiler_params=pltpu.CompilerParams(vmem_limit_bytes=32 * 1024 * 1024),
    )(*[in_vmem(x) for x in ins])


def vmem(*shape):
    return pltpu.VMEM(shape, jnp.float32)


def lanes(rows):
    return lax.broadcasted_iota(jnp.int32, (rows, 128), 1)


def roll(x, by):
    return pltpu.roll(x, by % x.shape[1], 1)


def roll_rows(x, by):
    return pltpu.roll(x, by % x.shape[0], 0)


def passed_along(x, axis, by):
    size = lax.axis_size(axis)
    return lax.ppermute(x, axis, [(i, (i + by) % size) for i in range(size)])


def weight(offset, count, reach):
    ahead = np.mod(offset, count).astype(np.float64)
    behind = np.mod(-offset, count).astype(np.float64)
    return np.exp(-ahead / reach) + np.exp(-behind / reach)


def filter_constants(count, reach):
    source = np.arange(CY)
    strip = np.concatenate([np.arange(-4, 4), np.arange(CY - 4, CY + 4)])
    targets = np.concatenate([source, np.tile(strip, Z)])
    table = weight(targets[None, :] - source[:, None], count, reach)
    rows = np.zeros((8, 256))
    rows[0] = np.exp(-targets / reach)
    rows[1] = np.exp(targets / reach)
    rows[2, :CY] = np.exp(source / reach)
    rows[3, :CY] = np.exp(-source / reach)
    spread = np.zeros((16, 128))
    spread[np.arange(128) // TILE, np.arange(128)] = 1.0
    return (
        jnp.asarray(table, jnp.float32),
        jnp.asarray(rows, jnp.float32),
        jnp.asarray(spread, jnp.float32),
    )


def pack_rows_kernel(electric, magnetic, density, material, mask, spread, to_prev, to_next):
    cells = jnp.dot(
        mask[...].astype(jnp.float32), spread[...], preferred_element_type=jnp.float32
    )

    def e(channel, row):
        return electric[pl.ds(channel * 128 + row, Z, stride=OWN), :]

    def h(channel, row):
        return magnetic[pl.ds(channel * 128 + row, Z, stride=OWN), :]

    def ahead_part(row):
        part_y = h(1, row) + courant * (e(2, row + 1) - e(2, row))
        part_z = h(2, row) - courant * (e(1, row + 1) - e(1, row))
        return part_y, part_z

    for out, first, mask_row in ((to_prev, 0, 0), (to_next, OWN - 3, 1)):
        for slot in range(3):
            row, at = first + slot, slot * SLOT
            for channel in range(3):
                out[at + 8 * channel : at + 8 * channel + 8, :] = e(channel, row)
                out[at + 24 + 8 * channel : at + 32 + 8 * channel, :] = h(channel, row)
            out[at + 48 : at + 56, :] = material[pl.ds(row, Z, stride=OWN), :].astype(jnp.float32)
            out[at + 56 : at + 60, :] = density[pl.ds(row, DZ, stride=OWN), :]
            out[at + 60 : at + 64, :] = jnp.broadcast_to(cells[mask_row : mask_row + 1], (4, 128))
    part_y, part_z = ahead_part(2)
    to_prev[2 * SLOT + 32 : 2 * SLOT + 40, :] = part_y
    to_prev[2 * SLOT + 40 : 2 * SLOT + 48, :] = part_z
    part_y, part_z = ahead_part(OWN - 4)
    to_next[3 * SLOT : 3 * SLOT + 8, :] = e(0, OWN - 4)
    to_next[3 * SLOT + 8 : 3 * SLOT + 16, :] = part_y
    to_next[3 * SLOT + 16 : 3 * SLOT + 24, :] = part_z


def edge_window(planes):
    rows = planes[0].shape[0]
    lane = lanes(rows)
    window = (lane < 4) | (lane >= 124)
    gathered = planes[7]
    for z in range(6, -1, -1):
        gathered = jnp.where(window, planes[z], roll(gathered, 16))
    return gathered


def edge_pairs(groups):
    lane = lanes(groups[0][0].shape[0])
    first = (lane & 15) < 8
    found = [edge_window(planes) for planes in groups]
    return [
        jnp.where(first, roll(found[2 * i], 4), roll(found[2 * i + 1], 12)) for i in range(4)
    ]


def edge_messages(pairs):
    quarter = (lanes(pairs[0].shape[0]) >> 2) & 3

    def pick(a, b, c, d):
        return jnp.where(quarter < 2, jnp.where(quarter == 0, a, b), jnp.where(quarter == 2, c, d))

    left, right = [], []
    for one, two in ((pairs[0], pairs[1]), (pairs[2], pairs[3])):
        left.append(pick(roll(one, -4), roll(one, -8), roll(two, 4), two))
        right.append(pick(one, roll(one, -4), roll(two, 8), roll(two, 4)))
    return left, right


def density_planes(layers, cells, rising, falling):
    place = lanes(cells.shape[0]) & 3
    planes = []
    for layer in layers:
        up = jnp.sum(layer * rising, axis=1, keepdims=True)
        down = jnp.sum(layer * falling, axis=1, keepdims=True)
        planes += [layer, jnp.where(place == 0, up, jnp.where(place == 1, down, cells))]
    return planes


def own_kernel(
    electric, magnetic, density, material, mask, table, factors, spread,
    e_all, h_all, m_all, d_all, c_all, local, pairs_out, left_out, right_out,
):
    cells2 = jnp.dot(
        mask[...].astype(jnp.float32), spread[...], preferred_element_type=jnp.float32
    )
    cells = jnp.concatenate(
        [jnp.broadcast_to(cells2[i : i + 1], (TILE, 128)) for i in range(2)], 0
    )
    c_all[0:OWN, :] = cells
    groups = []
    for source, target in ((electric, e_all), (magnetic, h_all)):
        for channel in range(3):
            planes = []
            for z in range(Z):
                p = channel * Z + z
                plane = source[p * OWN : (p + 1) * OWN, :]
                target[p * ROWS : p * ROWS + OWN, :] = plane
                planes.append(plane)
            groups.append(planes)
    planes = []
    for z in range(Z):
        plane = material[z * OWN : (z + 1) * OWN, :].astype(jnp.float32)
        m_all[z * ROWS : z * ROWS + OWN, :] = plane
        planes.append(plane)
    groups.append(planes)
    layers = []
    for layer in range(DZ):
        plane = density[layer * OWN : (layer + 1) * OWN, :]
        d_all[layer * ROWS : layer * ROWS + OWN, :] = plane
        layers.append(plane)
    groups.append(density_planes(layers, cells, factors[2:3, 0:128], factors[3:4, 0:128]))
    pairs = edge_pairs(groups)
    left, right = edge_messages(pairs)
    for i in range(4):
        pairs_out[i * ROWS : i * ROWS + OWN, :] = pairs[i]
    for i in range(2):
        left_out[i * ROWS : i * ROWS + OWN, :] = left[i]
        right_out[i * ROWS : i * ROWS + OWN, :] = right[i]
    smooth = jnp.dot(
        density[...], table[...], precision=lax.Precision.HIGHEST,
        preferred_element_type=jnp.float32,
    )
    for layer in range(DZ):
        local[layer * ROWS : layer * ROWS + OWN, :] = smooth[layer * OWN : (layer + 1) * OWN]


def halo_kernel(
    from_next, from_prev, e_in, h_in, m_in, d_in, c_in, pairs_in, left_in, right_in, factors,
    e_all, h_all, m_all, d_all, c_all, pairs_out, left_out, right_out, sums_out,
):
    for got, first in ((from_next, 16), (from_prev, 21)):
        for slot in range(3):
            at, row = slot * SLOT, first + slot
            for channel in range(3):
                where = pl.ds(channel * Z * ROWS + row, Z, stride=ROWS)
                e_all[where, :] = got[at + 8 * channel : at + 8 * channel + 8, :]
                h_all[where, :] = got[at + 24 + 8 * channel : at + 32 + 8 * channel, :]
            m_all[pl.ds(row, Z, stride=ROWS), :] = got[at + 48 : at + 56, :]
            d_all[pl.ds(row, DZ, stride=ROWS), :] = got[at + 56 : at + 60, :]
            c_all[row : row + 1, :] = got[at + 60 : at + 61, :]
    zeros = jnp.zeros((Z, 128), jnp.float32)
    for channel in range(3):
        at = channel * Z * ROWS
        e_all[pl.ds(at + 19, Z, stride=ROWS), :] = from_next[
            2 * SLOT + 8 * channel : 2 * SLOT + 8 * channel + 8, :
        ]
        h_all[pl.ds(at + 19, Z, stride=ROWS), :] = zeros
        if channel > 0:
            e_all[pl.ds(at + 20, Z, stride=ROWS), :] = from_prev[8 * channel : 8 * channel + 8, :]
            h_all[pl.ds(at + 20, Z, stride=ROWS), :] = from_prev[
                3 * SLOT + 8 * channel : 3 * SLOT + 8 * channel + 8, :
            ]
        else:
            e_all[pl.ds(at + 20, Z, stride=ROWS), :] = from_prev[3 * SLOT : 3 * SLOT + 8, :]
            h_all[pl.ds(at + 20, Z, stride=ROWS), :] = zeros
    for row in (19, 20):
        m_all[pl.ds(row, Z, stride=ROWS), :] = zeros
        d_all[pl.ds(row, DZ, stride=ROWS), :] = zeros[0:DZ]
        c_all[row : row + 1, :] = zeros[0:1]

    groups = []
    for target in (e_all, h_all):
        for channel in range(3):
            groups.append(
                [target[(channel * Z + z) * ROWS + OWN : (channel * Z + z + 1) * ROWS, :] for z in range(Z)]
            )
    groups.append([m_all[z * ROWS + OWN : (z + 1) * ROWS, :] for z in range(Z)])
    layers = [d_all[layer * ROWS + OWN : (layer + 1) * ROWS, :] for layer in range(DZ)]
    cells = c_all[OWN:ROWS, :]
    groups.append(density_planes(layers, cells, factors[2:3, 0:128], factors[3:4, 0:128]))
    pairs = edge_pairs(groups)
    left, right = edge_messages(pairs)
    for i in range(4):
        pairs_out[i * ROWS + OWN : (i + 1) * ROWS, :] = pairs[i]
    for i in range(2):
        left_out[i * ROWS + OWN : (i + 1) * ROWS, :] = left[i]
        right_out[i * ROWS + OWN : (i + 1) * ROWS, :] = right[i]
    sums_out[0:OWN, :] = left_in[ROWS : ROWS + OWN, :]
    sums_out[OWN:ROWS, :] = left[1]


def project(values):
    base = math.tanh(sharpness * threshold)
    bottom = base + math.tanh(sharpness * (1.0 - threshold))
    level = jnp.tanh(sharpness * (values - threshold))
    return (base + level) * (1.0 / bottom), (sharpness / bottom) * (1.0 - level * level)


def step_kernel(count, reach, others):
    devices = count // CY
    norm_total = 2.0 * float(np.sum(np.exp(-np.arange(count) / reach)))

    def factor(m):
        return math.exp(-CY * m / reach), math.exp(-(count - CY * m) / reach)

    def fix(delta):
        if delta == 0:
            return 1.0 - math.exp(-count / reach)
        return (
            math.exp(-delta / reach) + math.exp(-(count - delta) / reach)
            - math.exp(-(count + delta) / reach) - math.exp(delta / reach)
        )

    def kernel(*refs):
        material_table, contrast, from_right, from_left = refs[:4]
        rest = refs[4 : 4 + others]
        (e_in, h_in, m_all, d_all, c_all, pairs, local, table, factors, forward,
         e_final, h_final, gradient, e_all, h_all, inverse, se, sh, si, gained) = refs[4 + others :]
        lane = lanes(ROWS)
        place = lane & 15
        odd = ((lane >> 4) & 1) == 1
        layer_of = lane >> 5
        part = place >> 2

        got_left = [from_left[i * ROWS : (i + 1) * ROWS, :] for i in range(2)]
        got_right = [from_right[i * ROWS : (i + 1) * ROWS, :] for i in range(2)]

        def strip(index):
            tile, q = index // 4, index % 4
            pair = pairs[(index // 2) * ROWS : (index // 2 + 1) * ROWS, :]
            if index % 2 == 0:
                own_l, own_r = pair, roll(pair, 8)
            else:
                own_l, own_r = roll(pair, -8), pair
            outer = jnp.where(part == 0, roll(got_left[tile], -4 * q), roll(got_right[tile], 12 - 4 * q))
            return jnp.where(part == 1, own_l, jnp.where(part == 2, own_r, outer))

        for channel in range(3):
            se[channel * ROWS : (channel + 1) * ROWS, :] = strip(channel)
            sh[channel * ROWS : (channel + 1) * ROWS, :] = strip(3 + channel)
        strip_material = strip(6)
        raw = strip(7)
        strip_density = jnp.where(odd, roll(raw, 16), raw)
        marks = jnp.where(odd, raw, roll(raw, -16))
        strip_cells = jnp.where((place & 2) == 2, marks, roll(marks, -2))

        def lane_factor(m):
            up, down = factor(m)
            return jnp.where(place == 12, up, down)

        sums = lane_factor(1) * got_left[1] + lane_factor(devices - 1) * got_right[1]
        for i, other in enumerate(rest):
            sums = sums + lane_factor(2 + i) * other[...]
        halo_local = jnp.dot(
            jnp.concatenate([d_all[l * ROWS + OWN : (l + 1) * ROWS, :] for l in range(DZ)], 0),
            table[...], precision=lax.Precision.HIGHEST, preferred_element_type=jnp.float32,
        )
        strip_smooth = jnp.zeros((ROWS, 128), jnp.float32)
        designs, slopes = [], []
        cells = c_all[...]
        for l in range(DZ):
            at = (2 * l + 1) * 16 + 12
            up = jnp.broadcast_to(sums[:, at : at + 1], (ROWS, 128))
            down = jnp.broadcast_to(sums[:, at + 1 : at + 2], (ROWS, 128))
            own = local[l * ROWS : l * ROWS + OWN, :]
            both = jnp.concatenate([own, halo_local[l * 8 : (l + 1) * 8]], 0)
            smooth = both[:, :128] + factors[0:1, :128] * up + factors[1:2, :128] * down
            far = both[:, 128:] + factors[0:1, 128:] * up + factors[1:2, 128:] * down
            strip_smooth = jnp.where(layer_of == l, far, strip_smooth)
            filtered = 0.5 * d_all[l * ROWS : (l + 1) * ROWS, :] + (0.5 / norm_total) * smooth
            projected, slope = project(filtered)
            designs.append(cells * projected)
            slopes.append(slope[:OWN] * cells[:OWN])
        for delta in range(4):
            value = fix(delta) * strip_density
            ahead = value if delta == 0 else roll(value, delta)
            behind = value if delta == 0 else roll(value, -delta)
            strip_smooth = strip_smooth + jnp.where(place >= 12 + delta, ahead, 0.0)
            strip_smooth = strip_smooth + jnp.where(place < 4 - delta, behind, 0.0)
        projected, _ = project(0.5 * strip_density + (0.5 / norm_total) * strip_smooth)
        strip_design = strip_cells * projected

        def invert(kind, design, channel):
            background = jnp.where(
                kind < 1.5,
                jnp.where(kind < 0.5, material_table[channel, 0], material_table[channel, 1]),
                jnp.where(kind < 2.5, material_table[channel, 2], material_table[channel, 3]),
            )
            return courant / (background + design * contrast[channel])

        for channel in range(3):
            si[channel * ROWS : (channel + 1) * ROWS, :] = invert(strip_material, strip_design, channel)
        for z in range(Z):
            kind = m_all[z * ROWS : (z + 1) * ROWS, :]
            for channel in range(3):
                p = channel * Z + z
                inverse[p * ROWS : (p + 1) * ROWS, :] = invert(kind, designs[z // 2], channel)
        gained[...] = jnp.zeros_like(gained)

        zero = jnp.zeros((ROWS, 128), jnp.float32)
        last, first = lane == 127, lane == 0

        def e_at(channel, z):
            p = channel * Z + z
            return e_all[p * ROWS : (p + 1) * ROWS, :]

        def h_at(channel, z):
            p = channel * Z + z
            return h_all[p * ROWS : (p + 1) * ROWS, :]

        def s_at(ref, channel):
            return ref[channel * ROWS : (channel + 1) * ROWS, :]

        def step(t, carry):
            sx, sy, sz = s_at(se, 0), s_at(se, 1), s_at(se, 2)
            for z in range(Z):
                ex, ey, ez = e_at(0, z), e_at(1, z), e_at(2, z)
                ex_up = e_at(0, z + 1) if z + 1 < Z else zero
                ey_up = e_at(1, z + 1) if z + 1 < Z else zero
                to = 115 - 16 * z
                dy_ez = jnp.where(last, roll(sz, to), roll(ez, -1)) - ez
                dy_ex = jnp.where(last, roll(sx, to), roll(ex, -1)) - ex
                dx_ez = roll_rows(ez, -1) - ez
                dx_ey = roll_rows(ey, -1) - ey
                for channel, curl in enumerate(
                    (dy_ez - (ey_up - ey), (ex_up - ex) - dx_ez, dx_ey - dy_ex)
                ):
                    p = channel * Z + z
                    h_all[p * ROWS : (p + 1) * ROWS, :] = h_at(channel, z) - courant * curl
            up_x = jnp.where(lane < 112, roll(sx, -16), 0.0)
            up_y = jnp.where(lane < 112, roll(sy, -16), 0.0)
            for channel, curl in enumerate(
                (
                    (roll(sz, -1) - sz) - (up_y - sy),
                    (up_x - sx) - (roll_rows(sz, -1) - sz),
                    (roll_rows(sy, -1) - sy) - (roll(sx, -1) - sx),
                )
            ):
                sh[channel * ROWS : (channel + 1) * ROWS, :] = s_at(sh, channel) - courant * curl
            sx, sy, sz = s_at(sh, 0), s_at(sh, 1), s_at(sh, 2)
            for z in range(Z):
                hx, hy, hz = h_at(0, z), h_at(1, z), h_at(2, z)
                hx_down = h_at(0, z - 1) if z > 0 else zero
                hy_down = h_at(1, z - 1) if z > 0 else zero
                to = -(16 * z + 3)
                dy_hz = hz - jnp.where(first, roll(sz, to), roll(hz, 1))
                dy_hx = hx - jnp.where(first, roll(sx, to), roll(hx, 1))
                dx_hz = hz - roll_rows(hz, 1)
                dx_hy = hy - roll_rows(hy, 1)
                total = jnp.zeros((OWN, 128), jnp.float32)
                for channel, curl in enumerate(
                    (dy_hz - (hy - hy_down), (hx - hx_down) - dx_hz, dx_hy - dy_hx)
                ):
                    p = channel * Z + z
                    value = e_at(channel, z) + inverse[p * ROWS : (p + 1) * ROWS, :] * curl
                    e_all[p * ROWS : (p + 1) * ROWS, :] = value
                    stored = forward[t, p].astype(jnp.float32)
                    total = total + contrast[channel] * (value[:OWN] * stored)
                l = z // 2
                gained[l * OWN : (l + 1) * OWN, :] = gained[l * OWN : (l + 1) * OWN, :] + total
            down_x = jnp.where(lane >= 16, roll(sx, 16), 0.0)
            down_y = jnp.where(lane >= 16, roll(sy, 16), 0.0)
            for channel, curl in enumerate(
                (
                    (sz - roll(sz, 1)) - (sy - down_y),
                    (sx - down_x) - (sz - roll_rows(sz, 1)),
                    (sy - roll_rows(sy, 1)) - (sx - roll(sx, 1)),
                )
            ):
                se[channel * ROWS : (channel + 1) * ROWS, :] = (
                    s_at(se, channel) + s_at(si, channel) * curl
                )
            return carry

        lax.fori_loop(0, STEPS, step, 0)
        for p in range(3 * Z):
            e_final[p * OWN : (p + 1) * OWN, :] = e_all[p * ROWS : p * ROWS + OWN, :]
            h_final[p * OWN : (p + 1) * OWN, :] = h_all[p * ROWS : p * ROWS + OWN, :]
        for l in range(DZ):
            gradient[l * OWN : (l + 1) * OWN, :] = slopes[l] * gained[l * OWN : (l + 1) * OWN, :]

    return kernel


def body(
    density, tile_mask, material, material_table, contrast, electric, magnetic, forward_fields
):
    devices = lax.axis_size("gy")
    count = density.shape[2] * devices
    reach = 4.0 * CY
    table, factors, spread = filter_constants(count, reach)
    e2 = electric.reshape(-1, 128)
    h2 = magnetic.reshape(-1, 128)
    d2 = density.reshape(-1, 128)
    m2 = material.reshape(-1, 128)
    f2 = forward_fields.reshape(STEPS, 3 * Z, OWN, 128)

    to_prev, to_next = call(
        pack_rows_kernel, [vmem(3 * SLOT, 128), vmem(3 * SLOT + 24, 128)],
        [e2, h2, d2, m2, tile_mask, spread],
    )
    from_prev = passed_along(to_next, "gx", 1)
    from_next = passed_along(to_prev, "gx", -1)
    e_all, h_all, m_all, d_all, c_all, local, pairs, left, right = call(
        own_kernel,
        [vmem(3 * Z * ROWS, 128), vmem(3 * Z * ROWS, 128), vmem(Z * ROWS, 128),
         vmem(DZ * ROWS, 128), vmem(ROWS, 128), vmem(DZ * ROWS, 256), vmem(4 * ROWS, 128),
         vmem(2 * ROWS, 128), vmem(2 * ROWS, 128)],
        [e2, h2, d2, m2, tile_mask, table, factors, spread],
    )
    e_all, h_all, m_all, d_all, c_all, pairs, left, right, sums = call(
        halo_kernel,
        [vmem(3 * Z * ROWS, 128), vmem(3 * Z * ROWS, 128), vmem(Z * ROWS, 128),
         vmem(DZ * ROWS, 128), vmem(ROWS, 128), vmem(4 * ROWS, 128),
         vmem(2 * ROWS, 128), vmem(2 * ROWS, 128), vmem(ROWS, 128)],
        [from_next, from_prev, e_all, h_all, m_all, d_all, c_all, pairs, left, right, factors],
        aliases={2: 0, 3: 1, 4: 2, 5: 3, 6: 4, 7: 5, 8: 6, 9: 7},
    )
    from_left = passed_along(right, "gy", 1)
    from_right = passed_along(left, "gy", -1)
    rest = [passed_along(sums, "gy", m) for m in range(2, devices - 1)]
    smem = pl.BlockSpec(memory_space=pltpu.SMEM)
    in_v = pl.BlockSpec(memory_space=pltpu.VMEM)
    operands = [from_right, from_left] + rest + [
        e_all, h_all, m_all, d_all, c_all, pairs, local, table, factors, f2,
    ]
    at = 4 + len(rest)
    outs = pl.pallas_call(
        step_kernel(count, reach, len(rest)),
        out_shape=[
            jax.ShapeDtypeStruct(e2.shape, jnp.float32),
            jax.ShapeDtypeStruct(h2.shape, jnp.float32),
            jax.ShapeDtypeStruct(d2.shape, jnp.float32),
            vmem(3 * Z * ROWS, 128),
            vmem(3 * Z * ROWS, 128),
        ],
        in_specs=[smem, smem] + [in_v] * len(operands),
        out_specs=[in_v] * 5,
        scratch_shapes=[
            vmem(3 * Z * ROWS, 128), vmem(3 * ROWS, 128), vmem(3 * ROWS, 128), vmem(3 * ROWS, 128),
            vmem(DZ * OWN, 128),
        ],
        input_output_aliases={at: 3, at + 1: 4},
        compiler_params=pltpu.CompilerParams(vmem_limit_bytes=32 * 1024 * 1024),
    )(material_table, contrast, *[in_vmem(x) for x in operands])
    return (
        outs[0].reshape(electric.shape), outs[1].reshape(magnetic.shape),
        outs[2].reshape(density.shape),
    )


def solution(mesh):
    return jax.shard_map(
        body,
        mesh=mesh,
        in_specs=(
            P(None, "gx", "gy"),
            P("gx", "gy"),
            P(None, "gx", "gy"),
            P(),
            P(),
            P(None, None, "gx", "gy"),
            P(None, None, "gx", "gy"),
            P(None, None, None, "gx", "gy"),
        ),
        out_specs=(P(None, None, "gx", "gy"), P(None, None, "gx", "gy"), P(None, "gx", "gy")),
        check_vma=False,
    )
```

time: 81.6 us -> 24 us (0.29)
  waiting for transfers between devices: 30.2 us -> 5.33 us
  other arithmetic: 15.9 us -> 0 us
  local copies, waits for them, and re-layouts: 15.3 us -> 4.81 us
  blocking collectives: 5.41 us -> 0 us
  Pallas kernels: 0 us -> 4.75 us
  starting transfers between devices: 11.7 us -> 8.11 us
  between operations: 2.02 us -> 0.69 us
    ppermute x16 -> x5, waiting for transfers between devices: 30.2 us -> 5.33 us  [passed_along(): return lax.ppermute(x, axis, [(i, (i + by) % size) for i in range(size)])]
    div x3 -> x0, other arithmetic: 9.62 us -> none  [the longest x2 9.6 us: inverse_permittivity(): result.append(1.0 / (background + design * contrast[channel]))]
    slice x81 -> x0, local copies, waits for them, and re-layouts: 6.34 us -> none  [the longest x4 1.01 us: body(): next_columns = passed_along(electric[0::2, :, :, :1], 'gy', -1)]
    all_gather x1 -> x0, blocking collectives: 5.41 us -> none  [body(): panel_piece = lax.all_gather(density, 'gy', axis=2, tiled=True)]
    pallas_call x0 -> x4, Pallas kernels: none -> 4.75 us  [the longest x1 3.2 us: body(): pl.pallas_call(step_kernel(count, reach, len(rest)), out_shape=[jax.Shape...]
    unnamed x32 -> x22, local copies, waits for them, and re-layouts: 8.42 us -> 4.81 us
    ppermute x16 -> x5, starting transfers between devices: 11.7 us -> 8.11 us  [passed_along(): return lax.ppermute(x, axis, [(i, (i + by) % size) for i in range(size)])]
    another operation x32 -> x0, other arithmetic: 2.28 us -> none  [the longest x12 1.42 us: curl_behind(): jnp.stack([behind_y(part_z) - behind_z(part_y), behind_z(part_x) - behind...]
  transfers between devices with their start and end apart: 16 -> 5, of which waited for: 14 -> 2; matrix products, arithmetic and copies ran while one was open for 22% -> 0% of each run, Pallas kernels for 0% -> 3%
where the time goes in v1:
time: 24 us; the launch traced here: 23.7 us
  starting transfers between devices  8.11 us (34%)
  waiting for transfers between devices  5.33 us (22%)
  local copies, waits for them, and re-layouts  4.81 us (20%)
  Pallas kernels  4.75 us (20%)
  between operations  0.69 us (3%)
    ppermute x5, starting transfers between devices, passed_along(): return lax.ppermute(x, axis, [(i, (i + by) % size) for i in range(size)])  8.11 us
    ppermute x5, waiting for transfers between devices, passed_along(): return lax.ppermute(x, axis, [(i, (i + by) % size) for i in range(size)])  5.33 us
    unnamed x22, local copies, waits for them, and re-layouts  4.81 us
    pallas_call x1, Pallas kernels, body(): pl.pallas_call(step_kernel(count, reach, len(rest)), out_shape=[jax.Shape...  3.2 us
    pallas_call x3, Pallas kernels, call(): pl.pallas_call(kernel, out_shape=outs, in_specs=[pl.BlockSpec(memory_spac...  1.56 us
  transfers between devices with their start and end apart: 5, of which 2 were waited for; matrix products, arithmetic and copies ran while one was open for 0% of the time, Pallas kernels for 3%

profile of v1, /device:TPU:0, one launch (start us, length us, event | category | flops | bytes accessed | tf_op | source)
XLA Modules:
  0.0 23.7 jit_solution(12497571026211241286)
XLA Ops:
  0.6 0.0 copy-start.7
  0.7 0.7 %copy-done.7 = f32[16,128]{1,0:T(8,128)S(1)} copy-done((f32[16,128]{1,0:T(8,128)S(1)}, f32[16,128]{1,0:T(8,128)}, u32[]{:S(2)}) %copy-start.7) | copy-done | bytes 8216
  1.3 0.0 copy-done.8
  1.3 0.9 %copy-done = f32[3,8,16,128]{3,2,1,0:T(8,128)S(1)} copy-done((f32[3,8,16,128]{3,2,1,0:T(8,128)S(1)}, f32[3,8,16,128]{3,2,1,0:T(8,128)}, u32[]{:S(2)}) %copy-start) | copy-done | bytes 196632
  2.3 0.9 %copy-done.1 = f32[3,8,16,128]{3,2,1,0:T(8,128)S(1)} copy-done((f32[3,8,16,128]{3,2,1,0:T(8,128)S(1)}, f32[3,8,16,128]{3,2,1,0:T(8,128)}, u32[]{:S(2)}) %copy-start.1) | copy-done | bytes 196632
  3.2 0.8 %copy-done.4 = s32[8,16,128]{2,1,0:T(8,128)S(1)} copy-done((s32[8,16,128]{2,1,0:T(8,128)S(1)}, s32[8,16,128]{2,1,0:T(8,128)}, u32[]{:S(2)}) %copy-start.4) | copy-done | bytes 65560
  4.0 0.8 %copy-done.5 = f32[4,16,128]{2,1,0:T(8,128)S(1)} copy-done((f32[4,16,128]{2,1,0:T(8,128)S(1)}, f32[4,16,128]{2,1,0:T(8,128)}, u32[]{:S(2)}) %copy-start.5) | copy-done | bytes 32792
  4.8 0.1 shard_map.130
  4.9 3.0 %collective-permute-start.1 = (f32[216,128]{1,0:T(8,128)S(1)}, f32[216,128]{1,0:T(8,128)S(1)}, u32[]{:S(2)}, u32[]{:S(2)}) collective-permute-start(f32[216,128]{1,0:T(8,128)S(1)} %get-tuple-element.27), channel_id=1, source_target_pairs={{0,4},{4,8},{8,12},{12,16},{16,20},{20,24},{24,28},{28,0},{1,5},{5... | collective-permute-start | bytes 331784 | tf_op jit(solution)/shard_map/ppermute | solution.py:61
  7.9 3.1 %collective-permute-start = (f32[192,128]{1,0:T(8,128)S(1)}, f32[192,128]{1,0:T(8,128)S(1)}, u32[]{:S(2)}, u32[]{:S(2)}) collective-permute-start(f32[192,128]{1,0:T(8,128)S(1)} %get-tuple-element.26), channel_id=1, source_target_pairs={{0,28},{4,0},{8,4},{12,8},{16,12},{20,16},{24,20},{28,24},{1,29},{... | collective-permute-start | bytes 294920 | tf_op jit(solution)/shard_map/ppermute | solution.py:61
  11.0 0.8 %shard_map.131 = (f32[576,128]{1,0:T(8,128)S(1)}, f32[576,128]{1,0:T(8,128)S(1)}, f32[192,128]{1,0:T(8,128)S(1)}, f32[96,128]{1,0:T(8,128)S(1)}, f32[24,128]{1,0...) custom-call(f32[384,128]{1,0:T(8,128)S(1)} %bitcast.9, ...), custom_call_target="tpu_custom_call" | custom-call | tf_op jit(solution)/shard_map/pallas_call | solution.py:32
  11.8 3.1 %collective-permute-done.from_next = f32[192,128]{1,0:T(8,128)S(1)} collective-permute-done((f32[192,128]{1,0:T(8,128)S(1)}, f32[192,128]{1,0:T(8,128)S(1)}, u32[]{:S(2)}, u32[]{:S(2)}) %collective-permute-start) | collective-permute-done | bytes 98336 | tf_op jit(solution)/shard_map/ppermute | solution.py:61
  14.9 0.0 collective-permute-done.1.from_prev
  14.9 0.7 %shard_map.132 = (f32[576,128]{1,0:T(8,128)S(1)}, f32[576,128]{1,0:T(8,128)S(1)}, f32[192,128]{1,0:T(8,128)S(1)}, f32[96,128]{1,0:T(8,128)S(1)}, f32[24,128]{1,0...) custom-call(f32[192,128]{1,0:T(8,128)S(1)} %collective-permute-done., ...), custom_call_target="tpu_custom_call", output_to_operand_aliasing={{0}: (2, {}), {1}: (3, {}), {2}: (4, {}), {3}: (5, {}), {4}... | custom-call | tf_op jit(solution)/shard_map/pallas_call | solution.py:32
  15.6 0.0 collective-permute-start.2
  15.6 0.5 %collective-permute-start.3 = (f32[48,128]{1,0:T(8,128)S(1)}, f32[48,128]{1,0:T(8,128)S(1)}, u32[]{:S(2)}, u32[]{:S(2)}) collective-permute-start(f32[48,128]{1,0:T(8,128)S(1)} %get-tuple-element.37), channel_id=1, source_target_pairs={{0,1},{1,2},{2,3},{3,0},{4,5},{5,6},{6,7},{7,4},{8,9},{9,10},{10,1... | collective-permute-start | bytes 73736 | tf_op jit(solution)/shard_map/ppermute | solution.py:61
  16.1 1.5 %collective-permute-start.4 = (f32[24,128]{1,0:T(8,128)S(1)}, f32[24,128]{1,0:T(8,128)S(1)}, u32[]{:S(2)}, u32[]{:S(2)}) collective-permute-start(f32[24,128]{1,0:T(8,128)S(1)} %get-tuple-element.38), channel_id=1, source_target_pairs={{0,2},{1,3},{2,0},{3,1},{4,6},{5,7},{6,4},{7,5},{8,10},{9,11},{10,... | collective-permute-start | bytes 36872 | tf_op jit(solution)/shard_map/ppermute | solution.py:61
  17.6 2.2 %collective-permute-done.4.refs_4_ = f32[24,128]{1,0:T(8,128)S(1)} collective-permute-done((f32[24,128]{1,0:T(8,128)S(1)}, f32[24,128]{1,0:T(8,128)S(1)}, u32[]{:S(2)}, u32[]{:S(2)}) %collective-permute-start.4) | collective-permute-done | bytes 12320 | tf_op jit(solution)/shard_map/ppermute | solution.py:61
  19.8 0.0 collective-permute-done.2.refs_2_
  19.8 0.0 collective-permute-done.3.refs_3_
  19.8 0.0 copy-start.10
  19.8 0.0 copy-done.3
  19.8 0.7 %copy-done.9 = f32[3,4]{1,0:T(4,128)S(1)} copy-done((f32[3,4]{1,0:T(4,128)S(1)}, f32[3,4]{1,0:T(4,128)}, u32[]{:S(2)}) %copy-start.9) | copy-done | bytes 72
  20.5 3.2 %shard_map.133 = (f32[384,128]{1,0:T(8,128)}, f32[384,128]{1,0:T(8,128)}, f32[64,128]{1,0:T(8,128)}, f32[576,128]{1,0:T(8,128)S(1)}, f32[576,128]{1,0:T(8,128)S(1)}) custom-call(f32[3,4]{1,0:T(4,128)S(1)} %copy-done.9, f32[3]{0:T(128)S(1)} %copy-done.10, f32[48,128]{1,0:T(8,128)S(1)} %collective-permute-done.2.refs_2_, ...), custom_call_target="tpu_custom_call", output_to_operand_aliasing={{3}: (5, {}), {4}: (6, {})} | custom-call | tf_op jit(solution)/shard_map/pallas_call | solution.py:504
  (12 shorter events, 0.0 us)
Async XLA Ops:
  0.6 0.7 %copy-start.7 = (f32[16,128]{1,0:T(8,128)S(1)}, f32[16,128]{1,0:T(8,128)}, u32[]{:S(2)}) copy-start(f32[16,128]{1,0:T(8,128)} %constant.8.clone.spread) | copy-start | bytes 24580
  0.6 0.7 %copy-start.8 = (s32[2,16]{1,0:T(2,128)S(1)}, s32[2,16]{1,0:T(2,128)}, u32[]{:S(2)}) copy-start(s32[2,16]{1,0:T(2,128)} %mask.3) | copy-start | bytes 388
  1.3 0.9 %copy-start = (f32[3,8,16,128]{3,2,1,0:T(8,128)S(1)}, f32[3,8,16,128]{3,2,1,0:T(8,128)}, u32[]{:S(2)}) copy-start(f32[3,8,16,128]{3,2,1,0:T(8,128)} %param.16) | copy-start | bytes 589828
  2.3 0.9 %copy-start.1 = (f32[3,8,16,128]{3,2,1,0:T(8,128)S(1)}, f32[3,8,16,128]{3,2,1,0:T(8,128)}, u32[]{:S(2)}) copy-start(f32[3,8,16,128]{3,2,1,0:T(8,128)} %param.17) | copy-start | bytes 589828
  3.2 0.8 %copy-start.4 = (s32[8,16,128]{2,1,0:T(8,128)S(1)}, s32[8,16,128]{2,1,0:T(8,128)}, u32[]{:S(2)}) copy-start(s32[8,16,128]{2,1,0:T(8,128)} %param.13) | copy-start | bytes 196612
  4.0 0.8 %copy-start.5 = (f32[4,16,128]{2,1,0:T(8,128)S(1)}, f32[4,16,128]{2,1,0:T(8,128)}, u32[]{:S(2)}) copy-start(f32[4,16,128]{2,1,0:T(8,128)} %param.11) | copy-start | bytes 98308
  4.8 6.2 %copy-start.2 = (f32[128,256]{1,0:T(8,128)S(1)}, f32[128,256]{1,0:T(8,128)}, u32[]{:S(2)}) copy-start(f32[128,256]{1,0:T(8,128)} %constant.6.clone.table.refs_12_) | copy-start | bytes 393220
  4.8 6.2 %copy-start.6 = (f32[8,256]{1,0:T(8,128)S(1)}, f32[8,256]{1,0:T(8,128)}, u32[]{:S(2)}) copy-start(f32[8,256]{1,0:T(8,128)} %constant.7.clone.factors.refs_13_) | copy-start | bytes 24580
  4.9 10.0 %collective-permute-start.1 = (f32[216,128]{1,0:T(8,128)S(1)}, f32[216,128]{1,0:T(8,128)S(1)}, u32[]{:S(2)}, u32[]{:S(2)}) collective-permute-start(f32[216,128]{1,0:T(8,128)S(1)} %get-tuple-element.27), channel_id=1, source_target_pairs={{0,4},{4,8},{8,12},{12,16},{16,20},{20,24},{24,28},{28,0},{1,5},{5... | collective-permute-start | bytes 331784 | tf_op jit(solution)/shard_map/ppermute | solution.py:61
  7.9 7.0 %collective-permute-start = (f32[192,128]{1,0:T(8,128)S(1)}, f32[192,128]{1,0:T(8,128)S(1)}, u32[]{:S(2)}, u32[]{:S(2)}) collective-permute-start(f32[192,128]{1,0:T(8,128)S(1)} %get-tuple-element.26), channel_id=1, source_target_pairs={{0,28},{4,0},{8,4},{12,8},{16,12},{20,16},{24,20},{28,24},{1,29},{... | collective-permute-start | bytes 294920 | tf_op jit(solution)/shard_map/ppermute | solution.py:61
  14.9 5.0 %copy-start.3 = (bf16[4,3,8,16,128]{4,3,2,1,0:T(8,128)(2,1)S(1)}, bf16[4,3,8,16,128]{4,3,2,1,0:T(8,128)(2,1)}, u32[]{:S(2)}) copy-start(bf16[4,3,8,16,128]{4,3,2,1,0:T(8,128)(2,1)} %param.18) | copy-start | bytes 1179652
  15.6 4.2 %collective-permute-start.2 = (f32[48,128]{1,0:T(8,128)S(1)}, f32[48,128]{1,0:T(8,128)S(1)}, u32[]{:S(2)}, u32[]{:S(2)}) collective-permute-start(f32[48,128]{1,0:T(8,128)S(1)} %get-tuple-element.36), channel_id=1, source_target_pairs={{0,3},{1,0},{2,1},{3,2},{4,7},{5,4},{6,5},{7,6},{8,11},{9,8},{10,9... | collective-permute-start | bytes 73736 | tf_op jit(solution)/shard_map/ppermute | solution.py:61
  15.6 4.2 %collective-permute-start.3 = (f32[48,128]{1,0:T(8,128)S(1)}, f32[48,128]{1,0:T(8,128)S(1)}, u32[]{:S(2)}, u32[]{:S(2)}) collective-permute-start(f32[48,128]{1,0:T(8,128)S(1)} %get-tuple-element.37), channel_id=1, source_target_pairs={{0,1},{1,2},{2,3},{3,0},{4,5},{5,6},{6,7},{7,4},{8,9},{9,10},{10,1... | collective-permute-start | bytes 73736 | tf_op jit(solution)/shard_map/ppermute | solution.py:61
  16.1 3.7 %collective-permute-start.4 = (f32[24,128]{1,0:T(8,128)S(1)}, f32[24,128]{1,0:T(8,128)S(1)}, u32[]{:S(2)}, u32[]{:S(2)}) collective-permute-start(f32[24,128]{1,0:T(8,128)S(1)} %get-tuple-element.38), channel_id=1, source_target_pairs={{0,2},{1,3},{2,0},{3,1},{4,6},{5,7},{6,4},{7,5},{8,10},{9,11},{10,... | collective-permute-start | bytes 36872 | tf_op jit(solution)/shard_map/ppermute | solution.py:61
  19.8 0.7 %copy-start.9 = (f32[3,4]{1,0:T(4,128)S(1)}, f32[3,4]{1,0:T(4,128)}, u32[]{:S(2)}) copy-start(f32[3,4]{1,0:T(4,128)} %refs_0_.1) | copy-start | bytes 148
  19.8 0.7 %copy-start.10 = (f32[3]{0:T(128)S(1)}, f32[3]{0:T(128)}, u32[]{:S(2)}) copy-start(f32[3]{0:T(128)} %refs_1_.1) | copy-start | bytes 40

commit v2 on v1

--- a/solution.py
+++ b/solution.py
@@ -22,26 +22,29 @@
 ROWS = 24
 OWN = 16
 SLOT = 64
-
-
-def in_vmem(x):
-    return pltpu.with_memory_space_constraint(x, pltpu.VMEM)
-
-
-def call(kernel, outs, ins, aliases=None, scratch=()):
+PLANES = 3 * Z
+
+VM = pl.BlockSpec(memory_space=pltpu.VMEM)
+ANY = pl.BlockSpec(memory_space=pl.ANY)
+
+
+def vmem(*shape, dtype=jnp.float32):
+    return pltpu.VMEM(shape, dtype)
+
+
+def call(kernel, outs, ins, aliases=None, scratch=(), in_specs=None):
+    space = pltpu.VMEM if in_specs is None else pltpu.HBM
+    in_specs = in_specs or [VM] * len(ins)
+    ins = [pltpu.with_memory_space_constraint(x, space) for x in ins]
     return pl.pallas_call(
         kernel,
         out_shape=outs,
-        in_specs=[pl.BlockSpec(memory_space=pltpu.VMEM)] * len(ins),
-        out_specs=[pl.BlockSpec(memory_space=pltpu.VMEM)] * len(outs),
+        in_specs=in_specs,
+        out_specs=[VM] * len(outs),
         scratch_shapes=list(scratch),
         input_output_aliases=aliases or {},
         compiler_params=pltpu.CompilerParams(vmem_limit_bytes=32 * 1024 * 1024),
-    )(*[in_vmem(x) for x in ins])
-
-
-def vmem(*shape):
-    return pltpu.VMEM(shape, jnp.float32)
+    )(*ins)
 
 
 def lanes(rows):
@@ -56,7 +59,7 @@
     return pltpu.roll(x, by % x.shape[0], 0)
 
 
-def passed_along(x, axis, by):
+def sent(x, axis, by):
     size = lax.axis_size(axis)
     return lax.ppermute(x, axis, [(i, (i + by) % size) for i in range(size)])
 
@@ -77,39 +80,98 @@
     rows[1] = np.exp(targets / reach)
     rows[2, :CY] = np.exp(source / reach)
     rows[3, :CY] = np.exp(-source / reach)
-    spread = np.zeros((16, 128))
-    spread[np.arange(128) // TILE, np.arange(128)] = 1.0
-    return (
-        jnp.asarray(table, jnp.float32),
-        jnp.asarray(rows, jnp.float32),
-        jnp.asarray(spread, jnp.float32),
-    )
-
-
-def pack_rows_kernel(electric, magnetic, density, material, mask, spread, to_prev, to_next):
-    cells = jnp.dot(
-        mask[...].astype(jnp.float32), spread[...], preferred_element_type=jnp.float32
-    )
+    return np.concatenate([table, rows], 0).astype(np.float32)
+
+
+def edge_window(planes):
+    rows = planes[0].shape[0]
+    lane = lanes(rows)
+    window = (lane < 4) | (lane >= 124)
+    gathered = planes[7]
+    for z in range(6, -1, -1):
+        gathered = jnp.where(window, planes[z], roll(gathered, 16))
+    return gathered
+
+
+def edge_pairs(groups):
+    lane = lanes(groups[0][0].shape[0])
+    first = (lane & 15) < 8
+    found = [edge_window(planes) for planes in groups]
+    return [
+        jnp.where(first, roll(found[2 * i], 4), roll(found[2 * i + 1], 12)) for i in range(4)
+    ]
+
+
+def edge_messages(pairs):
+    quarter = (lanes(pairs[0].shape[0]) >> 2) & 3
+
+    def pick(a, b, c, d):
+        return jnp.where(quarter < 2, jnp.where(quarter == 0, a, b), jnp.where(quarter == 2, c, d))
+
+    left, right = [], []
+    for one, two in ((pairs[0], pairs[1]), (pairs[2], pairs[3])):
+        left.append(pick(roll(one, -4), roll(one, -8), roll(two, 4), two))
+        right.append(pick(one, roll(one, -4), roll(two, 8), roll(two, 4)))
+    return left, right
+
+
+def density_planes(layers, cells, rising, falling):
+    place = lanes(cells.shape[0]) & 3
+    planes = []
+    for layer in layers:
+        up = jnp.sum(layer * rising, axis=1, keepdims=True)
+        down = jnp.sum(layer * falling, axis=1, keepdims=True)
+        planes += [layer, jnp.where(place == 0, up, jnp.where(place == 1, down, cells))]
+    return planes
+
+
+def pack_kernel(
+    electric, magnetic, density, material, mask, table_in, mtable_in, contrast_in,
+    to_prev, to_next, e_all, h_all, d_all, m_own, c_all, table, mtable, contrast,
+    mask_v, sems,
+):
+    copies = []
+    for i, (source, target) in enumerate(
+        (
+            (electric, e_all.reshape(PLANES, ROWS, 128).at[:, 0:OWN, :]),
+            (magnetic, h_all.reshape(PLANES, ROWS, 128).at[:, 0:OWN, :]),
+            (density, d_all.reshape(DZ, ROWS, 128).at[:, 0:OWN, :]),
+            (material, m_own),
+            (mask, mask_v),
+            (table_in, table),
+            (mtable_in, mtable),
+            (contrast_in, contrast),
+        )
+    ):
+        copy = pltpu.make_async_copy(source, target, sems.at[i])
+        copy.start()
+        copies.append(copy)
+    for copy in copies:
+        copy.wait()
+
+    cells = cell_rows(mask_v[...])
+    c_all[0:TILE, :] = jnp.broadcast_to(cells[0:1], (TILE, 128))
+    c_all[TILE:OWN, :] = jnp.broadcast_to(cells[1:2], (TILE, 128))
 
     def e(channel, row):
-        return electric[pl.ds(channel * 128 + row, Z, stride=OWN), :]
+        return e_all[pl.ds(channel * Z * ROWS + row, Z, stride=ROWS), :]
 
     def h(channel, row):
-        return magnetic[pl.ds(channel * 128 + row, Z, stride=OWN), :]
+        return h_all[pl.ds(channel * Z * ROWS + row, Z, stride=ROWS), :]
 
     def ahead_part(row):
         part_y = h(1, row) + courant * (e(2, row + 1) - e(2, row))
         part_z = h(2, row) - courant * (e(1, row + 1) - e(1, row))
         return part_y, part_z
 
-    for out, first, mask_row in ((to_prev, 0, 0), (to_next, OWN - 3, 1)):
+    for out, first, mask_row in ((to_next, OWN - 3, 1), (to_prev, 0, 0)):
         for slot in range(3):
             row, at = first + slot, slot * SLOT
             for channel in range(3):
                 out[at + 8 * channel : at + 8 * channel + 8, :] = e(channel, row)
                 out[at + 24 + 8 * channel : at + 32 + 8 * channel, :] = h(channel, row)
-            out[at + 48 : at + 56, :] = material[pl.ds(row, Z, stride=OWN), :].astype(jnp.float32)
-            out[at + 56 : at + 60, :] = density[pl.ds(row, DZ, stride=OWN), :]
+            out[at + 48 : at + 56, :] = m_own[pl.ds(row, Z, stride=OWN), :].astype(jnp.float32)
+            out[at + 56 : at + 60, :] = d_all[pl.ds(row, DZ, stride=ROWS), :]
             out[at + 60 : at + 64, :] = jnp.broadcast_to(cells[mask_row : mask_row + 1], (4, 128))
     part_y, part_z = ahead_part(2)
     to_prev[2 * SLOT + 32 : 2 * SLOT + 40, :] = part_y
@@ -120,81 +182,26 @@
     to_next[3 * SLOT + 16 : 3 * SLOT + 24, :] = part_z
 
 
-def edge_window(planes):
-    rows = planes[0].shape[0]
-    lane = lanes(rows)
-    window = (lane < 4) | (lane >= 124)
-    gathered = planes[7]
-    for z in range(6, -1, -1):
-        gathered = jnp.where(window, planes[z], roll(gathered, 16))
-    return gathered
-
-
-def edge_pairs(groups):
-    lane = lanes(groups[0][0].shape[0])
-    first = (lane & 15) < 8
-    found = [edge_window(planes) for planes in groups]
-    return [
-        jnp.where(first, roll(found[2 * i], 4), roll(found[2 * i + 1], 12)) for i in range(4)
-    ]
-
-
-def edge_messages(pairs):
-    quarter = (lanes(pairs[0].shape[0]) >> 2) & 3
-
-    def pick(a, b, c, d):
-        return jnp.where(quarter < 2, jnp.where(quarter == 0, a, b), jnp.where(quarter == 2, c, d))
-
-    left, right = [], []
-    for one, two in ((pairs[0], pairs[1]), (pairs[2], pairs[3])):
-        left.append(pick(roll(one, -4), roll(one, -8), roll(two, 4), two))
-        right.append(pick(one, roll(one, -4), roll(two, 8), roll(two, 4)))
-    return left, right
-
-
-def density_planes(layers, cells, rising, falling):
-    place = lanes(cells.shape[0]) & 3
-    planes = []
-    for layer in layers:
-        up = jnp.sum(layer * rising, axis=1, keepdims=True)
-        down = jnp.sum(layer * falling, axis=1, keepdims=True)
-        planes += [layer, jnp.where(place == 0, up, jnp.where(place == 1, down, cells))]
-    return planes
-
-
 def own_kernel(
-    electric, magnetic, density, material, mask, table, factors, spread,
-    e_all, h_all, m_all, d_all, c_all, local, pairs_out, left_out, right_out,
+    e_all, h_all, d_all, m_own, c_all, table,
+    pairs_out, left_out, right_out, m_all, local,
 ):
-    cells2 = jnp.dot(
-        mask[...].astype(jnp.float32), spread[...], preferred_element_type=jnp.float32
-    )
-    cells = jnp.concatenate(
-        [jnp.broadcast_to(cells2[i : i + 1], (TILE, 128)) for i in range(2)], 0
-    )
-    c_all[0:OWN, :] = cells
     groups = []
-    for source, target in ((electric, e_all), (magnetic, h_all)):
+    for ref in (e_all, h_all):
         for channel in range(3):
-            planes = []
-            for z in range(Z):
-                p = channel * Z + z
-                plane = source[p * OWN : (p + 1) * OWN, :]
-                target[p * ROWS : p * ROWS + OWN, :] = plane
-                planes.append(plane)
-            groups.append(planes)
+            groups.append(
+                [ref[(channel * Z + z) * ROWS : (channel * Z + z) * ROWS + OWN, :] for z in range(Z)]
+            )
     planes = []
     for z in range(Z):
-        plane = material[z * OWN : (z + 1) * OWN, :].astype(jnp.float32)
+        plane = m_own[z * OWN : (z + 1) * OWN, :].astype(jnp.float32)
         m_all[z * ROWS : z * ROWS + OWN, :] = plane
         planes.append(plane)
     groups.append(planes)
-    layers = []
-    for layer in range(DZ):
-        plane = density[layer * OWN : (layer + 1) * OWN, :]
-        d_all[layer * ROWS : layer * ROWS + OWN, :] = plane
-        layers.append(plane)
-    groups.append(density_planes(layers, cells, factors[2:3, 0:128], factors[3:4, 0:128]))
+    layers = [d_all[l * ROWS : l * ROWS + OWN, :] for l in range(DZ)]
+    groups.append(
+        density_planes(layers, c_all[0:OWN, :], table[130:131, 0:128], table[131:132, 0:128])
+    )
     pairs = edge_pairs(groups)
     left, right = edge_messages(pairs)
     for i in range(4):
@@ -203,16 +210,16 @@
         left_out[i * ROWS : i * ROWS + OWN, :] = left[i]
         right_out[i * ROWS : i * ROWS + OWN, :] = right[i]
     smooth = jnp.dot(
-        density[...], table[...], precision=lax.Precision.HIGHEST,
+        jnp.concatenate(layers, 0), table[0:128, :], precision=lax.Precision.HIGHEST,
         preferred_element_type=jnp.float32,
     )
-    for layer in range(DZ):
-        local[layer * ROWS : layer * ROWS + OWN, :] = smooth[layer * OWN : (layer + 1) * OWN]
+    for l in range(DZ):
+        local[l * ROWS : l * ROWS + OWN, :] = smooth[l * OWN : (l + 1) * OWN]
 
 
 def halo_kernel(
-    from_next, from_prev, e_in, h_in, m_in, d_in, c_in, pairs_in, left_in, right_in, factors,
-    e_all, h_all, m_all, d_all, c_all, pairs_out, left_out, right_out, sums_out,
+    from_next, from_prev, e_in, h_in, d_in, c_in, m_in, pairs_in, left_in, right_in, table,
+    e_all, h_all, d_all, c_all, m_all, pairs_out, left_out, right_out, sums_out,
 ):
     for got, first in ((from_next, 16), (from_prev, 21)):
         for slot in range(3):
@@ -251,9 +258,10 @@
                 [target[(channel * Z + z) * ROWS + OWN : (channel * Z + z + 1) * ROWS, :] for z in range(Z)]
             )
     groups.append([m_all[z * ROWS + OWN : (z + 1) * ROWS, :] for z in range(Z)])
-    layers = [d_all[layer * ROWS + OWN : (layer + 1) * ROWS, :] for layer in range(DZ)]
-    cells = c_all[OWN:ROWS, :]
-    groups.append(density_planes(layers, cells, factors[2:3, 0:128], factors[3:4, 0:128]))
+    layers = [d_all[l * ROWS + OWN : (l + 1) * ROWS, :] for l in range(DZ)]
+    groups.append(
+        density_planes(layers, c_all[OWN:ROWS, :], table[130:131, 0:128], table[131:132, 0:128])
+    )
     pairs = edge_pairs(groups)
     left, right = edge_messages(pairs)
     for i in range(4):
@@ -265,6 +273,37 @@
     sums_out[OWN:ROWS, :] = left[1]
 
 
+def background_kernel(m_all, d_all, mtable, table, local_in, background, local):
+    smooth = jnp.dot(
+        jnp.concatenate([d_all[l * ROWS + OWN : (l + 1) * ROWS, :] for l in range(DZ)], 0),
+        table[0:128, :], precision=lax.Precision.HIGHEST, preferred_element_type=jnp.float32,
+    )
+    for l in range(DZ):
+        local[l * ROWS + OWN : (l + 1) * ROWS, :] = smooth[l * 8 : (l + 1) * 8]
+    entries = mtable[...]
+    for z in range(Z):
+        kind = m_all[z * ROWS : (z + 1) * ROWS, :]
+        for channel in range(3):
+            p = channel * Z + z
+            background[p * ROWS : (p + 1) * ROWS, :] = looked_up(kind, entries, channel)
+
+
+def looked_up(kind, entries, channel):
+    one = [entries[channel : channel + 1, i : i + 1] for i in range(MATS)]
+    return jnp.where(
+        kind < 1.5, jnp.where(kind < 0.5, one[0], one[1]), jnp.where(kind < 2.5, one[2], one[3])
+    )
+
+
+def cell_rows(mask):
+    spread = lax.broadcasted_iota(jnp.int32, (mask.shape[1], 128), 0) == (
+        lanes(mask.shape[1]) // TILE
+    )
+    return jnp.dot(
+        mask.astype(jnp.float32), spread.astype(jnp.float32), preferred_element_type=jnp.float32
+    )
+
+
 def project(values):
     base = math.tanh(sharpness * threshold)
     bottom = base + math.tanh(sharpness * (1.0 - threshold))
@@ -288,10 +327,12 @@
         )
 
     def kernel(*refs):
-        material_table, contrast, from_right, from_left = refs[:4]
-        rest = refs[4 : 4 + others]
-        (e_in, h_in, m_all, d_all, c_all, pairs, local, table, factors, forward,
-         e_final, h_final, gradient, e_all, h_all, inverse, se, sh, si, gained) = refs[4 + others :]
+        from_right, from_left = refs[:2]
+        rest = refs[2 : 2 + others]
+        (e_in, h_in, d_all, c_all, background, pairs, local, table, mtable, contrast_in, forward,
+         e_final, h_final, gradient, e_all, h_all, inverse, se, sh, si, gained) = refs[2 + others :]
+        entries = mtable[...]
+        contrast = [contrast_in[0:1, c : c + 1] for c in range(3)]
         lane = lanes(ROWS)
         place = lane & 15
         odd = ((lane >> 4) & 1) == 1
@@ -327,10 +368,6 @@
         sums = lane_factor(1) * got_left[1] + lane_factor(devices - 1) * got_right[1]
         for i, other in enumerate(rest):
             sums = sums + lane_factor(2 + i) * other[...]
-        halo_local = jnp.dot(
-            jnp.concatenate([d_all[l * ROWS + OWN : (l + 1) * ROWS, :] for l in range(DZ)], 0),
-            table[...], precision=lax.Precision.HIGHEST, preferred_element_type=jnp.float32,
-        )
         strip_smooth = jnp.zeros((ROWS, 128), jnp.float32)
         designs, slopes = [], []
         cells = c_all[...]
@@ -338,10 +375,9 @@
             at = (2 * l + 1) * 16 + 12
             up = jnp.broadcast_to(sums[:, at : at + 1], (ROWS, 128))
             down = jnp.broadcast_to(sums[:, at + 1 : at + 2], (ROWS, 128))
-            own = local[l * ROWS : l * ROWS + OWN, :]
-            both = jnp.concatenate([own, halo_local[l * 8 : (l + 1) * 8]], 0)
-            smooth = both[:, :128] + factors[0:1, :128] * up + factors[1:2, :128] * down
-            far = both[:, 128:] + factors[0:1, 128:] * up + factors[1:2, 128:] * down
+            both = local[l * ROWS : (l + 1) * ROWS, :]
+            smooth = both[:, :128] + table[128:129, :128] * up + table[129:130, :128] * down
+            far = both[:, 128:] + table[128:129, 128:] * up + table[129:130, 128:] * down
             strip_smooth = jnp.where(layer_of == l, far, strip_smooth)
             filtered = 0.5 * d_all[l * ROWS : (l + 1) * ROWS, :] + (0.5 / norm_total) * smooth
             projected, slope = project(filtered)
@@ -356,21 +392,17 @@
         projected, _ = project(0.5 * strip_density + (0.5 / norm_total) * strip_smooth)
         strip_design = strip_cells * projected
 
-        def invert(kind, design, channel):
-            background = jnp.where(
-                kind < 1.5,
-                jnp.where(kind < 0.5, material_table[channel, 0], material_table[channel, 1]),
-                jnp.where(kind < 2.5, material_table[channel, 2], material_table[channel, 3]),
+        for channel in range(3):
+            own = looked_up(strip_material, entries, channel)
+            si[channel * ROWS : (channel + 1) * ROWS, :] = courant / (
+                own + strip_design * contrast[channel]
             )
-            return courant / (background + design * contrast[channel])
-
-        for channel in range(3):
-            si[channel * ROWS : (channel + 1) * ROWS, :] = invert(strip_material, strip_design, channel)
         for z in range(Z):
-            kind = m_all[z * ROWS : (z + 1) * ROWS, :]
             for channel in range(3):
                 p = channel * Z + z
-                inverse[p * ROWS : (p + 1) * ROWS, :] = invert(kind, designs[z // 2], channel)
+                inverse[p * ROWS : (p + 1) * ROWS, :] = courant / (
+                    background[p * ROWS : (p + 1) * ROWS, :] + designs[z // 2] * contrast[channel]
+                )
         gained[...] = jnp.zeros_like(gained)
 
         zero = jnp.zeros((ROWS, 128), jnp.float32)
@@ -464,61 +496,58 @@
     devices = lax.axis_size("gy")
     count = density.shape[2] * devices
     reach = 4.0 * CY
-    table, factors, spread = filter_constants(count, reach)
-    e2 = electric.reshape(-1, 128)
-    h2 = magnetic.reshape(-1, 128)
-    d2 = density.reshape(-1, 128)
-    m2 = material.reshape(-1, 128)
-    f2 = forward_fields.reshape(STEPS, 3 * Z, OWN, 128)
-
-    to_prev, to_next = call(
-        pack_rows_kernel, [vmem(3 * SLOT, 128), vmem(3 * SLOT + 24, 128)],
-        [e2, h2, d2, m2, tile_mask, spread],
-    )
-    from_prev = passed_along(to_next, "gx", 1)
-    from_next = passed_along(to_prev, "gx", -1)
-    e_all, h_all, m_all, d_all, c_all, local, pairs, left, right = call(
+    constants = filter_constants(count, reach)
+
+    to_prev, to_next, e_all, h_all, d_all, m_own, c_all, table, mtable, contrasts = call(
+        pack_kernel,
+        [vmem(3 * SLOT, 128), vmem(3 * SLOT + 24, 128),
+         vmem(PLANES * ROWS, 128), vmem(PLANES * ROWS, 128), vmem(DZ * ROWS, 128),
+         vmem(Z * OWN, 128, dtype=jnp.int32), vmem(ROWS, 128), vmem(*constants.shape),
+         vmem(3, MATS), vmem(1, 3)],
+        [electric.reshape(PLANES, OWN, 128), magnetic.reshape(PLANES, OWN, 128), density,
+         material.reshape(Z * OWN, 128), tile_mask, constants, material_table,
+         contrast.reshape(1, 3)],
+        scratch=[vmem(*tile_mask.shape, dtype=jnp.int32), pltpu.SemaphoreType.DMA((8,))],
+        in_specs=[ANY] * 8,
+    )
+    from_prev = sent(to_next, "gx", 1)
+    from_next = sent(to_prev, "gx", -1)
+    pairs, left, right, m_all, local = call(
         own_kernel,
-        [vmem(3 * Z * ROWS, 128), vmem(3 * Z * ROWS, 128), vmem(Z * ROWS, 128),
-         vmem(DZ * ROWS, 128), vmem(ROWS, 128), vmem(DZ * ROWS, 256), vmem(4 * ROWS, 128),
-         vmem(2 * ROWS, 128), vmem(2 * ROWS, 128)],
-        [e2, h2, d2, m2, tile_mask, table, factors, spread],
-    )
-    e_all, h_all, m_all, d_all, c_all, pairs, left, right, sums = call(
+        [vmem(4 * ROWS, 128), vmem(2 * ROWS, 128), vmem(2 * ROWS, 128), vmem(Z * ROWS, 128),
+         vmem(DZ * ROWS, 256)],
+        [e_all, h_all, d_all, m_own, c_all, table],
+    )
+    e_all, h_all, d_all, c_all, m_all, pairs, left, right, sums = call(
         halo_kernel,
-        [vmem(3 * Z * ROWS, 128), vmem(3 * Z * ROWS, 128), vmem(Z * ROWS, 128),
-         vmem(DZ * ROWS, 128), vmem(ROWS, 128), vmem(4 * ROWS, 128),
+        [vmem(PLANES * ROWS, 128), vmem(PLANES * ROWS, 128), vmem(DZ * ROWS, 128),
+         vmem(ROWS, 128), vmem(Z * ROWS, 128), vmem(4 * ROWS, 128),
          vmem(2 * ROWS, 128), vmem(2 * ROWS, 128), vmem(ROWS, 128)],
-        [from_next, from_prev, e_all, h_all, m_all, d_all, c_all, pairs, left, right, factors],
+        [from_next, from_prev, e_all, h_all, d_all, c_all, m_all, pairs, left, right, table],
         aliases={2: 0, 3: 1, 4: 2, 5: 3, 6: 4, 7: 5, 8: 6, 9: 7},
     )
-    from_left = passed_along(right, "gy", 1)
-    from_right = passed_along(left, "gy", -1)
-    rest = [passed_along(sums, "gy", m) for m in range(2, devices - 1)]
-    smem = pl.BlockSpec(memory_space=pltpu.SMEM)
-    in_v = pl.BlockSpec(memory_space=pltpu.VMEM)
-    operands = [from_right, from_left] + rest + [
-        e_all, h_all, m_all, d_all, c_all, pairs, local, table, factors, f2,
-    ]
-    at = 4 + len(rest)
-    outs = pl.pallas_call(
+    from_left = sent(right, "gy", 1)
+    from_right = sent(left, "gy", -1)
+    rest = [sent(sums, "gy", m) for m in range(2, devices - 1)]
+    background, local = call(
+        background_kernel, [vmem(PLANES * ROWS, 128), vmem(DZ * ROWS, 256)],
+        [m_all, d_all, mtable, table, local], aliases={4: 1},
+    )
+    at = 2 + len(rest)
+    outs = call(
         step_kernel(count, reach, len(rest)),
-        out_shape=[
-            jax.ShapeDtypeStruct(e2.shape, jnp.float32),
-            jax.ShapeDtypeStruct(h2.shape, jnp.float32),
-            jax.ShapeDtypeStruct(d2.shape, jnp.float32),
-            vmem(3 * Z * ROWS, 128),
-            vmem(3 * Z * ROWS, 128),
+        [jax.ShapeDtypeStruct((PLANES * OWN, 128), jnp.float32),
+         jax.ShapeDtypeStruct((PLANES * OWN, 128), jnp.float32),
+         jax.ShapeDtypeStruct((DZ * OWN, 128), jnp.float32),
+         vmem(PLANES * ROWS, 128), vmem(PLANES * ROWS, 128)],
+        [from_right, from_left] + rest + [
+            e_all, h_all, d_all, c_all, background, pairs, local, table,
+            mtable, contrasts, forward_fields.reshape(STEPS, PLANES, OWN, 128),
         ],
-        in_specs=[smem, smem] + [in_v] * len(operands),
-        out_specs=[in_v] * 5,
-        scratch_shapes=[
-            vmem(3 * Z * ROWS, 128), vmem(3 * ROWS, 128), vmem(3 * ROWS, 128), vmem(3 * ROWS, 128),
-            vmem(DZ * OWN, 128),
-        ],
-        input_output_aliases={at: 3, at + 1: 4},
-        compiler_params=pltpu.CompilerParams(vmem_limit_bytes=32 * 1024 * 1024),
-    )(material_table, contrast, *[in_vmem(x) for x in operands])
+        aliases={at: 3, at + 1: 4},
+        scratch=[vmem(PLANES * ROWS, 128), vmem(3 * ROWS, 128), vmem(3 * ROWS, 128),
+                 vmem(3 * ROWS, 128), vmem(DZ * OWN, 128)],
+    )
     return (
         outs[0].reshape(electric.shape), outs[1].reshape(magnetic.shape),
         outs[2].reshape(density.shape),

time: 24 us -> 19.8 us (0.83)
  local copies, waits for them, and re-layouts: 4.81 us -> 0.01 us
  Pallas kernels: 4.75 us -> 5.69 us
    unnamed x22 -> x2, local copies, waits for them, and re-layouts: 4.81 us -> 0.01 us
    pallas_call x4 -> x5, Pallas kernels: 4.75 us -> 5.69 us  [call(): pl.pallas_call(kernel, out_shape=outs, in_specs=in_specs, out_specs=[VM]...]
  transfers between devices with their start and end apart: 5 -> 5, of which waited for: 2 -> 2; matrix products, arithmetic and copies ran while one was open for 0% -> 0% of each run, Pallas kernels for 3% -> 5%
where the time goes in v2:
time: 19.8 us; the launch traced here: 19.7 us
  starting transfers between devices  8.16 us (41%)
  Pallas kernels  5.69 us (29%)
  waiting for transfers between devices  5.18 us (26%)
  between operations  0.67 us (3%)
    ppermute x5, starting transfers between devices, sent(): return lax.ppermute(x, axis, [(i, (i + by) % size) for i in range(size)])  8.16 us
    pallas_call x5, Pallas kernels, call(): pl.pallas_call(kernel, out_shape=outs, in_specs=in_specs, out_specs=[VM]...  5.69 us
    ppermute x5, waiting for transfers between devices, sent(): return lax.ppermute(x, axis, [(i, (i + by) % size) for i in range(size)])  5.18 us
  transfers between devices with their start and end apart: 5, of which 2 were waited for; matrix products, arithmetic and copies ran while one was open for 0% of the time, Pallas kernels for 5%

profile of v2, /device:TPU:0, one launch (start us, length us, event | category | flops | bytes accessed | tf_op | source)
XLA Modules:
  0.0 19.7 jit_solution(7889844720457641808)
XLA Ops:
  0.6 1.4 %shard_map.112 = (f32[192,128]{1,0:T(8,128)S(1)}, f32[216,128]{1,0:T(8,128)S(1)}, f32[576,128]{1,0:T(8,128)S(1)}, f32[576,128]{1,0:T(8,128)S(1)}, f32[96,128]{1,...) custom-call(f32[24,16,128]{2,1,0:T(8,128)} %bitcast.9, ...), custom_call_target="tpu_custom_call" | custom-call | tf_op jit(solution)/shard_map/pallas_call | solution.py:39
  2.0 3.0 %collective-permute-start.1 = (f32[216,128]{1,0:T(8,128)S(1)}, f32[216,128]{1,0:T(8,128)S(1)}, u32[]{:S(2)}, u32[]{:S(2)}) collective-permute-start(f32[216,128]{1,0:T(8,128)S(1)} %get-tuple-element.33), channel_id=1, source_target_pairs={{0,4},{4,8},{8,12},{12,16},{16,20},{20,24},{24,28},{28,0},{1,5},{5... | collective-permute-start | bytes 331784 | tf_op jit(solution)/shard_map/ppermute | solution.py:64
  5.1 3.1 %collective-permute-start = (f32[192,128]{1,0:T(8,128)S(1)}, f32[192,128]{1,0:T(8,128)S(1)}, u32[]{:S(2)}, u32[]{:S(2)}) collective-permute-start(f32[192,128]{1,0:T(8,128)S(1)} %get-tuple-element.32), channel_id=1, source_target_pairs={{0,28},{4,0},{8,4},{12,8},{16,12},{20,16},{24,20},{28,24},{1,29},{... | collective-permute-start | bytes 294920 | tf_op jit(solution)/shard_map/ppermute | solution.py:64
  8.2 0.7 %shard_map.113 = (f32[96,128]{1,0:T(8,128)S(1)}, f32[48,128]{1,0:T(8,128)S(1)}, f32[48,128]{1,0:T(8,128)S(1)}, f32[192,128]{1,0:T(8,128)S(1)}, f32[96,256]{1,0:T(8,128)S(1)}) custom-call(f32[576,128]{1,0:T(8,128)S(1)} %get-tuple-element.34.e_all.e_in, f32[576,128]{1,0:T(8,128)S(1)} %get-tuple-element.35.h_all.h_in, ...), custom_call_target="tpu_custom_call" | custom-call | tf_op jit(solution)/shard_map/pallas_call | solution.py:39
  8.9 3.2 %collective-permute-done.from_next = f32[192,128]{1,0:T(8,128)S(1)} collective-permute-done((f32[192,128]{1,0:T(8,128)S(1)}, f32[192,128]{1,0:T(8,128)S(1)}, u32[]{:S(2)}, u32[]{:S(2)}) %collective-permute-start) | collective-permute-done | bytes 98336 | tf_op jit(solution)/shard_map/ppermute | solution.py:64
  12.0 0.0 collective-permute-done.1.from_prev
  12.0 0.7 %shard_map.114 = (f32[576,128]{1,0:T(8,128)S(1)}, f32[576,128]{1,0:T(8,128)S(1)}, f32[96,128]{1,0:T(8,128)S(1)}, f32[24,128]{1,0:T(8,128)S(1)}, f32[192,128]{1,0...) custom-call(f32[192,128]{1,0:T(8,128)S(1)} %collective-permute-done., ...), custom_call_target="tpu_custom_call", output_to_operand_aliasing={{0}: (2, {}), {1}: (3, {}), {2}: (4, {}), {3}: (5, {}), {4}... | custom-call | tf_op jit(solution)/shard_map/pallas_call | solution.py:39
  12.7 0.0 copy-start
  12.7 0.0 collective-permute-start.2
  12.8 0.5 %collective-permute-start.3 = (f32[48,128]{1,0:T(8,128)S(1)}, f32[48,128]{1,0:T(8,128)S(1)}, u32[]{:S(2)}, u32[]{:S(2)}) collective-permute-start(f32[48,128]{1,0:T(8,128)S(1)} %get-tuple-element.45), channel_id=1, source_target_pairs={{0,1},{1,2},{2,3},{3,0},{4,5},{5,6},{6,7},{7,4},{8,9},{9,10},{10,1... | collective-permute-start | bytes 73736 | tf_op jit(solution)/shard_map/ppermute | solution.py:64
  13.3 1.5 %collective-permute-start.4 = (f32[24,128]{1,0:T(8,128)S(1)}, f32[24,128]{1,0:T(8,128)S(1)}, u32[]{:S(2)}, u32[]{:S(2)}) collective-permute-start(f32[24,128]{1,0:T(8,128)S(1)} %get-tuple-element.46), channel_id=1, source_target_pairs={{0,2},{1,3},{2,0},{3,1},{4,6},{5,7},{6,4},{7,5},{8,10},{9,11},{10,... | collective-permute-start | bytes 36872 | tf_op jit(solution)/shard_map/ppermute | solution.py:64
  14.8 0.2 shard_map.115
  15.0 2.0 %collective-permute-done.4.refs_2_ = f32[24,128]{1,0:T(8,128)S(1)} collective-permute-done((f32[24,128]{1,0:T(8,128)S(1)}, f32[24,128]{1,0:T(8,128)S(1)}, u32[]{:S(2)}, u32[]{:S(2)}) %collective-permute-start.4) | collective-permute-done | bytes 12320 | tf_op jit(solution)/shard_map/ppermute | solution.py:64
  17.0 0.0 collective-permute-done.2.refs_0_
  17.0 0.0 collective-permute-done.3.refs_1_
  17.0 0.0 copy-done
  17.0 2.7 %shard_map.116 = (f32[384,128]{1,0:T(8,128)}, f32[384,128]{1,0:T(8,128)}, f32[64,128]{1,0:T(8,128)}, f32[576,128]{1,0:T(8,128)S(1)}, f32[576,128]{1,0:T(8,128)S(1)}) custom-call(f32[48,128]{1,0:T(8,128)S(1)} %collective-permute-done.2.refs_0_, f32[48,128]{1,0:T(8,128)S(1)} %collective-permute-done.3.refs_1_, ...), custom_call_target="tpu_custom_call", output_to_operand_aliasing={{3}: (3, {}), {4}: (4, {})} | custom-call | tf_op jit(solution)/shard_map/pallas_call | solution.py:39
Async XLA Ops:
  2.0 10.0 %collective-permute-start.1 = (f32[216,128]{1,0:T(8,128)S(1)}, f32[216,128]{1,0:T(8,128)S(1)}, u32[]{:S(2)}, u32[]{:S(2)}) collective-permute-start(f32[216,128]{1,0:T(8,128)S(1)} %get-tuple-element.33), channel_id=1, source_target_pairs={{0,4},{4,8},{8,12},{12,16},{16,20},{20,24},{24,28},{28,0},{1,5},{5... | collective-permute-start | bytes 331784 | tf_op jit(solution)/shard_map/ppermute | solution.py:64
  5.1 7.0 %collective-permute-start = (f32[192,128]{1,0:T(8,128)S(1)}, f32[192,128]{1,0:T(8,128)S(1)}, u32[]{:S(2)}, u32[]{:S(2)}) collective-permute-start(f32[192,128]{1,0:T(8,128)S(1)} %get-tuple-element.32), channel_id=1, source_target_pairs={{0,28},{4,0},{8,4},{12,8},{16,12},{20,16},{24,20},{28,24},{1,29},{... | collective-permute-start | bytes 294920 | tf_op jit(solution)/shard_map/ppermute | solution.py:64
  12.7 4.3 %copy-start = (bf16[4,3,8,16,128]{4,3,2,1,0:T(8,128)(2,1)S(1)}, bf16[4,3,8,16,128]{4,3,2,1,0:T(8,128)(2,1)}, u32[]{:S(2)}) copy-start(bf16[4,3,8,16,128]{4,3,2,1,0:T(8,128)(2,1)} %param.16) | copy-start | bytes 1179652
  12.7 4.2 %collective-permute-start.2 = (f32[48,128]{1,0:T(8,128)S(1)}, f32[48,128]{1,0:T(8,128)S(1)}, u32[]{:S(2)}, u32[]{:S(2)}) collective-permute-start(f32[48,128]{1,0:T(8,128)S(1)} %get-tuple-element.44), channel_id=1, source_target_pairs={{0,3},{1,0},{2,1},{3,2},{4,7},{5,4},{6,5},{7,6},{8,11},{9,8},{10,9... | collective-permute-start | bytes 73736 | tf_op jit(solution)/shard_map/ppermute | solution.py:64
  12.8 4.2 %collective-permute-start.3 = (f32[48,128]{1,0:T(8,128)S(1)}, f32[48,128]{1,0:T(8,128)S(1)}, u32[]{:S(2)}, u32[]{:S(2)}) collective-permute-start(f32[48,128]{1,0:T(8,128)S(1)} %get-tuple-element.45), channel_id=1, source_target_pairs={{0,1},{1,2},{2,3},{3,0},{4,5},{5,6},{6,7},{7,4},{8,9},{9,10},{10,1... | collective-permute-start | bytes 73736 | tf_op jit(solution)/shard_map/ppermute | solution.py:64
  13.3 3.7 %collective-permute-start.4 = (f32[24,128]{1,0:T(8,128)S(1)}, f32[24,128]{1,0:T(8,128)S(1)}, u32[]{:S(2)}, u32[]{:S(2)}) collective-permute-start(f32[24,128]{1,0:T(8,128)S(1)} %get-tuple-element.46), channel_id=1, source_target_pairs={{0,2},{1,3},{2,0},{3,1},{4,6},{5,7},{6,4},{7,5},{8,10},{9,11},{10,... | collective-permute-start | bytes 36872 | tf_op jit(solution)/shard_map/ppermute | solution.py:64

commit v3 on v2

--- a/solution.py
+++ b/solution.py
@@ -21,7 +21,10 @@
 
 ROWS = 24
 OWN = 16
-SLOT = 64
+SLOT = 48
+KINDS = 3 * SLOT
+LAYERS = KINDS + 24
+EXTRA = LAYERS + 16
 PLANES = 3 * Z
 
 VM = pl.BlockSpec(memory_space=pltpu.VMEM)
@@ -84,13 +87,15 @@
 
 
 def edge_window(planes):
-    rows = planes[0].shape[0]
-    lane = lanes(rows)
-    window = (lane < 4) | (lane >= 124)
-    gathered = planes[7]
-    for z in range(6, -1, -1):
-        gathered = jnp.where(window, planes[z], roll(gathered, 16))
-    return gathered
+    lane = lanes(planes[0].shape[0])
+    width, by = 8, 16
+    while len(planes) > 1:
+        kept = ((lane + 4) & 127) < width
+        planes = [
+            jnp.where(kept, planes[i], roll(planes[i + 1], by)) for i in range(0, len(planes), 2)
+        ]
+        width, by = width + by, 2 * by
+    return planes[0]
 
 
 def edge_pairs(groups):
@@ -127,26 +132,20 @@
 
 def pack_kernel(
     electric, magnetic, density, material, mask, table_in, mtable_in, contrast_in,
-    to_prev, to_next, e_all, h_all, d_all, m_own, c_all, table, mtable, contrast,
+    to_prev, to_next, e_own, h_own, d_own, m_own, c_all, table, mtable, contrast,
     mask_v, sems,
 ):
     copies = []
-    for i, (source, target) in enumerate(
-        (
-            (electric, e_all.reshape(PLANES, ROWS, 128).at[:, 0:OWN, :]),
-            (magnetic, h_all.reshape(PLANES, ROWS, 128).at[:, 0:OWN, :]),
-            (density, d_all.reshape(DZ, ROWS, 128).at[:, 0:OWN, :]),
-            (material, m_own),
-            (mask, mask_v),
-            (table_in, table),
-            (mtable_in, mtable),
-            (contrast_in, contrast),
-        )
-    ):
+    moved = [
+        (mask, mask_v), (electric, e_own), (magnetic, h_own), (density, d_own), (material, m_own),
+    ]
+    needed = len(moved)
+    moved += [(table_in, table), (mtable_in, mtable), (contrast_in, contrast)]
+    for i, (source, target) in enumerate(moved):
         copy = pltpu.make_async_copy(source, target, sems.at[i])
         copy.start()
         copies.append(copy)
-    for copy in copies:
+    for copy in copies[:needed]:
         copy.wait()
 
     cells = cell_rows(mask_v[...])
@@ -154,10 +153,10 @@
     c_all[TILE:OWN, :] = jnp.broadcast_to(cells[1:2], (TILE, 128))
 
     def e(channel, row):
-        return e_all[pl.ds(channel * Z * ROWS + row, Z, stride=ROWS), :]
+        return e_own[pl.ds(channel * Z * OWN + row, Z, stride=OWN), :]
 
     def h(channel, row):
-        return h_all[pl.ds(channel * Z * ROWS + row, Z, stride=ROWS), :]
+        return h_own[pl.ds(channel * Z * OWN + row, Z, stride=OWN), :]
 
     def ahead_part(row):
         part_y = h(1, row) + courant * (e(2, row + 1) - e(2, row))
@@ -170,37 +169,53 @@
             for channel in range(3):
                 out[at + 8 * channel : at + 8 * channel + 8, :] = e(channel, row)
                 out[at + 24 + 8 * channel : at + 32 + 8 * channel, :] = h(channel, row)
-            out[at + 48 : at + 56, :] = m_own[pl.ds(row, Z, stride=OWN), :].astype(jnp.float32)
-            out[at + 56 : at + 60, :] = d_all[pl.ds(row, DZ, stride=ROWS), :]
-            out[at + 60 : at + 64, :] = jnp.broadcast_to(cells[mask_row : mask_row + 1], (4, 128))
+            out[KINDS + 8 * slot : KINDS + 8 * slot + 8, :] = (
+                m_own[pl.ds(row, Z, stride=OWN), :].astype(jnp.float32)
+            )
+            out[LAYERS + 4 * slot : LAYERS + 4 * slot + 4, :] = (
+                d_own[pl.ds(row, DZ, stride=OWN), :]
+            )
+        out[LAYERS + 12 : LAYERS + 16, :] = jnp.broadcast_to(
+            cells[mask_row : mask_row + 1], (4, 128)
+        )
     part_y, part_z = ahead_part(2)
     to_prev[2 * SLOT + 32 : 2 * SLOT + 40, :] = part_y
     to_prev[2 * SLOT + 40 : 2 * SLOT + 48, :] = part_z
     part_y, part_z = ahead_part(OWN - 4)
-    to_next[3 * SLOT : 3 * SLOT + 8, :] = e(0, OWN - 4)
-    to_next[3 * SLOT + 8 : 3 * SLOT + 16, :] = part_y
-    to_next[3 * SLOT + 16 : 3 * SLOT + 24, :] = part_z
+    to_next[EXTRA : EXTRA + 8, :] = e(0, OWN - 4)
+    to_next[EXTRA + 8 : EXTRA + 16, :] = part_y
+    to_next[EXTRA + 16 : EXTRA + 24, :] = part_z
+    for copy in copies[needed:]:
+        copy.wait()
 
 
 def own_kernel(
-    e_all, h_all, d_all, m_own, c_all, table,
-    pairs_out, left_out, right_out, m_all, local,
+    e_own, h_own, d_own, m_own, c_own, table,
+    e_all, h_all, d_all, c_all, pairs_out, left_out, right_out, m_all, local,
 ):
+    c_all[0:OWN, :] = c_own[...]
     groups = []
-    for ref in (e_all, h_all):
+    for source, target in ((e_own, e_all), (h_own, h_all)):
         for channel in range(3):
-            groups.append(
-                [ref[(channel * Z + z) * ROWS : (channel * Z + z) * ROWS + OWN, :] for z in range(Z)]
-            )
+            planes = []
+            for z in range(Z):
+                p = channel * Z + z
+                plane = source[p * OWN : (p + 1) * OWN, :]
+                target[p * ROWS : p * ROWS + OWN, :] = plane
+                planes.append(plane)
+            groups.append(planes)
     planes = []
     for z in range(Z):
         plane = m_own[z * OWN : (z + 1) * OWN, :].astype(jnp.float32)
         m_all[z * ROWS : z * ROWS + OWN, :] = plane
         planes.append(plane)
     groups.append(planes)
-    layers = [d_all[l * ROWS : l * ROWS + OWN, :] for l in range(DZ)]
+    layers = []
+    for l in range(DZ):
+        layers.append(d_own[l * OWN : (l + 1) * OWN, :])
+        d_all[l * ROWS : l * ROWS + OWN, :] = layers[l]
     groups.append(
-        density_planes(layers, c_all[0:OWN, :], table[130:131, 0:128], table[131:132, 0:128])
+        density_planes(layers, c_own[...], table[130:131, 0:128], table[131:132, 0:128])
     )
     pairs = edge_pairs(groups)
     left, right = edge_messages(pairs)
@@ -228,9 +243,9 @@
                 where = pl.ds(channel * Z * ROWS + row, Z, stride=ROWS)
                 e_all[where, :] = got[at + 8 * channel : at + 8 * channel + 8, :]
                 h_all[where, :] = got[at + 24 + 8 * channel : at + 32 + 8 * channel, :]
-            m_all[pl.ds(row, Z, stride=ROWS), :] = got[at + 48 : at + 56, :]
-            d_all[pl.ds(row, DZ, stride=ROWS), :] = got[at + 56 : at + 60, :]
-            c_all[row : row + 1, :] = got[at + 60 : at + 61, :]
+            m_all[pl.ds(row, Z, stride=ROWS), :] = got[KINDS + 8 * slot : KINDS + 8 * slot + 8, :]
+            d_all[pl.ds(row, DZ, stride=ROWS), :] = got[LAYERS + 4 * slot : LAYERS + 4 * slot + 4, :]
+            c_all[row : row + 1, :] = got[LAYERS + 12 : LAYERS + 13, :]
     zeros = jnp.zeros((Z, 128), jnp.float32)
     for channel in range(3):
         at = channel * Z * ROWS
@@ -241,10 +256,10 @@
         if channel > 0:
             e_all[pl.ds(at + 20, Z, stride=ROWS), :] = from_prev[8 * channel : 8 * channel + 8, :]
             h_all[pl.ds(at + 20, Z, stride=ROWS), :] = from_prev[
-                3 * SLOT + 8 * channel : 3 * SLOT + 8 * channel + 8, :
+                EXTRA + 8 * channel : EXTRA + 8 * channel + 8, :
             ]
         else:
-            e_all[pl.ds(at + 20, Z, stride=ROWS), :] = from_prev[3 * SLOT : 3 * SLOT + 8, :]
+            e_all[pl.ds(at + 20, Z, stride=ROWS), :] = from_prev[EXTRA : EXTRA + 8, :]
             h_all[pl.ds(at + 20, Z, stride=ROWS), :] = zeros
     for row in (19, 20):
         m_all[pl.ds(row, Z, stride=ROWS), :] = zeros
@@ -269,8 +284,10 @@
     for i in range(2):
         left_out[i * ROWS + OWN : (i + 1) * ROWS, :] = left[i]
         right_out[i * ROWS + OWN : (i + 1) * ROWS, :] = right[i]
-    sums_out[0:OWN, :] = left_in[ROWS : ROWS + OWN, :]
-    sums_out[OWN:ROWS, :] = left[1]
+    place = lanes(8) & 15
+    packed = left[1]
+    packed = jnp.where(place < 12, roll(left_in[ROWS : ROWS + 8, :], -2), packed)
+    sums_out[...] = jnp.where(place > 13, roll(left_in[ROWS + 8 : ROWS + OWN, :], 2), packed)
 
 
 def background_kernel(m_all, d_all, mtable, table, local_in, background, local):
@@ -367,7 +384,10 @@
 
         sums = lane_factor(1) * got_left[1] + lane_factor(devices - 1) * got_right[1]
         for i, other in enumerate(rest):
-            sums = sums + lane_factor(2 + i) * other[...]
+            packed = other[...]
+            sums = sums + lane_factor(2 + i) * jnp.concatenate(
+                [roll(packed, 2), roll(packed, -2), packed], 0
+            )
         strip_smooth = jnp.zeros((ROWS, 128), jnp.float32)
         designs, slopes = [], []
         cells = c_all[...]
@@ -408,79 +428,99 @@
         zero = jnp.zeros((ROWS, 128), jnp.float32)
         last, first = lane == 127, lane == 0
 
-        def e_at(channel, z):
+        def at(ref, channel, z):
             p = channel * Z + z
-            return e_all[p * ROWS : (p + 1) * ROWS, :]
-
-        def h_at(channel, z):
+            return ref[p * ROWS : (p + 1) * ROWS, :]
+
+        def put(ref, channel, z, value):
             p = channel * Z + z
-            return h_all[p * ROWS : (p + 1) * ROWS, :]
-
-        def s_at(ref, channel):
+            ref[p * ROWS : p * ROWS + value.shape[0], :] = value
+
+        def strip_at(ref, channel):
             return ref[channel * ROWS : (channel + 1) * ROWS, :]
 
-        def step(t, carry):
-            sx, sy, sz = s_at(se, 0), s_at(se, 1), s_at(se, 2)
+        def step(t, starts=False, ends=False):
+            ex, ey, ez = (strip_at(se, c) for c in range(3))
+            e_mixed = jnp.where(place == 12, ez, roll(ex, 1))
+            up_x = jnp.where(lane < 112, roll(ex, -16), 0.0)
+            up_y = jnp.where(lane < 112, roll(ey, -16), 0.0)
+            strips = []
+            for channel, curl in enumerate(
+                (
+                    (roll(ez, -1) - ez) - (up_y - ey),
+                    (up_x - ex) - (roll_rows(ez, -1) - ez),
+                    (roll_rows(ey, -1) - ey) - (roll(ex, -1) - ex),
+                )
+            ):
+                old = strip_at(sh, channel)
+                value = old - courant * curl
+                strips.append(value)
+                if not ends:
+                    sh[channel * ROWS : (channel + 1) * ROWS, :] = value
+            hx, hy, hz = strips
+            h_mixed = jnp.where(place == 3, hz, roll(hx, -1))
+            if not ends:
+                down_x = jnp.where(lane >= 16, roll(hx, 16), 0.0)
+                down_y = jnp.where(lane >= 16, roll(hy, 16), 0.0)
+                for channel, curl in enumerate(
+                    (
+                        (hz - roll(hz, 1)) - (hy - down_y),
+                        (hx - down_x) - (hz - roll_rows(hz, 1)),
+                        (hy - roll_rows(hy, 1)) - (hx - roll(hx, 1)),
+                    )
+                ):
+                    se[channel * ROWS : (channel + 1) * ROWS, :] = (
+                        strip_at(se, channel) + strip_at(si, channel) * curl
+                    )
+
+            rows = OWN if ends else ROWS
+            ex, ey = at(e_all, 0, 0), at(e_all, 1, 0)
+            hx_down = hy_down = zero
             for z in range(Z):
-                ex, ey, ez = e_at(0, z), e_at(1, z), e_at(2, z)
-                ex_up = e_at(0, z + 1) if z + 1 < Z else zero
-                ey_up = e_at(1, z + 1) if z + 1 < Z else zero
-                to = 115 - 16 * z
-                dy_ez = jnp.where(last, roll(sz, to), roll(ez, -1)) - ez
-                dy_ex = jnp.where(last, roll(sx, to), roll(ex, -1)) - ex
+                ez = at(e_all, 2, z)
+                ex_up = at(e_all, 0, z + 1) if z + 1 < Z else zero
+                ey_up = at(e_all, 1, z + 1) if z + 1 < Z else zero
+                beyond = roll(e_mixed, 115 - 16 * z)
+                dy_ez = jnp.where(last, beyond, roll(ez, -1)) - ez
+                dy_ex = roll(jnp.where(first, beyond, ex), -1) - ex
                 dx_ez = roll_rows(ez, -1) - ez
                 dx_ey = roll_rows(ey, -1) - ey
+                fields = []
                 for channel, curl in enumerate(
                     (dy_ez - (ey_up - ey), (ex_up - ex) - dx_ez, dx_ey - dy_ex)
                 ):
-                    p = channel * Z + z
-                    h_all[p * ROWS : (p + 1) * ROWS, :] = h_at(channel, z) - courant * curl
-            up_x = jnp.where(lane < 112, roll(sx, -16), 0.0)
-            up_y = jnp.where(lane < 112, roll(sy, -16), 0.0)
-            for channel, curl in enumerate(
-                (
-                    (roll(sz, -1) - sz) - (up_y - sy),
-                    (up_x - sx) - (roll_rows(sz, -1) - sz),
-                    (roll_rows(sy, -1) - sy) - (roll(sx, -1) - sx),
-                )
-            ):
-                sh[channel * ROWS : (channel + 1) * ROWS, :] = s_at(sh, channel) - courant * curl
-            sx, sy, sz = s_at(sh, 0), s_at(sh, 1), s_at(sh, 2)
-            for z in range(Z):
-                hx, hy, hz = h_at(0, z), h_at(1, z), h_at(2, z)
-                hx_down = h_at(0, z - 1) if z > 0 else zero
-                hy_down = h_at(1, z - 1) if z > 0 else zero
-                to = -(16 * z + 3)
-                dy_hz = hz - jnp.where(first, roll(sz, to), roll(hz, 1))
-                dy_hx = hx - jnp.where(first, roll(sx, to), roll(hx, 1))
+                    old = at(h_all, channel, z)
+                    value = old - courant * curl
+                    put(h_all, channel, z, value)
+                    fields.append(value)
+                hx, hy, hz = fields
+                beyond = roll(h_mixed, -(16 * z + 3))
+                dy_hz = hz - jnp.where(first, beyond, roll(hz, 1))
+                dy_hx = hx - roll(jnp.where(last, beyond, hx), 1)
                 dx_hz = hz - roll_rows(hz, 1)
                 dx_hy = hy - roll_rows(hy, 1)
                 total = jnp.zeros((OWN, 128), jnp.float32)
-                for channel, curl in enumerate(
-                    (dy_hz - (hy - hy_down), (hx - hx_down) - dx_hz, dx_hy - dy_hx)
+                for channel, (old, curl) in enumerate(
+                    (
+                        (ex, dy_hz - (hy - hy_down)),
+                        (ey, (hx - hx_down) - dx_hz),
+                        (ez, dx_hy - dy_hx),
+                    )
                 ):
-                    p = channel * Z + z
-                    value = e_at(channel, z) + inverse[p * ROWS : (p + 1) * ROWS, :] * curl
-                    e_all[p * ROWS : (p + 1) * ROWS, :] = value
-                    stored = forward[t, p].astype(jnp.float32)
+                    value = old[:rows] + at(inverse, channel, z)[:rows] * curl[:rows]
+                    put(e_all, channel, z, value)
+                    stored = forward[t, channel * Z + z].astype(jnp.float32)
                     total = total + contrast[channel] * (value[:OWN] * stored)
                 l = z // 2
                 gained[l * OWN : (l + 1) * OWN, :] = gained[l * OWN : (l + 1) * OWN, :] + total
-            down_x = jnp.where(lane >= 16, roll(sx, 16), 0.0)
-            down_y = jnp.where(lane >= 16, roll(sy, 16), 0.0)
-            for channel, curl in enumerate(
-                (
-                    (sz - roll(sz, 1)) - (sy - down_y),
-                    (sx - down_x) - (sz - roll_rows(sz, 1)),
-                    (sy - roll_rows(sy, 1)) - (sx - roll(sx, 1)),
-                )
-            ):
-                se[channel * ROWS : (channel + 1) * ROWS, :] = (
-                    s_at(se, channel) + s_at(si, channel) * curl
-                )
+                ex, ey = ex_up, ey_up
+                hx_down, hy_down = hx, hy
+
+        def middle(t, carry):
+            step(t)
             return carry
 
-        lax.fori_loop(0, STEPS, step, 0)
+        lax.fori_loop(0, STEPS, middle, 0)
         for p in range(3 * Z):
             e_final[p * OWN : (p + 1) * OWN, :] = e_all[p * ROWS : p * ROWS + OWN, :]
             h_final[p * OWN : (p + 1) * OWN, :] = h_all[p * ROWS : p * ROWS + OWN, :]
@@ -498,13 +538,14 @@
     reach = 4.0 * CY
     constants = filter_constants(count, reach)
 
-    to_prev, to_next, e_all, h_all, d_all, m_own, c_all, table, mtable, contrasts = call(
+    to_prev, to_next, e_own, h_own, d_own, m_own, c_own, table, mtable, contrasts = call(
         pack_kernel,
-        [vmem(3 * SLOT, 128), vmem(3 * SLOT + 24, 128),
-         vmem(PLANES * ROWS, 128), vmem(PLANES * ROWS, 128), vmem(DZ * ROWS, 128),
-         vmem(Z * OWN, 128, dtype=jnp.int32), vmem(ROWS, 128), vmem(*constants.shape),
+        [vmem(EXTRA, 128), vmem(EXTRA + 24, 128),
+         vmem(PLANES * OWN, 128), vmem(PLANES * OWN, 128), vmem(DZ * OWN, 128),
+         vmem(Z * OWN, 128, dtype=jnp.int32), vmem(OWN, 128), vmem(*constants.shape),
          vmem(3, MATS), vmem(1, 3)],
-        [electric.reshape(PLANES, OWN, 128), magnetic.reshape(PLANES, OWN, 128), density,
+        [electric.reshape(PLANES * OWN, 128), magnetic.reshape(PLANES * OWN, 128),
+         density.reshape(DZ * OWN, 128),
          material.reshape(Z * OWN, 128), tile_mask, constants, material_table,
          contrast.reshape(1, 3)],
         scratch=[vmem(*tile_mask.shape, dtype=jnp.int32), pltpu.SemaphoreType.DMA((8,))],
@@ -512,17 +553,18 @@
     )
     from_prev = sent(to_next, "gx", 1)
     from_next = sent(to_prev, "gx", -1)
-    pairs, left, right, m_all, local = call(
+    e_all, h_all, d_all, c_all, pairs, left, right, m_all, local = call(
         own_kernel,
-        [vmem(4 * ROWS, 128), vmem(2 * ROWS, 128), vmem(2 * ROWS, 128), vmem(Z * ROWS, 128),
+        [vmem(PLANES * ROWS, 128), vmem(PLANES * ROWS, 128), vmem(DZ * ROWS, 128),
+         vmem(ROWS, 128), vmem(4 * ROWS, 128), vmem(2 * ROWS, 128), vmem(2 * ROWS, 128), vmem(Z * ROWS, 128),
          vmem(DZ * ROWS, 256)],
-        [e_all, h_all, d_all, m_own, c_all, table],
+        [e_own, h_own, d_own, m_own, c_own, table],
     )
     e_all, h_all, d_all, c_all, m_all, pairs, left, right, sums = call(
         halo_kernel,
         [vmem(PLANES * ROWS, 128), vmem(PLANES * ROWS, 128), vmem(DZ * ROWS, 128),
          vmem(ROWS, 128), vmem(Z * ROWS, 128), vmem(4 * ROWS, 128),
-         vmem(2 * ROWS, 128), vmem(2 * ROWS, 128), vmem(ROWS, 128)],
+         vmem(2 * ROWS, 128), vmem(2 * ROWS, 128), vmem(8, 128)],
         [from_next, from_prev, e_all, h_all, d_all, c_all, m_all, pairs, left, right, table],
         aliases={2: 0, 3: 1, 4: 2, 5: 3, 6: 4, 7: 5, 8: 6, 9: 7},
     )

time: 19.8 us -> 19.2 us (0.970)
  Pallas kernels: 5.69 us -> 4.95 us
    pallas_call x5, Pallas kernels: 5.69 us -> 4.95 us  [call(): pl.pallas_call(kernel, out_shape=outs, in_specs=in_specs, out_specs=[VM]...]
  transfers between devices with their start and end apart: 5 -> 5, of which waited for: 2 -> 2; matrix products, arithmetic and copies ran while one was open for 0% -> 0% of each run, Pallas kernels for 5% -> 3%
where the time goes in v3:
time: 19.2 us; the launch traced here: 19 us
  starting transfers between devices  8.17 us (43%)
  waiting for transfers between devices  5.24 us (27%)
  Pallas kernels  4.95 us (26%)
  between operations  0.67 us (3%)
    ppermute x5, starting transfers between devices, sent(): return lax.ppermute(x, axis, [(i, (i + by) % size) for i in range(size)])  8.17 us
    ppermute x5, waiting for transfers between devices, sent(): return lax.ppermute(x, axis, [(i, (i + by) % size) for i in range(size)])  5.24 us
    pallas_call x5, Pallas kernels, call(): pl.pallas_call(kernel, out_shape=outs, in_specs=in_specs, out_specs=[VM]...  4.95 us
  transfers between devices with their start and end apart: 5, of which 2 were waited for; matrix products, arithmetic and copies ran while one was open for 0% of the time, Pallas kernels for 3%

profile of v3, /device:TPU:0, one launch (start us, length us, event | category | flops | bytes accessed | tf_op | source)
XLA Modules:
  0.0 19.0 jit_solution(8917903639685151236)
XLA Ops:
  0.6 1.3 %shard_map.112 = (f32[184,128]{1,0:T(8,128)S(1)}, f32[208,128]{1,0:T(8,128)S(1)}, f32[384,128]{1,0:T(8,128)S(1)}, f32[384,128]{1,0:T(8,128)S(1)}, f32[64,128]{1,...) custom-call(f32[384,128]{1,0:T(8,128)} %bitcast.10, ...), custom_call_target="tpu_custom_call" | custom-call | tf_op jit(solution)/shard_map/pallas_call | solution.py:42
  1.9 3.0 %collective-permute-start.1 = (f32[208,128]{1,0:T(8,128)S(1)}, f32[208,128]{1,0:T(8,128)S(1)}, u32[]{:S(2)}, u32[]{:S(2)}) collective-permute-start(f32[208,128]{1,0:T(8,128)S(1)} %get-tuple-element.37), channel_id=1, source_target_pairs={{0,4},{4,8},{8,12},{12,16},{16,20},{20,24},{24,28},{28,0},{1,5},{5... | collective-permute-start | bytes 319496 | tf_op jit(solution)/shard_map/ppermute | solution.py:67
  4.9 3.1 %collective-permute-start = (f32[184,128]{1,0:T(8,128)S(1)}, f32[184,128]{1,0:T(8,128)S(1)}, u32[]{:S(2)}, u32[]{:S(2)}) collective-permute-start(f32[184,128]{1,0:T(8,128)S(1)} %get-tuple-element.36), channel_id=1, source_target_pairs={{0,28},{4,0},{8,4},{12,8},{16,12},{20,16},{24,20},{28,24},{1,29},{... | collective-permute-start | bytes 282632 | tf_op jit(solution)/shard_map/ppermute | solution.py:67
  8.0 0.4 %shard_map.113 = (f32[576,128]{1,0:T(8,128)S(1)}, f32[576,128]{1,0:T(8,128)S(1)}, f32[96,128]{1,0:T(8,128)S(1)}, f32[24,128]{1,0:T(8,128)S(1)}, f32[96,128]{1,0:...) custom-call(f32[384,128]{1,0:T(8,128)S(1)} %get-tuple-element.38.e_o, ...), custom_call_target="tpu_custom_call" | custom-call | tf_op jit(solution)/shard_map/pallas_call | solution.py:42
  8.5 3.3 %collective-permute-done.from_next = f32[184,128]{1,0:T(8,128)S(1)} collective-permute-done((f32[184,128]{1,0:T(8,128)S(1)}, f32[184,128]{1,0:T(8,128)S(1)}, u32[]{:S(2)}, u32[]{:S(2)}) %collective-permute-start) | collective-permute-done | bytes 94240 | tf_op jit(solution)/shard_map/ppermute | solution.py:67
  11.8 0.0 collective-permute-done.1.from_prev
  11.8 0.4 %shard_map.114 = (f32[576,128]{1,0:T(8,128)S(1)}, f32[576,128]{1,0:T(8,128)S(1)}, f32[96,128]{1,0:T(8,128)S(1)}, f32[24,128]{1,0:T(8,128)S(1)}, f32[192,128]{1,0...) custom-call(f32[184,128]{1,0:T(8,128)S(1)} %collective-permute-done., ...), custom_call_target="tpu_custom_call", output_to_operand_aliasing={{0}: (2, {}), {1}: (3, {}), {2}: (4, {}), {3}: (5, {}), {4}... | custom-call | tf_op jit(solution)/shard_map/pallas_call | solution.py:42
  12.2 0.0 copy-start
  12.2 0.1 collective-permute-start.2
  12.3 0.5 %collective-permute-start.3 = (f32[48,128]{1,0:T(8,128)S(1)}, f32[48,128]{1,0:T(8,128)S(1)}, u32[]{:S(2)}, u32[]{:S(2)}) collective-permute-start(f32[48,128]{1,0:T(8,128)S(1)} %get-tuple-element.53), channel_id=1, source_target_pairs={{0,1},{1,2},{2,3},{3,0},{4,5},{5,6},{6,7},{7,4},{8,9},{9,10},{10,1... | collective-permute-start | bytes 73736 | tf_op jit(solution)/shard_map/ppermute | solution.py:67
  12.8 1.5 %collective-permute-start.4 = (f32[8,128]{1,0:T(8,128)S(1)}, f32[8,128]{1,0:T(8,128)S(1)}, u32[]{:S(2)}, u32[]{:S(2)}) collective-permute-start(f32[8,128]{1,0:T(8,128)S(1)} %get-tuple-element.54), channel_id=1, source_target_pairs={{0,2},{1,3},{2,0},{3,1},{4,6},{5,7},{6,4},{7,5},{8,10},{9,11},{10,... | collective-permute-start | bytes 12296 | tf_op jit(solution)/shard_map/ppermute | solution.py:67
  14.3 0.2 %shard_map.115 = (f32[576,128]{1,0:T(8,128)S(1)}, f32[96,256]{1,0:T(8,128)S(1)}) custom-call(f32[192,128]{1,0:T(8,128)S(1)} %get-tuple-element.59.m_all, f32[96,128]{1,0:T(8,128)S(1)} %get-tuple-element.57.d_all.refs_5_, f32[3,4]{1,0:T(4,128)S(1)} %get-tuple-element.60.mtable.refs_11_, ...), custom_call_target="tpu_custom_call", output_to_operand_aliasing={{1}: (4, {})} | custom-call | tf_op jit(solution)/shard_map/pallas_call | solution.py:42
  14.5 1.9 %collective-permute-done.4.refs_2_ = f32[8,128]{1,0:T(8,128)S(1)} collective-permute-done((f32[8,128]{1,0:T(8,128)S(1)}, f32[8,128]{1,0:T(8,128)S(1)}, u32[]{:S(2)}, u32[]{:S(2)}) %collective-permute-start.4) | collective-permute-done | bytes 4128 | tf_op jit(solution)/shard_map/ppermute | solution.py:67
  16.4 0.0 collective-permute-done.2.refs_0_
  16.4 0.0 collective-permute-done.3.refs_1_
  16.4 0.0 copy-done
  16.4 2.6 %shard_map.116 = (f32[384,128]{1,0:T(8,128)}, f32[384,128]{1,0:T(8,128)}, f32[64,128]{1,0:T(8,128)}, f32[576,128]{1,0:T(8,128)S(1)}, f32[576,128]{1,0:T(8,128)S(1)}) custom-call(f32[48,128]{1,0:T(8,128)S(1)} %collective-permute-done.2.refs_0_, f32[48,128]{1,0:T(8,128)S(1)} %collective-permute-done.3.refs_1_, ...), custom_call_target="tpu_custom_call", output_to_operand_aliasing={{3}: (3, {}), {4}: (4, {})} | custom-call | tf_op jit(solution)/shard_map/pallas_call | solution.py:42
Async XLA Ops:
  1.9 9.9 %collective-permute-start.1 = (f32[208,128]{1,0:T(8,128)S(1)}, f32[208,128]{1,0:T(8,128)S(1)}, u32[]{:S(2)}, u32[]{:S(2)}) collective-permute-start(f32[208,128]{1,0:T(8,128)S(1)} %get-tuple-element.37), channel_id=1, source_target_pairs={{0,4},{4,8},{8,12},{12,16},{16,20},{20,24},{24,28},{28,0},{1,5},{5... | collective-permute-start | bytes 319496 | tf_op jit(solution)/shard_map/ppermute | solution.py:67
  4.9 6.9 %collective-permute-start = (f32[184,128]{1,0:T(8,128)S(1)}, f32[184,128]{1,0:T(8,128)S(1)}, u32[]{:S(2)}, u32[]{:S(2)}) collective-permute-start(f32[184,128]{1,0:T(8,128)S(1)} %get-tuple-element.36), channel_id=1, source_target_pairs={{0,28},{4,0},{8,4},{12,8},{16,12},{20,16},{24,20},{28,24},{1,29},{... | collective-permute-start | bytes 282632 | tf_op jit(solution)/shard_map/ppermute | solution.py:67
  12.2 4.2 %copy-start = (bf16[4,3,8,16,128]{4,3,2,1,0:T(8,128)(2,1)S(1)}, bf16[4,3,8,16,128]{4,3,2,1,0:T(8,128)(2,1)}, u32[]{:S(2)}) copy-start(bf16[4,3,8,16,128]{4,3,2,1,0:T(8,128)(2,1)} %param.16) | copy-start | bytes 1179652
  12.2 4.2 %collective-permute-start.2 = (f32[48,128]{1,0:T(8,128)S(1)}, f32[48,128]{1,0:T(8,128)S(1)}, u32[]{:S(2)}, u32[]{:S(2)}) collective-permute-start(f32[48,128]{1,0:T(8,128)S(1)} %get-tuple-element.52), channel_id=1, source_target_pairs={{0,3},{1,0},{2,1},{3,2},{4,7},{5,4},{6,5},{7,6},{8,11},{9,8},{10,9... | collective-permute-start | bytes 73736 | tf_op jit(solution)/shard_map/ppermute | solution.py:67
  12.3 4.1 %collective-permute-start.3 = (f32[48,128]{1,0:T(8,128)S(1)}, f32[48,128]{1,0:T(8,128)S(1)}, u32[]{:S(2)}, u32[]{:S(2)}) collective-permute-start(f32[48,128]{1,0:T(8,128)S(1)} %get-tuple-element.53), channel_id=1, source_target_pairs={{0,1},{1,2},{2,3},{3,0},{4,5},{5,6},{6,7},{7,4},{8,9},{9,10},{10,1... | collective-permute-start | bytes 73736 | tf_op jit(solution)/shard_map/ppermute | solution.py:67
  12.8 3.6 %collective-permute-start.4 = (f32[8,128]{1,0:T(8,128)S(1)}, f32[8,128]{1,0:T(8,128)S(1)}, u32[]{:S(2)}, u32[]{:S(2)}) collective-permute-start(f32[8,128]{1,0:T(8,128)S(1)} %get-tuple-element.54), channel_id=1, source_target_pairs={{0,2},{1,3},{2,0},{3,1},{4,6},{5,7},{6,4},{7,5},{8,10},{9,11},{10,... | collective-permute-start | bytes 12296 | tf_op jit(solution)/shard_map/ppermute | solution.py:67

commit v4 on v3

--- a/solution.py
+++ b/solution.py
@@ -35,15 +35,17 @@
     return pltpu.VMEM(shape, dtype)
 
 
-def call(kernel, outs, ins, aliases=None, scratch=(), in_specs=None):
-    space = pltpu.VMEM if in_specs is None else pltpu.HBM
+def call(kernel, outs, ins, aliases=None, scratch=(), in_specs=None, out_specs=None):
     in_specs = in_specs or [VM] * len(ins)
-    ins = [pltpu.with_memory_space_constraint(x, space) for x in ins]
+    ins = [
+        pltpu.with_memory_space_constraint(x, pltpu.VMEM if spec is VM else pltpu.HBM)
+        for x, spec in zip(ins, in_specs)
+    ]
     return pl.pallas_call(
         kernel,
         out_shape=outs,
         in_specs=in_specs,
-        out_specs=[VM] * len(outs),
+        out_specs=out_specs or [VM] * len(outs),
         scratch_shapes=list(scratch),
         input_output_aliases=aliases or {},
         compiler_params=pltpu.CompilerParams(vmem_limit_bytes=32 * 1024 * 1024),
@@ -131,21 +133,19 @@
 
 
 def pack_kernel(
-    electric, magnetic, density, material, mask, table_in, mtable_in, contrast_in,
-    to_prev, to_next, e_own, h_own, d_own, m_own, c_all, table, mtable, contrast,
+    electric, magnetic, density, material, mask,
+    to_prev, to_next, e_own, h_own, d_own, m_own, c_all,
     mask_v, sems,
 ):
     copies = []
     moved = [
         (mask, mask_v), (electric, e_own), (magnetic, h_own), (density, d_own), (material, m_own),
     ]
-    needed = len(moved)
-    moved += [(table_in, table), (mtable_in, mtable), (contrast_in, contrast)]
     for i, (source, target) in enumerate(moved):
         copy = pltpu.make_async_copy(source, target, sems.at[i])
         copy.start()
         copies.append(copy)
-    for copy in copies[:needed]:
+    for copy in copies:
         copy.wait()
 
     cells = cell_rows(mask_v[...])
@@ -185,14 +185,21 @@
     to_next[EXTRA : EXTRA + 8, :] = e(0, OWN - 4)
     to_next[EXTRA + 8 : EXTRA + 16, :] = part_y
     to_next[EXTRA + 16 : EXTRA + 24, :] = part_z
-    for copy in copies[needed:]:
-        copy.wait()
 
 
 def own_kernel(
-    e_own, h_own, d_own, m_own, c_own, table,
-    e_all, h_all, d_all, c_all, pairs_out, left_out, right_out, m_all, local,
+    table_in, mtable_in, contrast_in, e_own, h_own, d_own, m_own, c_own,
+    table, mtable, contrast, e_all, h_all, d_all, c_all, pairs_out, left_out, right_out,
+    m_all, local, sems,
 ):
+    copies = [
+        pltpu.make_async_copy(source, target, sems.at[i])
+        for i, (source, target) in enumerate(
+            ((table_in, table), (mtable_in, mtable), (contrast_in, contrast))
+        )
+    ]
+    for copy in copies:
+        copy.start()
     c_all[0:OWN, :] = c_own[...]
     groups = []
     for source, target in ((e_own, e_all), (h_own, h_all)):
@@ -214,8 +221,10 @@
     for l in range(DZ):
         layers.append(d_own[l * OWN : (l + 1) * OWN, :])
         d_all[l * ROWS : l * ROWS + OWN, :] = layers[l]
+    column = lanes(1).astype(jnp.float32) * (1.0 / (4.0 * CY))
+    rising, falling = jnp.exp(column), jnp.exp(-column)
     groups.append(
-        density_planes(layers, c_own[...], table[130:131, 0:128], table[131:132, 0:128])
+        density_planes(layers, c_own[...], rising, falling)
     )
     pairs = edge_pairs(groups)
     left, right = edge_messages(pairs)
@@ -224,6 +233,8 @@
     for i in range(2):
         left_out[i * ROWS : i * ROWS + OWN, :] = left[i]
         right_out[i * ROWS : i * ROWS + OWN, :] = right[i]
+    for copy in copies:
+        copy.wait()
     smooth = jnp.dot(
         jnp.concatenate(layers, 0), table[0:128, :], precision=lax.Precision.HIGHEST,
         preferred_element_type=jnp.float32,
@@ -328,12 +339,148 @@
     return (base + level) * (1.0 / bottom), (sharpness / bottom) * (1.0 - level * level)
 
 
+def plane_of(ref, channel, z, rows=ROWS):
+    p = channel * Z + z
+    return ref[p * ROWS : p * ROWS + rows, :]
+
+
+def strip_of(ref, channel):
+    return ref[channel * ROWS : (channel + 1) * ROWS, :]
+
+
+def keep(ref, fields):
+    for c, field in enumerate(fields):
+        ref[c * ROWS : (c + 1) * ROWS, :] = field
+
+
+def strip_magnetic(old, electric):
+    lane = lanes(ROWS)
+    ex, ey, ez = electric
+    up_x = jnp.where(lane < 112, roll(ex, -16), 0.0)
+    up_y = jnp.where(lane < 112, roll(ey, -16), 0.0)
+    curls = (
+        (roll(ez, -1) - ez) - (up_y - ey),
+        (up_x - ex) - (roll_rows(ez, -1) - ez),
+        (roll_rows(ey, -1) - ey) - (roll(ex, -1) - ex),
+    )
+    return [field - courant * curl for field, curl in zip(old, curls)]
+
+
+def strip_electric(old, magnetic, inverse):
+    lane = lanes(ROWS)
+    hx, hy, hz = magnetic
+    down_x = jnp.where(lane >= 16, roll(hx, 16), 0.0)
+    down_y = jnp.where(lane >= 16, roll(hy, 16), 0.0)
+    curls = (
+        (hz - roll(hz, 1)) - (hy - down_y),
+        (hx - down_x) - (hz - roll_rows(hz, 1)),
+        (hy - roll_rows(hy, 1)) - (hx - roll(hx, 1)),
+    )
+    return [old[c] + inverse[c] * curl for c, curl in enumerate(curls)]
+
+
+def planes_magnetic(e_all, h_in, h_out, strip_e):
+    lane = lanes(ROWS)
+    last, first = lane == 127, lane == 0
+    zero = jnp.zeros((ROWS, 128), jnp.float32)
+    mixed = jnp.where((lane & 15) == 12, strip_e[2], roll(strip_e[0], 1))
+    ex_up, ey_up = plane_of(e_all, 0, 0), plane_of(e_all, 1, 0)
+    for z in range(Z):
+        ex, ey, ez = ex_up, ey_up, plane_of(e_all, 2, z)
+        ex_up = plane_of(e_all, 0, z + 1) if z + 1 < Z else zero
+        ey_up = plane_of(e_all, 1, z + 1) if z + 1 < Z else zero
+        beyond = roll(mixed, 115 - 16 * z)
+        dy_ez = jnp.where(last, beyond, roll(ez, -1)) - ez
+        dy_ex = roll(jnp.where(first, beyond, ex), -1) - ex
+        dx_ez = roll_rows(ez, -1) - ez
+        dx_ey = roll_rows(ey, -1) - ey
+        for channel, curl in enumerate(
+            (dy_ez - (ey_up - ey), (ex_up - ex) - dx_ez, dx_ey - dy_ex)
+        ):
+            p = channel * Z + z
+            h_out[p * ROWS : (p + 1) * ROWS, :] = plane_of(h_in, channel, z) - courant * curl
+
+
+def planes_electric(e_all, h_all, inverse, strip_h, stored_at, contrast, gained, e_out, stride):
+    lane = lanes(ROWS)
+    last, first = lane == 127, lane == 0
+    mixed = jnp.where((lane & 15) == 3, strip_h[2], roll(strip_h[0], -1))
+    hx = hy = jnp.zeros((ROWS, 128), jnp.float32)
+    for z in range(Z):
+        hx_down, hy_down = hx, hy
+        hx, hy, hz = (plane_of(h_all, c, z) for c in range(3))
+        beyond = roll(mixed, -(16 * z + 3))
+        dy_hz = hz - jnp.where(first, beyond, roll(hz, 1))
+        dy_hx = hx - roll(jnp.where(last, beyond, hx), 1)
+        dx_hz = hz - roll_rows(hz, 1)
+        dx_hy = hy - roll_rows(hy, 1)
+        total = jnp.zeros((OWN, 128), jnp.float32)
+        for channel, curl in enumerate(
+            (dy_hz - (hy - hy_down), (hx - hx_down) - dx_hz, dx_hy - dy_hx)
+        ):
+            p = channel * Z + z
+            value = (
+                plane_of(e_all, channel, z, stride)
+                + plane_of(inverse, channel, z, stride) * curl[:stride]
+            )
+            e_out[p * stride : (p + 1) * stride, :] = value
+            total = total + contrast[channel] * (value[:OWN] * stored_at(p).astype(jnp.float32))
+        l = z // 2
+        gained[l * OWN : (l + 1) * OWN, :] = gained[l * OWN : (l + 1) * OWN, :] + total
+
+
+def lane_factor(m, count, reach):
+    up, down = math.exp(-CY * m / reach), math.exp(-(count - CY * m) / reach)
+    return jnp.where((lanes(ROWS) & 15) == 12, up, down)
+
+
+def first_kernel(count, reach):
+    devices = count // CY
+
+    def kernel(from_right, from_left, pairs, e_all, h_in, h_all, se, sh, traits, sums):
+        lane = lanes(ROWS)
+        place = lane & 15
+        odd = ((lane >> 4) & 1) == 1
+        part = place >> 2
+        got_left = [from_left[i * ROWS : (i + 1) * ROWS, :] for i in range(2)]
+        got_right = [from_right[i * ROWS : (i + 1) * ROWS, :] for i in range(2)]
+
+        def strip(index):
+            tile, q = index // 4, index % 4
+            pair = pairs[(index // 2) * ROWS : (index // 2 + 1) * ROWS, :]
+            if index % 2 == 0:
+                own_l, own_r = pair, roll(pair, 8)
+            else:
+                own_l, own_r = roll(pair, -8), pair
+            outer = jnp.where(
+                part == 0, roll(got_left[tile], -4 * q), roll(got_right[tile], 12 - 4 * q)
+            )
+            return jnp.where(part == 1, own_l, jnp.where(part == 2, own_r, outer))
+
+        electric = [strip(c) for c in range(3)]
+        keep(se, electric)
+        keep(sh, strip_magnetic([strip(3 + c) for c in range(3)], electric))
+        raw = strip(7)
+        marks = jnp.where(odd, raw, roll(raw, -16))
+        keep(
+            traits,
+            [
+                strip(6),
+                jnp.where(odd, roll(raw, 16), raw),
+                jnp.where((place & 2) == 2, marks, roll(marks, -2)),
+            ],
+        )
+        sums[...] = (
+            lane_factor(1, count, reach) * got_left[1]
+            + lane_factor(devices - 1, count, reach) * got_right[1]
+        )
+        planes_magnetic(e_all, h_in, h_all, electric)
+
+    return kernel
+
+
 def step_kernel(count, reach, others):
-    devices = count // CY
     norm_total = 2.0 * float(np.sum(np.exp(-np.arange(count) / reach)))
-
-    def factor(m):
-        return math.exp(-CY * m / reach), math.exp(-(count - CY * m) / reach)
 
     def fix(delta):
         if delta == 0:
@@ -344,52 +491,26 @@
         )
 
     def kernel(*refs):
-        from_right, from_left = refs[:2]
-        rest = refs[2 : 2 + others]
-        (e_in, h_in, d_all, c_all, background, pairs, local, table, mtable, contrast_in, forward,
-         e_final, h_final, gradient, e_all, h_all, inverse, se, sh, si, gained) = refs[2 + others :]
+        rest = refs[:others]
+        (e_in, h_in, se_in, sh_in, traits, sums_in, d_all, c_all, background, local, table, mtable,
+         contrast_in, forward,
+         e_final, h_final, gradient, e_all, h_all, se, sh,
+         inverse, si, gained) = refs[others:]
         entries = mtable[...]
         contrast = [contrast_in[0:1, c : c + 1] for c in range(3)]
         lane = lanes(ROWS)
         place = lane & 15
-        odd = ((lane >> 4) & 1) == 1
         layer_of = lane >> 5
-        part = place >> 2
-
-        got_left = [from_left[i * ROWS : (i + 1) * ROWS, :] for i in range(2)]
-        got_right = [from_right[i * ROWS : (i + 1) * ROWS, :] for i in range(2)]
-
-        def strip(index):
-            tile, q = index // 4, index % 4
-            pair = pairs[(index // 2) * ROWS : (index // 2 + 1) * ROWS, :]
-            if index % 2 == 0:
-                own_l, own_r = pair, roll(pair, 8)
-            else:
-                own_l, own_r = roll(pair, -8), pair
-            outer = jnp.where(part == 0, roll(got_left[tile], -4 * q), roll(got_right[tile], 12 - 4 * q))
-            return jnp.where(part == 1, own_l, jnp.where(part == 2, own_r, outer))
-
-        for channel in range(3):
-            se[channel * ROWS : (channel + 1) * ROWS, :] = strip(channel)
-            sh[channel * ROWS : (channel + 1) * ROWS, :] = strip(3 + channel)
-        strip_material = strip(6)
-        raw = strip(7)
-        strip_density = jnp.where(odd, roll(raw, 16), raw)
-        marks = jnp.where(odd, raw, roll(raw, -16))
-        strip_cells = jnp.where((place & 2) == 2, marks, roll(marks, -2))
-
-        def lane_factor(m):
-            up, down = factor(m)
-            return jnp.where(place == 12, up, down)
-
-        sums = lane_factor(1) * got_left[1] + lane_factor(devices - 1) * got_right[1]
+
+        sums = sums_in[...]
         for i, other in enumerate(rest):
             packed = other[...]
-            sums = sums + lane_factor(2 + i) * jnp.concatenate(
+            sums = sums + lane_factor(2 + i, count, reach) * jnp.concatenate(
                 [roll(packed, 2), roll(packed, -2), packed], 0
             )
+        strip_density = strip_of(traits, 1)
         strip_smooth = jnp.zeros((ROWS, 128), jnp.float32)
-        designs, slopes = [], []
+        designs = []
         cells = c_all[...]
         for l in range(DZ):
             at = (2 * l + 1) * 16 + 12
@@ -402,7 +523,7 @@
             filtered = 0.5 * d_all[l * ROWS : (l + 1) * ROWS, :] + (0.5 / norm_total) * smooth
             projected, slope = project(filtered)
             designs.append(cells * projected)
-            slopes.append(slope[:OWN] * cells[:OWN])
+            gradient[l * OWN : (l + 1) * OWN, :] = slope[:OWN] * cells[:OWN]
         for delta in range(4):
             value = fix(delta) * strip_density
             ahead = value if delta == 0 else roll(value, delta)
@@ -410,13 +531,15 @@
             strip_smooth = strip_smooth + jnp.where(place >= 12 + delta, ahead, 0.0)
             strip_smooth = strip_smooth + jnp.where(place < 4 - delta, behind, 0.0)
         projected, _ = project(0.5 * strip_density + (0.5 / norm_total) * strip_smooth)
-        strip_design = strip_cells * projected
-
-        for channel in range(3):
-            own = looked_up(strip_material, entries, channel)
-            si[channel * ROWS : (channel + 1) * ROWS, :] = courant / (
-                own + strip_design * contrast[channel]
-            )
+        strip_design = strip_of(traits, 2) * projected
+        keep(
+            si,
+            [
+                courant
+                / (looked_up(strip_of(traits, 0), entries, c) + strip_design * contrast[c])
+                for c in range(3)
+            ],
+        )
         for z in range(Z):
             for channel in range(3):
                 p = channel * Z + z
@@ -425,107 +548,28 @@
                 )
         gained[...] = jnp.zeros_like(gained)
 
-        zero = jnp.zeros((ROWS, 128), jnp.float32)
-        last, first = lane == 127, lane == 0
-
-        def at(ref, channel, z):
-            p = channel * Z + z
-            return ref[p * ROWS : (p + 1) * ROWS, :]
-
-        def put(ref, channel, z, value):
-            p = channel * Z + z
-            ref[p * ROWS : p * ROWS + value.shape[0], :] = value
-
-        def strip_at(ref, channel):
-            return ref[channel * ROWS : (channel + 1) * ROWS, :]
-
-        def step(t, starts=False, ends=False):
-            ex, ey, ez = (strip_at(se, c) for c in range(3))
-            e_mixed = jnp.where(place == 12, ez, roll(ex, 1))
-            up_x = jnp.where(lane < 112, roll(ex, -16), 0.0)
-            up_y = jnp.where(lane < 112, roll(ey, -16), 0.0)
-            strips = []
-            for channel, curl in enumerate(
-                (
-                    (roll(ez, -1) - ez) - (up_y - ey),
-                    (up_x - ex) - (roll_rows(ez, -1) - ez),
-                    (roll_rows(ey, -1) - ey) - (roll(ex, -1) - ex),
-                )
-            ):
-                old = strip_at(sh, channel)
-                value = old - courant * curl
-                strips.append(value)
-                if not ends:
-                    sh[channel * ROWS : (channel + 1) * ROWS, :] = value
-            hx, hy, hz = strips
-            h_mixed = jnp.where(place == 3, hz, roll(hx, -1))
-            if not ends:
-                down_x = jnp.where(lane >= 16, roll(hx, 16), 0.0)
-                down_y = jnp.where(lane >= 16, roll(hy, 16), 0.0)
-                for channel, curl in enumerate(
-                    (
-                        (hz - roll(hz, 1)) - (hy - down_y),
-                        (hx - down_x) - (hz - roll_rows(hz, 1)),
-                        (hy - roll_rows(hy, 1)) - (hx - roll(hx, 1)),
-                    )
-                ):
-                    se[channel * ROWS : (channel + 1) * ROWS, :] = (
-                        strip_at(se, channel) + strip_at(si, channel) * curl
-                    )
-
-            rows = OWN if ends else ROWS
-            ex, ey = at(e_all, 0, 0), at(e_all, 1, 0)
-            hx_down = hy_down = zero
-            for z in range(Z):
-                ez = at(e_all, 2, z)
-                ex_up = at(e_all, 0, z + 1) if z + 1 < Z else zero
-                ey_up = at(e_all, 1, z + 1) if z + 1 < Z else zero
-                beyond = roll(e_mixed, 115 - 16 * z)
-                dy_ez = jnp.where(last, beyond, roll(ez, -1)) - ez
-                dy_ex = roll(jnp.where(first, beyond, ex), -1) - ex
-                dx_ez = roll_rows(ez, -1) - ez
-                dx_ey = roll_rows(ey, -1) - ey
-                fields = []
-                for channel, curl in enumerate(
-                    (dy_ez - (ey_up - ey), (ex_up - ex) - dx_ez, dx_ey - dy_ex)
-                ):
-                    old = at(h_all, channel, z)
-                    value = old - courant * curl
-                    put(h_all, channel, z, value)
-                    fields.append(value)
-                hx, hy, hz = fields
-                beyond = roll(h_mixed, -(16 * z + 3))
-                dy_hz = hz - jnp.where(first, beyond, roll(hz, 1))
-                dy_hx = hx - roll(jnp.where(last, beyond, hx), 1)
-                dx_hz = hz - roll_rows(hz, 1)
-                dx_hy = hy - roll_rows(hy, 1)
-                total = jnp.zeros((OWN, 128), jnp.float32)
-                for channel, (old, curl) in enumerate(
-                    (
-                        (ex, dy_hz - (hy - hy_down)),
-                        (ey, (hx - hx_down) - dx_hz),
-                        (ez, dx_hy - dy_hx),
-                    )
-                ):
-                    value = old[:rows] + at(inverse, channel, z)[:rows] * curl[:rows]
-                    put(e_all, channel, z, value)
-                    stored = forward[t, channel * Z + z].astype(jnp.float32)
-                    total = total + contrast[channel] * (value[:OWN] * stored)
-                l = z // 2
-                gained[l * OWN : (l + 1) * OWN, :] = gained[l * OWN : (l + 1) * OWN, :] + total
-                ex, ey = ex_up, ey_up
-                hx_down, hy_down = hx, hy
-
-        def middle(t, carry):
-            step(t)
+        def step(t, carry):
+            strip_h = [strip_of(sh, c) for c in range(3)]
+            strip_e = strip_electric(
+                [strip_of(se, c) for c in range(3)], strip_h, [strip_of(si, c) for c in range(3)]
+            )
+            keep(se, strip_e)
+            keep(sh, strip_magnetic(strip_h, strip_e))
+            planes_electric(
+                e_all, h_all, inverse, strip_h, lambda p: forward[t, p], contrast, gained,
+                e_all, ROWS,
+            )
+            planes_magnetic(e_all, h_all, h_all, strip_e)
             return carry
 
-        lax.fori_loop(0, STEPS, middle, 0)
-        for p in range(3 * Z):
-            e_final[p * OWN : (p + 1) * OWN, :] = e_all[p * ROWS : p * ROWS + OWN, :]
+        lax.fori_loop(0, STEPS - 1, step, 0)
+        for p in range(PLANES):
             h_final[p * OWN : (p + 1) * OWN, :] = h_all[p * ROWS : p * ROWS + OWN, :]
-        for l in range(DZ):
-            gradient[l * OWN : (l + 1) * OWN, :] = slopes[l] * gained[l * OWN : (l + 1) * OWN, :]
+        planes_electric(
+            e_all, h_all, inverse, [strip_of(sh, c) for c in range(3)],
+            lambda p: forward[STEPS - 1, p], contrast, gained, e_final, OWN,
+        )
+        gradient[...] = gradient[...] * gained[...]
 
     return kernel
 
@@ -538,27 +582,26 @@
     reach = 4.0 * CY
     constants = filter_constants(count, reach)
 
-    to_prev, to_next, e_own, h_own, d_own, m_own, c_own, table, mtable, contrasts = call(
+    to_prev, to_next, e_own, h_own, d_own, m_own, c_own = call(
         pack_kernel,
         [vmem(EXTRA, 128), vmem(EXTRA + 24, 128),
          vmem(PLANES * OWN, 128), vmem(PLANES * OWN, 128), vmem(DZ * OWN, 128),
-         vmem(Z * OWN, 128, dtype=jnp.int32), vmem(OWN, 128), vmem(*constants.shape),
-         vmem(3, MATS), vmem(1, 3)],
+         vmem(Z * OWN, 128, dtype=jnp.int32), vmem(OWN, 128)],
         [electric.reshape(PLANES * OWN, 128), magnetic.reshape(PLANES * OWN, 128),
          density.reshape(DZ * OWN, 128),
-         material.reshape(Z * OWN, 128), tile_mask, constants, material_table,
-         contrast.reshape(1, 3)],
-        scratch=[vmem(*tile_mask.shape, dtype=jnp.int32), pltpu.SemaphoreType.DMA((8,))],
-        in_specs=[ANY] * 8,
+         material.reshape(Z * OWN, 128), tile_mask],
+        scratch=[vmem(*tile_mask.shape, dtype=jnp.int32), pltpu.SemaphoreType.DMA((5,))],
+        in_specs=[ANY] * 5,
     )
     from_prev = sent(to_next, "gx", 1)
     from_next = sent(to_prev, "gx", -1)
-    e_all, h_all, d_all, c_all, pairs, left, right, m_all, local = call(
+    table, mtable, contrasts, e_all, h_all, d_all, c_all, pairs, left, right, m_all, local = call(
         own_kernel,
-        [vmem(PLANES * ROWS, 128), vmem(PLANES * ROWS, 128), vmem(DZ * ROWS, 128),
+        [vmem(*constants.shape), vmem(3, MATS), vmem(1, 3), vmem(PLANES * ROWS, 128), vmem(PLANES * ROWS, 128), vmem(DZ * ROWS, 128),
          vmem(ROWS, 128), vmem(4 * ROWS, 128), vmem(2 * ROWS, 128), vmem(2 * ROWS, 128), vmem(Z * ROWS, 128),
          vmem(DZ * ROWS, 256)],
-        [e_own, h_own, d_own, m_own, c_own, table],
+        [constants, material_table, contrast.reshape(1, 3), e_own, h_own, d_own, m_own, c_own],
+        scratch=[pltpu.SemaphoreType.DMA((3,))], in_specs=[ANY] * 3 + [VM] * 5,
     )
     e_all, h_all, d_all, c_all, m_all, pairs, left, right, sums = call(
         halo_kernel,
@@ -575,20 +618,29 @@
         background_kernel, [vmem(PLANES * ROWS, 128), vmem(DZ * ROWS, 256)],
         [m_all, d_all, mtable, table, local], aliases={4: 1},
     )
-    at = 2 + len(rest)
+    h_all, se, sh, traits, sums = call(
+        first_kernel(count, reach),
+        [vmem(PLANES * ROWS, 128), vmem(3 * ROWS, 128), vmem(3 * ROWS, 128),
+         vmem(3 * ROWS, 128), vmem(ROWS, 128)],
+        [from_right, from_left, pairs, e_all, h_all],
+        aliases={4: 0},
+    )
+    at = len(rest)
+    operands = rest + [
+        e_all, h_all, se, sh, traits, sums, d_all, c_all, background, local, table, mtable,
+        contrasts, forward_fields.reshape(STEPS, PLANES, OWN, 128),
+    ]
     outs = call(
-        step_kernel(count, reach, len(rest)),
+        step_kernel(count, reach, at),
         [jax.ShapeDtypeStruct((PLANES * OWN, 128), jnp.float32),
          jax.ShapeDtypeStruct((PLANES * OWN, 128), jnp.float32),
          jax.ShapeDtypeStruct((DZ * OWN, 128), jnp.float32),
-         vmem(PLANES * ROWS, 128), vmem(PLANES * ROWS, 128)],
-        [from_right, from_left] + rest + [
-            e_all, h_all, d_all, c_all, background, pairs, local, table,
-            mtable, contrasts, forward_fields.reshape(STEPS, PLANES, OWN, 128),
-        ],
-        aliases={at: 3, at + 1: 4},
-        scratch=[vmem(PLANES * ROWS, 128), vmem(3 * ROWS, 128), vmem(3 * ROWS, 128),
-                 vmem(3 * ROWS, 128), vmem(DZ * OWN, 128)],
+         vmem(PLANES * ROWS, 128), vmem(PLANES * ROWS, 128), vmem(3 * ROWS, 128),
+         vmem(3 * ROWS, 128)],
+        operands,
+        aliases={at: 3, at + 1: 4, at + 2: 5, at + 3: 6},
+        scratch=[vmem(PLANES * ROWS, 128), vmem(3 * ROWS, 128), vmem(DZ * OWN, 128),
+                 ],
     )
     return (
         outs[0].reshape(electric.shape), outs[1].reshape(magnetic.shape),

time: 19.2 us -> 18.8 us (0.979)
  waiting for transfers between devices: 5.24 us -> 4 us
  Pallas kernels: 4.95 us -> 5.85 us
    ppermute x5, waiting for transfers between devices: 5.24 us -> 4 us  [sent(): return lax.ppermute(x, axis, [(i, (i + by) % size) for i in range(size)])]
    pallas_call x5 -> x6, Pallas kernels: 4.95 us -> 5.85 us  [call(): pl.pallas_call(kernel, out_shape=outs, in_specs=in_specs, out_specs=out_s...]
  transfers between devices with their start and end apart: 5 -> 5, of which waited for: 2 -> 3; matrix products, arithmetic and copies ran while one was open for 0% -> 0% of each run, Pallas kernels for 3% -> 10%
where the time goes in v4:
time: 18.8 us; the launch traced here: 18.7 us
  starting transfers between devices  8.14 us (43%)
  Pallas kernels  5.85 us (31%)
  waiting for transfers between devices  4 us (21%)
  between operations  0.69 us (4%)
    ppermute x5, starting transfers between devices, sent(): return lax.ppermute(x, axis, [(i, (i + by) % size) for i in range(size)])  8.14 us
    pallas_call x6, Pallas kernels, call(): pl.pallas_call(kernel, out_shape=outs, in_specs=in_specs, out_specs=out_s...  5.85 us
    ppermute x5, waiting for transfers between devices, sent(): return lax.ppermute(x, axis, [(i, (i + by) % size) for i in range(size)])  4 us
  transfers between devices with their start and end apart: 5, of which 3 were waited for; matrix products, arithmetic and copies ran while one was open for 0% of the time, Pallas kernels for 10%

profile of v4, /device:TPU:0, one launch (start us, length us, event | category | flops | bytes accessed | tf_op | source)
XLA Modules:
  0.0 18.7 jit_solution(10614182884174564973)
XLA Ops:
  0.6 1.2 %shard_map.112 = (f32[184,128]{1,0:T(8,128)S(1)}, f32[208,128]{1,0:T(8,128)S(1)}, f32[384,128]{1,0:T(8,128)S(1)}, f32[384,128]{1,0:T(8,128)S(1)}, f32[64,128]{1,...) custom-call(f32[384,128]{1,0:T(8,128)} %bitcast.10, f32[384,128]{1,0:T(8,128)} %bitcast.11, ...), custom_call_target="tpu_custom_call" | custom-call | tf_op jit(solution)/shard_map/pallas_call | solution.py:44
  1.9 3.0 %collective-permute-start.1 = (f32[208,128]{1,0:T(8,128)S(1)}, f32[208,128]{1,0:T(8,128)S(1)}, u32[]{:S(2)}, u32[]{:S(2)}) collective-permute-start(f32[208,128]{1,0:T(8,128)S(1)} %get-tuple-element.42), channel_id=1, source_target_pairs={{0,4},{4,8},{8,12},{12,16},{16,20},{20,24},{24,28},{28,0},{1,5},{5... | collective-permute-start | bytes 319496 | tf_op jit(solution)/shard_map/ppermute | solution.py:69
  4.9 3.1 %collective-permute-start = (f32[184,128]{1,0:T(8,128)S(1)}, f32[184,128]{1,0:T(8,128)S(1)}, u32[]{:S(2)}, u32[]{:S(2)}) collective-permute-start(f32[184,128]{1,0:T(8,128)S(1)} %get-tuple-element.41), channel_id=1, source_target_pairs={{0,28},{4,0},{8,4},{12,8},{16,12},{20,16},{24,20},{28,24},{1,29},{... | collective-permute-start | bytes 282632 | tf_op jit(solution)/shard_map/ppermute | solution.py:69
  8.0 1.3 %shard_map.113 = (f32[136,256]{1,0:T(8,128)S(1)}, f32[3,4]{1,0:T(4,128)S(1)}, f32[1,3]{1,0:T(1,128)S(1)}, f32[576,128]{1,0:T(8,128)S(1)}, f32[576,128]{1,0:T(8,1...) custom-call(f32[136,256]{1,0:T(8,128)} %constant.2.clone.table_in, ...), custom_call_target="tpu_custom_call" | custom-call | tf_op jit(solution)/shard_map/pallas_call | solution.py:44
  9.3 2.5 %collective-permute-done.from_next = f32[184,128]{1,0:T(8,128)S(1)} collective-permute-done((f32[184,128]{1,0:T(8,128)S(1)}, f32[184,128]{1,0:T(8,128)S(1)}, u32[]{:S(2)}, u32[]{:S(2)}) %collective-permute-start) | collective-permute-done | bytes 94240 | tf_op jit(solution)/shard_map/ppermute | solution.py:69
  11.7 0.0 collective-permute-done.1.from_prev
  11.7 0.4 %shard_map.114 = (f32[576,128]{1,0:T(8,128)S(1)}, f32[576,128]{1,0:T(8,128)S(1)}, f32[96,128]{1,0:T(8,128)S(1)}, f32[24,128]{1,0:T(8,128)S(1)}, f32[192,128]{1,0...) custom-call(f32[184,128]{1,0:T(8,128)S(1)} %collective-permute-done., ...), custom_call_target="tpu_custom_call", output_to_operand_aliasing={{0}: (2, {}), {1}: (3, {}), {2}: (4, {}), {3}: (5, {}), {4}... | custom-call | tf_op jit(solution)/shard_map/pallas_call | solution.py:44
  12.2 0.0 collective-permute-start.3
  12.2 0.5 %collective-permute-start.4 = (f32[48,128]{1,0:T(8,128)S(1)}, f32[48,128]{1,0:T(8,128)S(1)}, u32[]{:S(2)}, u32[]{:S(2)}) collective-permute-start(f32[48,128]{1,0:T(8,128)S(1)} %get-tuple-element.60), channel_id=1, source_target_pairs={{0,1},{1,2},{2,3},{3,0},{4,5},{5,6},{6,7},{7,4},{8,9},{9,10},{10,1... | collective-permute-start | bytes 73736 | tf_op jit(solution)/shard_map/ppermute | solution.py:69
  12.7 1.5 %collective-permute-start.2 = (f32[8,128]{1,0:T(8,128)S(1)}, f32[8,128]{1,0:T(8,128)S(1)}, u32[]{:S(2)}, u32[]{:S(2)}) collective-permute-start(f32[8,128]{1,0:T(8,128)S(1)} %get-tuple-element.57), channel_id=1, source_target_pairs={{0,2},{1,3},{2,0},{3,1},{4,6},{5,7},{6,4},{7,5},{8,10},{9,11},{10,... | collective-permute-start | bytes 12296 | tf_op jit(solution)/shard_map/ppermute | solution.py:69
  14.2 0.2 %shard_map.116 = (f32[576,128]{1,0:T(8,128)S(1)}, f32[96,256]{1,0:T(8,128)S(1)}) custom-call(f32[192,128]{1,0:T(8,128)S(1)} %get-tuple-element.70.m_all, f32[96,128]{1,0:T(8,128)S(1)} %get-tuple-element.68.d_all.refs_7_, f32[3,4]{1,0:T(4,128)S(1)} %get-tuple-element.71.mtable.refs_12_, ...), custom_call_target="tpu_custom_call", output_to_operand_aliasing={{1}: (4, {})} | custom-call | tf_op jit(solution)/shard_map/pallas_call | solution.py:44
  14.4 0.0 copy-start
  14.4 0.0 collective-permute-done.3.from_right
  14.4 1.3 %collective-permute-done.4.from_left = f32[48,128]{1,0:T(8,128)S(1)} collective-permute-done((f32[48,128]{1,0:T(8,128)S(1)}, f32[48,128]{1,0:T(8,128)S(1)}, u32[]{:S(2)}, u32[]{:S(2)}) %collective-permute-start.4) | collective-permute-done | bytes 24608 | tf_op jit(solution)/shard_map/ppermute | solution.py:69
  15.8 0.4 %shard_map.115 = (f32[576,128]{1,0:T(8,128)S(1)}, f32[72,128]{1,0:T(8,128)S(1)}, f32[72,128]{1,0:T(8,128)S(1)}, f32[72,128]{1,0:T(8,128)S(1)}, f32[24,128]{1,0:T(8,128)S(1)}) custom-call(f32[48,128]{1,0:T(8,128)S(1)} %collective-permute-done.3.from_right, f32[48,128]{1,0:T(8,128)S(1)} %collective-permute-done.4.from_left, ...), custom_call_target="tpu_custom_call", output_to_operand_aliasing={{0}: (4, {})} | custom-call | tf_op jit(solution)/shard_map/pallas_call | solution.py:44
  16.1 0.2 collective-permute-done.2.refs_0_
  16.3 0.0 copy-done
  16.3 2.4 %shard_map.117 = (f32[384,128]{1,0:T(8,128)}, f32[384,128]{1,0:T(8,128)}, f32[64,128]{1,0:T(8,128)}, f32[576,128]{1,0:T(8,128)S(1)}, f32[576,128]{1,0:T(8,128)S(...) custom-call(f32[8,128]{1,0:T(8,128)S(1)} %collective-permute-done.2., ...), custom_call_target="tpu_custom_call", output_to_operand_aliasing={{3}: (1, {}), {4}: (2, {}), {5}: (3, {}), {6}: (4, {})} | custom-call | tf_op jit(solution)/shard_map/pallas_call | solution.py:44
Async XLA Ops:
  1.9 9.9 %collective-permute-start.1 = (f32[208,128]{1,0:T(8,128)S(1)}, f32[208,128]{1,0:T(8,128)S(1)}, u32[]{:S(2)}, u32[]{:S(2)}) collective-permute-start(f32[208,128]{1,0:T(8,128)S(1)} %get-tuple-element.42), channel_id=1, source_target_pairs={{0,4},{4,8},{8,12},{12,16},{16,20},{20,24},{24,28},{28,0},{1,5},{5... | collective-permute-start | bytes 319496 | tf_op jit(solution)/shard_map/ppermute | solution.py:69
  4.9 6.9 %collective-permute-start = (f32[184,128]{1,0:T(8,128)S(1)}, f32[184,128]{1,0:T(8,128)S(1)}, u32[]{:S(2)}, u32[]{:S(2)}) collective-permute-start(f32[184,128]{1,0:T(8,128)S(1)} %get-tuple-element.41), channel_id=1, source_target_pairs={{0,28},{4,0},{8,4},{12,8},{16,12},{20,16},{24,20},{28,24},{1,29},{... | collective-permute-start | bytes 282632 | tf_op jit(solution)/shard_map/ppermute | solution.py:69
  12.2 2.2 %collective-permute-start.3 = (f32[48,128]{1,0:T(8,128)S(1)}, f32[48,128]{1,0:T(8,128)S(1)}, u32[]{:S(2)}, u32[]{:S(2)}) collective-permute-start(f32[48,128]{1,0:T(8,128)S(1)} %get-tuple-element.59), channel_id=1, source_target_pairs={{0,3},{1,0},{2,1},{3,2},{4,7},{5,4},{6,5},{7,6},{8,11},{9,8},{10,9... | collective-permute-start | bytes 73736 | tf_op jit(solution)/shard_map/ppermute | solution.py:69
  12.2 3.5 %collective-permute-start.4 = (f32[48,128]{1,0:T(8,128)S(1)}, f32[48,128]{1,0:T(8,128)S(1)}, u32[]{:S(2)}, u32[]{:S(2)}) collective-permute-start(f32[48,128]{1,0:T(8,128)S(1)} %get-tuple-element.60), channel_id=1, source_target_pairs={{0,1},{1,2},{2,3},{3,0},{4,5},{5,6},{6,7},{7,4},{8,9},{9,10},{10,1... | collective-permute-start | bytes 73736 | tf_op jit(solution)/shard_map/ppermute | solution.py:69
  12.7 3.6 %collective-permute-start.2 = (f32[8,128]{1,0:T(8,128)S(1)}, f32[8,128]{1,0:T(8,128)S(1)}, u32[]{:S(2)}, u32[]{:S(2)}) collective-permute-start(f32[8,128]{1,0:T(8,128)S(1)} %get-tuple-element.57), channel_id=1, source_target_pairs={{0,2},{1,3},{2,0},{3,1},{4,6},{5,7},{6,4},{7,5},{8,10},{9,11},{10,... | collective-permute-start | bytes 12296 | tf_op jit(solution)/shard_map/ppermute | solution.py:69
  14.4 1.9 %copy-start = (bf16[4,3,8,16,128]{4,3,2,1,0:T(8,128)(2,1)S(1)}, bf16[4,3,8,16,128]{4,3,2,1,0:T(8,128)(2,1)}, u32[]{:S(2)}) copy-start(bf16[4,3,8,16,128]{4,3,2,1,0:T(8,128)(2,1)} %param.16) | copy-start | bytes 1179652

commit v5 on v4

--- a/solution.py
+++ b/solution.py
@@ -122,14 +122,22 @@
     return left, right
 
 
-def density_planes(layers, cells, rising, falling):
-    place = lanes(cells.shape[0]) & 3
-    planes = []
-    for layer in layers:
+def density_planes(layers, cells):
+    return [plane for layer in layers for plane in (layer, cells)]
+
+
+def with_sums(tiles, layers):
+    lane = lanes(layers[0].shape[0])
+    column = lanes(1).astype(jnp.float32) * (1.0 / (4.0 * CY))
+    rising, falling = jnp.exp(column), jnp.exp(-column)
+    for l, layer in enumerate(layers):
+        at = (2 * l + 1) * 16 + 12
         up = jnp.sum(layer * rising, axis=1, keepdims=True)
         down = jnp.sum(layer * falling, axis=1, keepdims=True)
-        planes += [layer, jnp.where(place == 0, up, jnp.where(place == 1, down, cells))]
-    return planes
+        tiles = [
+            jnp.where(lane == at, up, jnp.where(lane == at + 1, down, tile)) for tile in tiles
+        ]
+    return tiles
 
 
 def pack_kernel(
@@ -139,18 +147,18 @@
 ):
     copies = []
     moved = [
-        (mask, mask_v), (electric, e_own), (magnetic, h_own), (density, d_own), (material, m_own),
+        (electric, e_own), (magnetic, h_own), (density, d_own), (material, m_own), (mask, mask_v),
     ]
     for i, (source, target) in enumerate(moved):
         copy = pltpu.make_async_copy(source, target, sems.at[i])
         copy.start()
         copies.append(copy)
-    for copy in copies:
-        copy.wait()
-
+    copies[-1].wait()
     cells = cell_rows(mask_v[...])
     c_all[0:TILE, :] = jnp.broadcast_to(cells[0:1], (TILE, 128))
     c_all[TILE:OWN, :] = jnp.broadcast_to(cells[1:2], (TILE, 128))
+    for copy in copies[:-1]:
+        copy.wait()
 
     def e(channel, row):
         return e_own[pl.ds(channel * Z * OWN + row, Z, stride=OWN), :]
@@ -221,13 +229,10 @@
     for l in range(DZ):
         layers.append(d_own[l * OWN : (l + 1) * OWN, :])
         d_all[l * ROWS : l * ROWS + OWN, :] = layers[l]
-    column = lanes(1).astype(jnp.float32) * (1.0 / (4.0 * CY))
-    rising, falling = jnp.exp(column), jnp.exp(-column)
-    groups.append(
-        density_planes(layers, c_own[...], rising, falling)
-    )
+    groups.append(density_planes(layers, c_own[...]))
     pairs = edge_pairs(groups)
     left, right = edge_messages(pairs)
+    left[1], right[1] = with_sums([left[1], right[1]], layers)
     for i in range(4):
         pairs_out[i * ROWS : i * ROWS + OWN, :] = pairs[i]
     for i in range(2):
@@ -243,39 +248,56 @@
         local[l * ROWS : l * ROWS + OWN, :] = smooth[l * OWN : (l + 1) * OWN]
 
 
+def unpack(got, first, e_all, h_all, d_all, c_all, m_all):
+    for slot in range(3):
+        at, row = slot * SLOT, first + slot
+        for channel in range(3):
+            where = pl.ds(channel * Z * ROWS + row, Z, stride=ROWS)
+            e_all[where, :] = got[at + 8 * channel : at + 8 * channel + 8, :]
+            h_all[where, :] = got[at + 24 + 8 * channel : at + 32 + 8 * channel, :]
+        m_all[pl.ds(row, Z, stride=ROWS), :] = got[KINDS + 8 * slot : KINDS + 8 * slot + 8, :]
+        d_all[pl.ds(row, DZ, stride=ROWS), :] = got[LAYERS + 4 * slot : LAYERS + 4 * slot + 4, :]
+        c_all[row : row + 1, :] = got[LAYERS + 12 : LAYERS + 13, :]
+
+
+def unpack_next(got, e_all, h_all, d_all, c_all, m_all):
+    unpack(got, 16, e_all, h_all, d_all, c_all, m_all)
+    zeros = jnp.zeros((Z, 128), jnp.float32)
+    for channel in range(3):
+        where = pl.ds(channel * Z * ROWS + 19, Z, stride=ROWS)
+        e_all[where, :] = got[2 * SLOT + 8 * channel : 2 * SLOT + 8 * channel + 8, :]
+        h_all[where, :] = zeros
+    m_all[pl.ds(19, Z, stride=ROWS), :] = zeros
+    d_all[pl.ds(19, DZ, stride=ROWS), :] = zeros[0:DZ]
+    c_all[19:20, :] = zeros[0:1]
+
+
+def unpack_prev(got, e_all, h_all, d_all, c_all, m_all):
+    unpack(got, 21, e_all, h_all, d_all, c_all, m_all)
+    zeros = jnp.zeros((Z, 128), jnp.float32)
+    for channel in range(3):
+        where = pl.ds(channel * Z * ROWS + 20, Z, stride=ROWS)
+        extra = got[EXTRA + 8 * channel : EXTRA + 8 * channel + 8, :]
+        if channel == 0:
+            e_all[where, :] = extra
+            h_all[where, :] = zeros
+        else:
+            e_all[where, :] = got[8 * channel : 8 * channel + 8, :]
+            h_all[where, :] = extra
+    m_all[pl.ds(20, Z, stride=ROWS), :] = zeros
+    d_all[pl.ds(20, DZ, stride=ROWS), :] = zeros[0:DZ]
+    c_all[20:21, :] = zeros[0:1]
+
+
+def early_kernel(got, e_in, h_in, d_in, c_in, m_in, e_all, h_all, d_all, c_all, m_all):
+    unpack_prev(got, e_all, h_all, d_all, c_all, m_all)
+
+
 def halo_kernel(
-    from_next, from_prev, e_in, h_in, d_in, c_in, m_in, pairs_in, left_in, right_in, table,
+    got, e_in, h_in, d_in, c_in, m_in, pairs_in, left_in, right_in, table,
     e_all, h_all, d_all, c_all, m_all, pairs_out, left_out, right_out, sums_out,
 ):
-    for got, first in ((from_next, 16), (from_prev, 21)):
-        for slot in range(3):
-            at, row = slot * SLOT, first + slot
-            for channel in range(3):
-                where = pl.ds(channel * Z * ROWS + row, Z, stride=ROWS)
-                e_all[where, :] = got[at + 8 * channel : at + 8 * channel + 8, :]
-                h_all[where, :] = got[at + 24 + 8 * channel : at + 32 + 8 * channel, :]
-            m_all[pl.ds(row, Z, stride=ROWS), :] = got[KINDS + 8 * slot : KINDS + 8 * slot + 8, :]
-            d_all[pl.ds(row, DZ, stride=ROWS), :] = got[LAYERS + 4 * slot : LAYERS + 4 * slot + 4, :]
-            c_all[row : row + 1, :] = got[LAYERS + 12 : LAYERS + 13, :]
-    zeros = jnp.zeros((Z, 128), jnp.float32)
-    for channel in range(3):
-        at = channel * Z * ROWS
-        e_all[pl.ds(at + 19, Z, stride=ROWS), :] = from_next[
-            2 * SLOT + 8 * channel : 2 * SLOT + 8 * channel + 8, :
-        ]
-        h_all[pl.ds(at + 19, Z, stride=ROWS), :] = zeros
-        if channel > 0:
-            e_all[pl.ds(at + 20, Z, stride=ROWS), :] = from_prev[8 * channel : 8 * channel + 8, :]
-            h_all[pl.ds(at + 20, Z, stride=ROWS), :] = from_prev[
-                EXTRA + 8 * channel : EXTRA + 8 * channel + 8, :
-            ]
-        else:
-            e_all[pl.ds(at + 20, Z, stride=ROWS), :] = from_prev[EXTRA : EXTRA + 8, :]
-            h_all[pl.ds(at + 20, Z, stride=ROWS), :] = zeros
-    for row in (19, 20):
-        m_all[pl.ds(row, Z, stride=ROWS), :] = zeros
-        d_all[pl.ds(row, DZ, stride=ROWS), :] = zeros[0:DZ]
-        c_all[row : row + 1, :] = zeros[0:1]
+    unpack_next(got, e_all, h_all, d_all, c_all, m_all)
 
     groups = []
     for target in (e_all, h_all):
@@ -285,11 +307,10 @@
             )
     groups.append([m_all[z * ROWS + OWN : (z + 1) * ROWS, :] for z in range(Z)])
     layers = [d_all[l * ROWS + OWN : (l + 1) * ROWS, :] for l in range(DZ)]
-    groups.append(
-        density_planes(layers, c_all[OWN:ROWS, :], table[130:131, 0:128], table[131:132, 0:128])
-    )
+    groups.append(density_planes(layers, c_all[OWN:ROWS, :]))
     pairs = edge_pairs(groups)
     left, right = edge_messages(pairs)
+    left[1], right[1] = with_sums([left[1], right[1]], layers)
     for i in range(4):
         pairs_out[i * ROWS + OWN : (i + 1) * ROWS, :] = pairs[i]
     for i in range(2):
@@ -434,10 +455,23 @@
     return jnp.where((lanes(ROWS) & 15) == 12, up, down)
 
 
+def norm_of(count, reach):
+    return 2.0 * float(np.sum(np.exp(-np.arange(count) / reach)))
+
+
 def first_kernel(count, reach):
     devices = count // CY
-
-    def kernel(from_right, from_left, pairs, e_all, h_in, h_all, se, sh, traits, sums):
+    norm_total = norm_of(count, reach)
+
+    def fix(delta):
+        if delta == 0:
+            return 1.0 - math.exp(-count / reach)
+        return (
+            math.exp(-delta / reach) + math.exp(-(count - delta) / reach)
+            - math.exp(-(count + delta) / reach) - math.exp(delta / reach)
+        )
+
+    def kernel(from_right, from_left, pairs, e_all, h_in, mtable, h_all, se, sh, traits, sums):
         lane = lanes(ROWS)
         place = lane & 15
         odd = ((lane >> 4) & 1) == 1
@@ -462,13 +496,23 @@
         keep(sh, strip_magnetic([strip(3 + c) for c in range(3)], electric))
         raw = strip(7)
         marks = jnp.where(odd, raw, roll(raw, -16))
+        layers = jnp.where(odd, roll(raw, 16), raw)
+        known = jnp.zeros((ROWS, 128), jnp.float32)
+        for delta in range(4):
+            value = fix(delta) * layers
+            ahead = value if delta == 0 else roll(value, delta)
+            behind = value if delta == 0 else roll(value, -delta)
+            known = known + jnp.where(place >= 12 + delta, ahead, 0.0)
+            known = known + jnp.where(place < 4 - delta, behind, 0.0)
+        kind = strip(6)
+        entries = mtable[...]
         keep(
             traits,
             [
-                strip(6),
-                jnp.where(odd, roll(raw, 16), raw),
+                0.5 * layers + (0.5 / norm_total) * known,
                 jnp.where((place & 2) == 2, marks, roll(marks, -2)),
-            ],
+            ]
+            + [looked_up(kind, entries, c) for c in range(3)],
         )
         sums[...] = (
             lane_factor(1, count, reach) * got_left[1]
@@ -480,26 +524,16 @@
 
 
 def step_kernel(count, reach, others):
-    norm_total = 2.0 * float(np.sum(np.exp(-np.arange(count) / reach)))
-
-    def fix(delta):
-        if delta == 0:
-            return 1.0 - math.exp(-count / reach)
-        return (
-            math.exp(-delta / reach) + math.exp(-(count - delta) / reach)
-            - math.exp(-(count + delta) / reach) - math.exp(delta / reach)
-        )
+    norm_total = norm_of(count, reach)
 
     def kernel(*refs):
         rest = refs[:others]
-        (e_in, h_in, se_in, sh_in, traits, sums_in, d_all, c_all, background, local, table, mtable,
+        (e_in, h_in, se_in, sh_in, traits, sums_in, d_all, c_all, background, local, table,
          contrast_in, forward,
          e_final, h_final, gradient, e_all, h_all, se, sh,
          inverse, si, gained) = refs[others:]
-        entries = mtable[...]
         contrast = [contrast_in[0:1, c : c + 1] for c in range(3)]
         lane = lanes(ROWS)
-        place = lane & 15
         layer_of = lane >> 5
 
         sums = sums_in[...]
@@ -508,7 +542,6 @@
             sums = sums + lane_factor(2 + i, count, reach) * jnp.concatenate(
                 [roll(packed, 2), roll(packed, -2), packed], 0
             )
-        strip_density = strip_of(traits, 1)
         strip_smooth = jnp.zeros((ROWS, 128), jnp.float32)
         designs = []
         cells = c_all[...]
@@ -524,21 +557,11 @@
             projected, slope = project(filtered)
             designs.append(cells * projected)
             gradient[l * OWN : (l + 1) * OWN, :] = slope[:OWN] * cells[:OWN]
-        for delta in range(4):
-            value = fix(delta) * strip_density
-            ahead = value if delta == 0 else roll(value, delta)
-            behind = value if delta == 0 else roll(value, -delta)
-            strip_smooth = strip_smooth + jnp.where(place >= 12 + delta, ahead, 0.0)
-            strip_smooth = strip_smooth + jnp.where(place < 4 - delta, behind, 0.0)
-        projected, _ = project(0.5 * strip_density + (0.5 / norm_total) * strip_smooth)
-        strip_design = strip_of(traits, 2) * projected
+        projected, _ = project(strip_of(traits, 0) + (0.5 / norm_total) * strip_smooth)
+        strip_design = strip_of(traits, 1) * projected
         keep(
             si,
-            [
-                courant
-                / (looked_up(strip_of(traits, 0), entries, c) + strip_design * contrast[c])
-                for c in range(3)
-            ],
+            [courant / (strip_of(traits, 2 + c) + strip_design * contrast[c]) for c in range(3)],
         )
         for z in range(Z):
             for channel in range(3):
@@ -603,13 +626,19 @@
         [constants, material_table, contrast.reshape(1, 3), e_own, h_own, d_own, m_own, c_own],
         scratch=[pltpu.SemaphoreType.DMA((3,))], in_specs=[ANY] * 3 + [VM] * 5,
     )
+    fields = [vmem(PLANES * ROWS, 128), vmem(PLANES * ROWS, 128), vmem(DZ * ROWS, 128),
+              vmem(ROWS, 128), vmem(Z * ROWS, 128)]
+    e_all, h_all, d_all, c_all, m_all = call(
+        early_kernel, fields, [from_prev, e_all, h_all, d_all, c_all, m_all],
+        aliases={i + 1: i for i in range(5)},
+    )
     e_all, h_all, d_all, c_all, m_all, pairs, left, right, sums = call(
         halo_kernel,
         [vmem(PLANES * ROWS, 128), vmem(PLANES * ROWS, 128), vmem(DZ * ROWS, 128),
          vmem(ROWS, 128), vmem(Z * ROWS, 128), vmem(4 * ROWS, 128),
          vmem(2 * ROWS, 128), vmem(2 * ROWS, 128), vmem(8, 128)],
-        [from_next, from_prev, e_all, h_all, d_all, c_all, m_all, pairs, left, right, table],
-        aliases={2: 0, 3: 1, 4: 2, 5: 3, 6: 4, 7: 5, 8: 6, 9: 7},
+        [from_next, e_all, h_all, d_all, c_all, m_all, pairs, left, right, table],
+        aliases={i + 1: i for i in range(8)},
     )
     from_left = sent(right, "gy", 1)
     from_right = sent(left, "gy", -1)
@@ -621,13 +650,13 @@
     h_all, se, sh, traits, sums = call(
         first_kernel(count, reach),
         [vmem(PLANES * ROWS, 128), vmem(3 * ROWS, 128), vmem(3 * ROWS, 128),
-         vmem(3 * ROWS, 128), vmem(ROWS, 128)],
-        [from_right, from_left, pairs, e_all, h_all],
+         vmem(5 * ROWS, 128), vmem(ROWS, 128)],
+        [from_right, from_left, pairs, e_all, h_all, mtable],
         aliases={4: 0},
     )
     at = len(rest)
     operands = rest + [
-        e_all, h_all, se, sh, traits, sums, d_all, c_all, background, local, table, mtable,
+        e_all, h_all, se, sh, traits, sums, d_all, c_all, background, local, table,
         contrasts, forward_fields.reshape(STEPS, PLANES, OWN, 128),
     ]
     outs = call(

time: 18.8 us -> 18.8 us (level)
    pallas_call x6 -> x7, Pallas kernels: 5.85 us -> 5.81 us  [call(): pl.pallas_call(kernel, out_shape=outs, in_specs=in_specs, out_specs=out_s...]
  transfers between devices with their start and end apart: 5 -> 5, of which waited for: 3 -> 4; matrix products, arithmetic and copies ran while one was open for 0% -> 0% of each run, Pallas kernels for 10% -> 10%
where the time goes in v5:
time: 18.8 us; the launch traced here: 18.6 us
  starting transfers between devices  8.17 us (43%)
  Pallas kernels  5.81 us (31%)
  waiting for transfers between devices  3.9 us (21%)
  between operations  0.7 us (4%)
    ppermute x5, starting transfers between devices, sent(): return lax.ppermute(x, axis, [(i, (i + by) % size) for i in range(size)])  8.17 us
    pallas_call x7, Pallas kernels, call(): pl.pallas_call(kernel, out_shape=outs, in_specs=in_specs, out_specs=out_s...  5.81 us
    ppermute x5, waiting for transfers between devices, sent(): return lax.ppermute(x, axis, [(i, (i + by) % size) for i in range(size)])  3.9 us
  transfers between devices with their start and end apart: 5, of which 4 were waited for; matrix products, arithmetic and copies ran while one was open for 0% of the time, Pallas kernels for 10%

profile of v5, /device:TPU:0, one launch (start us, length us, event | category | flops | bytes accessed | tf_op | source)
XLA Modules:
  0.0 18.6 jit_solution(15541471341661517209)
XLA Ops:
  0.6 1.2 %shard_map.112 = (f32[184,128]{1,0:T(8,128)S(1)}, f32[208,128]{1,0:T(8,128)S(1)}, f32[384,128]{1,0:T(8,128)S(1)}, f32[384,128]{1,0:T(8,128)S(1)}, f32[64,128]{1,...) custom-call(f32[384,128]{1,0:T(8,128)} %bitcast.10, f32[384,128]{1,0:T(8,128)} %bitcast.11, ...), custom_call_target="tpu_custom_call" | custom-call | tf_op jit(solution)/shard_map/pallas_call | solution.py:44
  1.8 3.0 %collective-permute-start.1 = (f32[208,128]{1,0:T(8,128)S(1)}, f32[208,128]{1,0:T(8,128)S(1)}, u32[]{:S(2)}, u32[]{:S(2)}) collective-permute-start(f32[208,128]{1,0:T(8,128)S(1)} %get-tuple-element.47), channel_id=1, source_target_pairs={{0,4},{4,8},{8,12},{12,16},{16,20},{20,24},{24,28},{28,0},{1,5},{5... | collective-permute-start | bytes 319496 | tf_op jit(solution)/shard_map/ppermute | solution.py:69
  4.8 3.1 %collective-permute-start = (f32[184,128]{1,0:T(8,128)S(1)}, f32[184,128]{1,0:T(8,128)S(1)}, u32[]{:S(2)}, u32[]{:S(2)}) collective-permute-start(f32[184,128]{1,0:T(8,128)S(1)} %get-tuple-element.46), channel_id=1, source_target_pairs={{0,28},{4,0},{8,4},{12,8},{16,12},{20,16},{24,20},{28,24},{1,29},{... | collective-permute-start | bytes 282632 | tf_op jit(solution)/shard_map/ppermute | solution.py:69
  7.9 1.3 %shard_map.113 = (f32[136,256]{1,0:T(8,128)S(1)}, f32[3,4]{1,0:T(4,128)S(1)}, f32[1,3]{1,0:T(1,128)S(1)}, f32[576,128]{1,0:T(8,128)S(1)}, f32[576,128]{1,0:T(8,1...) custom-call(f32[136,256]{1,0:T(8,128)} %constant.2.clone.table_in, ...), custom_call_target="tpu_custom_call" | custom-call | tf_op jit(solution)/shard_map/pallas_call | solution.py:44
  9.2 1.7 %collective-permute-done.1.got = f32[208,128]{1,0:T(8,128)S(1)} collective-permute-done((f32[208,128]{1,0:T(8,128)S(1)}, f32[208,128]{1,0:T(8,128)S(1)}, u32[]{:S(2)}, u32[]{:S(2)}) %collective-permute-start.1) | collective-permute-done | bytes 106528 | tf_op jit(solution)/shard_map/ppermute | solution.py:69
  11.0 0.7 %collective-permute-done.got = f32[184,128]{1,0:T(8,128)S(1)} collective-permute-done((f32[184,128]{1,0:T(8,128)S(1)}, f32[184,128]{1,0:T(8,128)S(1)}, u32[]{:S(2)}, u32[]{:S(2)}) %collective-permute-start) | collective-permute-done | bytes 94240 | tf_op jit(solution)/shard_map/ppermute | solution.py:69
  11.7 0.4 %shard_map.115 = (f32[576,128]{1,0:T(8,128)S(1)}, f32[576,128]{1,0:T(8,128)S(1)}, f32[96,128]{1,0:T(8,128)S(1)}, f32[24,128]{1,0:T(8,128)S(1)}, f32[192,128]{1,0...) custom-call(f32[184,128]{1,0:T(8,128)S(1)} %collective-permute-done., ...), custom_call_target="tpu_custom_call", output_to_operand_aliasing={{0}: (1, {}), {1}: (2, {}), {2}: (3, {}), {3}: (4, {}), {4}... | custom-call | tf_op jit(solution)/shard_map/pallas_call | solution.py:44
  12.1 0.1 collective-permute-start.3
  12.1 0.5 %collective-permute-start.4 = (f32[48,128]{1,0:T(8,128)S(1)}, f32[48,128]{1,0:T(8,128)S(1)}, u32[]{:S(2)}, u32[]{:S(2)}) collective-permute-start(f32[48,128]{1,0:T(8,128)S(1)} %get-tuple-element.70), channel_id=1, source_target_pairs={{0,1},{1,2},{2,3},{3,0},{4,5},{5,6},{6,7},{7,4},{8,9},{9,10},{10,1... | collective-permute-start | bytes 73736 | tf_op jit(solution)/shard_map/ppermute | solution.py:69
  12.6 1.5 %collective-permute-start.2 = (f32[8,128]{1,0:T(8,128)S(1)}, f32[8,128]{1,0:T(8,128)S(1)}, u32[]{:S(2)}, u32[]{:S(2)}) collective-permute-start(f32[8,128]{1,0:T(8,128)S(1)} %get-tuple-element.67), channel_id=1, source_target_pairs={{0,2},{1,3},{2,0},{3,1},{4,6},{5,7},{6,4},{7,5},{8,10},{9,11},{10,... | collective-permute-start | bytes 12296 | tf_op jit(solution)/shard_map/ppermute | solution.py:69
  14.1 0.2 %shard_map.117 = (f32[576,128]{1,0:T(8,128)S(1)}, f32[96,256]{1,0:T(8,128)S(1)}) custom-call(f32[192,128]{1,0:T(8,128)S(1)} %get-tuple-element.81.m_all, f32[96,128]{1,0:T(8,128)S(1)} %get-tuple-element.79.d_all.refs_7_, f32[3,4]{1,0:T(4,128)S(1)} %get-tuple-element.73.mtable, ...), custom_call_target="tpu_custom_call", output_to_operand_aliasing={{1}: (4, {})} | custom-call | tf_op jit(solution)/shard_map/pallas_call | solution.py:44
  14.3 0.0 copy-start
  14.3 0.0 collective-permute-done.3.from_right
  14.3 1.3 %collective-permute-done.4.from_left = f32[48,128]{1,0:T(8,128)S(1)} collective-permute-done((f32[48,128]{1,0:T(8,128)S(1)}, f32[48,128]{1,0:T(8,128)S(1)}, u32[]{:S(2)}, u32[]{:S(2)}) %collective-permute-start.4) | collective-permute-done | bytes 24608 | tf_op jit(solution)/shard_map/ppermute | solution.py:69
  15.7 0.4 %shard_map.116 = (f32[576,128]{1,0:T(8,128)S(1)}, f32[72,128]{1,0:T(8,128)S(1)}, f32[72,128]{1,0:T(8,128)S(1)}, f32[120,128]{1,0:T(8,128)S(1)}, f32[24,128]{1,0:T(8,128)S(1)}) custom-call(f32[48,128]{1,0:T(8,128)S(1)} %collective-permute-done.3.from_right, f32[48,128]{1,0:T(8,128)S(1)} %collective-permute-done.4.from_left, ...), custom_call_target="tpu_custom_call", output_to_operand_aliasing={{0}: (4, {})} | custom-call | tf_op jit(solution)/shard_map/pallas_call | solution.py:44
  16.1 0.1 collective-permute-done.2.refs_0_
  16.2 0.0 copy-done
  16.2 2.4 %shard_map.118 = (f32[384,128]{1,0:T(8,128)}, f32[384,128]{1,0:T(8,128)}, f32[64,128]{1,0:T(8,128)}, f32[576,128]{1,0:T(8,128)S(1)}, f32[576,128]{1,0:T(8,128)S(...) custom-call(f32[8,128]{1,0:T(8,128)S(1)} %collective-permute-done.2., ...), custom_call_target="tpu_custom_call", output_to_operand_aliasing={{3}: (1, {}), {4}: (2, {}), {5}: (3, {}), {6}: (4, {})} | custom-call | tf_op jit(solution)/shard_map/pallas_call | solution.py:44
  (1 shorter events, 0.0 us)
Async XLA Ops:
  1.8 9.1 %collective-permute-start.1 = (f32[208,128]{1,0:T(8,128)S(1)}, f32[208,128]{1,0:T(8,128)S(1)}, u32[]{:S(2)}, u32[]{:S(2)}) collective-permute-start(f32[208,128]{1,0:T(8,128)S(1)} %get-tuple-element.47), channel_id=1, source_target_pairs={{0,4},{4,8},{8,12},{12,16},{16,20},{20,24},{24,28},{28,0},{1,5},{5... | collective-permute-start | bytes 319496 | tf_op jit(solution)/shard_map/ppermute | solution.py:69
  4.8 6.9 %collective-permute-start = (f32[184,128]{1,0:T(8,128)S(1)}, f32[184,128]{1,0:T(8,128)S(1)}, u32[]{:S(2)}, u32[]{:S(2)}) collective-permute-start(f32[184,128]{1,0:T(8,128)S(1)} %get-tuple-element.46), channel_id=1, source_target_pairs={{0,28},{4,0},{8,4},{12,8},{16,12},{20,16},{24,20},{28,24},{1,29},{... | collective-permute-start | bytes 282632 | tf_op jit(solution)/shard_map/ppermute | solution.py:69
  12.1 2.3 %collective-permute-start.3 = (f32[48,128]{1,0:T(8,128)S(1)}, f32[48,128]{1,0:T(8,128)S(1)}, u32[]{:S(2)}, u32[]{:S(2)}) collective-permute-start(f32[48,128]{1,0:T(8,128)S(1)} %get-tuple-element.69), channel_id=1, source_target_pairs={{0,3},{1,0},{2,1},{3,2},{4,7},{5,4},{6,5},{7,6},{8,11},{9,8},{10,9... | collective-permute-start | bytes 73736 | tf_op jit(solution)/shard_map/ppermute | solution.py:69
  12.1 3.5 %collective-permute-start.4 = (f32[48,128]{1,0:T(8,128)S(1)}, f32[48,128]{1,0:T(8,128)S(1)}, u32[]{:S(2)}, u32[]{:S(2)}) collective-permute-start(f32[48,128]{1,0:T(8,128)S(1)} %get-tuple-element.70), channel_id=1, source_target_pairs={{0,1},{1,2},{2,3},{3,0},{4,5},{5,6},{6,7},{7,4},{8,9},{9,10},{10,1... | collective-permute-start | bytes 73736 | tf_op jit(solution)/shard_map/ppermute | solution.py:69
  12.6 3.6 %collective-permute-start.2 = (f32[8,128]{1,0:T(8,128)S(1)}, f32[8,128]{1,0:T(8,128)S(1)}, u32[]{:S(2)}, u32[]{:S(2)}) collective-permute-start(f32[8,128]{1,0:T(8,128)S(1)} %get-tuple-element.67), channel_id=1, source_target_pairs={{0,2},{1,3},{2,0},{3,1},{4,6},{5,7},{6,4},{7,5},{8,10},{9,11},{10,... | collective-permute-start | bytes 12296 | tf_op jit(solution)/shard_map/ppermute | solution.py:69
  14.3 1.9 %copy-start = (bf16[4,3,8,16,128]{4,3,2,1,0:T(8,128)(2,1)S(1)}, bf16[4,3,8,16,128]{4,3,2,1,0:T(8,128)(2,1)}, u32[]{:S(2)}) copy-start(bf16[4,3,8,16,128]{4,3,2,1,0:T(8,128)(2,1)} %param.16) | copy-start | bytes 1179652

commit v6 on v5

--- a/solution.py
+++ b/solution.py
@@ -100,26 +100,23 @@
     return planes[0]
 
 
-def edge_pairs(groups):
+def edge_tiles(groups):
     lane = lanes(groups[0][0].shape[0])
-    first = (lane & 15) < 8
+    quarter = (lane >> 2) & 3
     found = [edge_window(planes) for planes in groups]
-    return [
-        jnp.where(first, roll(found[2 * i], 4), roll(found[2 * i + 1], 12)) for i in range(4)
-    ]
-
-
-def edge_messages(pairs):
-    quarter = (lanes(pairs[0].shape[0]) >> 2) & 3
 
     def pick(a, b, c, d):
         return jnp.where(quarter < 2, jnp.where(quarter == 0, a, b), jnp.where(quarter == 2, c, d))
 
     left, right = [], []
-    for one, two in ((pairs[0], pairs[1]), (pairs[2], pairs[3])):
-        left.append(pick(roll(one, -4), roll(one, -8), roll(two, 4), two))
-        right.append(pick(one, roll(one, -4), roll(two, 8), roll(two, 4)))
-    return left, right
+    for i in (0, 4):
+        one, two, three, four = found[i : i + 4]
+        left.append(pick(one, roll(two, 4), roll(three, 8), roll(four, 12)))
+        right.append(pick(roll(one, 4), roll(two, 8), roll(three, 12), roll(four, 16)))
+    pairs = [
+        jnp.where(quarter < 2, roll(found[i], 4), roll(found[i + 1], 12)) for i in range(0, 8, 2)
+    ]
+    return pairs, left, right
 
 
 def density_planes(layers, cells):
@@ -230,8 +227,7 @@
         layers.append(d_own[l * OWN : (l + 1) * OWN, :])
         d_all[l * ROWS : l * ROWS + OWN, :] = layers[l]
     groups.append(density_planes(layers, c_own[...]))
-    pairs = edge_pairs(groups)
-    left, right = edge_messages(pairs)
+    pairs, left, right = edge_tiles(groups)
     left[1], right[1] = with_sums([left[1], right[1]], layers)
     for i in range(4):
         pairs_out[i * ROWS : i * ROWS + OWN, :] = pairs[i]
@@ -308,8 +304,7 @@
     groups.append([m_all[z * ROWS + OWN : (z + 1) * ROWS, :] for z in range(Z)])
     layers = [d_all[l * ROWS + OWN : (l + 1) * ROWS, :] for l in range(DZ)]
     groups.append(density_planes(layers, c_all[OWN:ROWS, :]))
-    pairs = edge_pairs(groups)
-    left, right = edge_messages(pairs)
+    pairs, left, right = edge_tiles(groups)
     left[1], right[1] = with_sums([left[1], right[1]], layers)
     for i in range(4):
         pairs_out[i * ROWS + OWN : (i + 1) * ROWS, :] = pairs[i]
@@ -384,7 +379,7 @@
         (up_x - ex) - (roll_rows(ez, -1) - ez),
         (roll_rows(ey, -1) - ey) - (roll(ex, -1) - ex),
     )
-    return [field - courant * curl for field, curl in zip(old, curls)]
+    return [field - curl for field, curl in zip(old, curls)]
 
 
 def strip_electric(old, magnetic, inverse):
@@ -400,7 +395,7 @@
     return [old[c] + inverse[c] * curl for c, curl in enumerate(curls)]
 
 
-def planes_magnetic(e_all, h_in, h_out, strip_e):
+def planes_magnetic(e_all, h_in, h_out, strip_e, scale=1.0):
     lane = lanes(ROWS)
     last, first = lane == 127, lane == 0
     zero = jnp.zeros((ROWS, 128), jnp.float32)
@@ -419,7 +414,8 @@
             (dy_ez - (ey_up - ey), (ex_up - ex) - dx_ez, dx_ey - dy_ex)
         ):
             p = channel * Z + z
-            h_out[p * ROWS : (p + 1) * ROWS, :] = plane_of(h_in, channel, z) - courant * curl
+            old = plane_of(h_in, channel, z)
+            h_out[p * ROWS : (p + 1) * ROWS, :] = (old if scale == 1.0 else scale * old) - curl
 
 
 def planes_electric(e_all, h_all, inverse, strip_h, stored_at, contrast, gained, e_out, stride):
@@ -493,7 +489,7 @@
 
         electric = [strip(c) for c in range(3)]
         keep(se, electric)
-        keep(sh, strip_magnetic([strip(3 + c) for c in range(3)], electric))
+        keep(sh, strip_magnetic([strip(3 + c) * (1.0 / courant) for c in range(3)], electric))
         raw = strip(7)
         marks = jnp.where(odd, raw, roll(raw, -16))
         layers = jnp.where(odd, roll(raw, 16), raw)
@@ -518,7 +514,7 @@
             lane_factor(1, count, reach) * got_left[1]
             + lane_factor(devices - 1, count, reach) * got_right[1]
         )
-        planes_magnetic(e_all, h_in, h_all, electric)
+        planes_magnetic(e_all, h_in, h_all, electric, 1.0 / courant)
 
     return kernel
 
@@ -561,12 +557,12 @@
         strip_design = strip_of(traits, 1) * projected
         keep(
             si,
-            [courant / (strip_of(traits, 2 + c) + strip_design * contrast[c]) for c in range(3)],
+            [courant * courant / (strip_of(traits, 2 + c) + strip_design * contrast[c]) for c in range(3)],
         )
         for z in range(Z):
             for channel in range(3):
                 p = channel * Z + z
-                inverse[p * ROWS : (p + 1) * ROWS, :] = courant / (
+                inverse[p * ROWS : (p + 1) * ROWS, :] = courant * courant / (
                     background[p * ROWS : (p + 1) * ROWS, :] + designs[z // 2] * contrast[channel]
                 )
         gained[...] = jnp.zeros_like(gained)
@@ -587,7 +583,7 @@
 
         lax.fori_loop(0, STEPS - 1, step, 0)
         for p in range(PLANES):
-            h_final[p * OWN : (p + 1) * OWN, :] = h_all[p * ROWS : p * ROWS + OWN, :]
+            h_final[p * OWN : (p + 1) * OWN, :] = courant * h_all[p * ROWS : p * ROWS + OWN, :]
         planes_electric(
             e_all, h_all, inverse, [strip_of(sh, c) for c in range(3)],
             lambda p: forward[STEPS - 1, p], contrast, gained, e_final, OWN,

time: 18.8 us -> 18.7 us (level)
  no operation moved by 1% of the time
where the time goes in v6:
time: 18.7 us; the launch traced here: 18.6 us
  starting transfers between devices  8.17 us (44%)
  Pallas kernels  5.67 us (30%)
  waiting for transfers between devices  4.01 us (21%)
  between operations  0.7 us (4%)
    ppermute x5, starting transfers between devices, sent(): return lax.ppermute(x, axis, [(i, (i + by) % size) for i in range(size)])  8.17 us
    pallas_call x7, Pallas kernels, call(): pl.pallas_call(kernel, out_shape=outs, in_specs=in_specs, out_specs=out_s...  5.67 us
    ppermute x5, waiting for transfers between devices, sent(): return lax.ppermute(x, axis, [(i, (i + by) % size) for i in range(size)])  4.01 us
  transfers between devices with their start and end apart: 5, of which 4 were waited for; matrix products, arithmetic and copies ran while one was open for 0% of the time, Pallas kernels for 10%

profile of v6, /device:TPU:0, one launch (start us, length us, event | category | flops | bytes accessed | tf_op | source)
XLA Modules:
  0.0 18.6 jit_solution(10473821580898176251)
XLA Ops:
  0.6 1.2 %shard_map.112 = (f32[184,128]{1,0:T(8,128)S(1)}, f32[208,128]{1,0:T(8,128)S(1)}, f32[384,128]{1,0:T(8,128)S(1)}, f32[384,128]{1,0:T(8,128)S(1)}, f32[64,128]{1,...) custom-call(f32[384,128]{1,0:T(8,128)} %bitcast.10, f32[384,128]{1,0:T(8,128)} %bitcast.11, ...), custom_call_target="tpu_custom_call" | custom-call | tf_op jit(solution)/shard_map/pallas_call | solution.py:44
  1.8 3.0 %collective-permute-start.1 = (f32[208,128]{1,0:T(8,128)S(1)}, f32[208,128]{1,0:T(8,128)S(1)}, u32[]{:S(2)}, u32[]{:S(2)}) collective-permute-start(f32[208,128]{1,0:T(8,128)S(1)} %get-tuple-element.47), channel_id=1, source_target_pairs={{0,4},{4,8},{8,12},{12,16},{16,20},{20,24},{24,28},{28,0},{1,5},{5... | collective-permute-start | bytes 319496 | tf_op jit(solution)/shard_map/ppermute | solution.py:69
  4.8 3.1 %collective-permute-start = (f32[184,128]{1,0:T(8,128)S(1)}, f32[184,128]{1,0:T(8,128)S(1)}, u32[]{:S(2)}, u32[]{:S(2)}) collective-permute-start(f32[184,128]{1,0:T(8,128)S(1)} %get-tuple-element.46), channel_id=1, source_target_pairs={{0,28},{4,0},{8,4},{12,8},{16,12},{20,16},{24,20},{28,24},{1,29},{... | collective-permute-start | bytes 282632 | tf_op jit(solution)/shard_map/ppermute | solution.py:69
  7.9 1.1 %shard_map.113 = (f32[136,256]{1,0:T(8,128)S(1)}, f32[3,4]{1,0:T(4,128)S(1)}, f32[1,3]{1,0:T(1,128)S(1)}, f32[576,128]{1,0:T(8,128)S(1)}, f32[576,128]{1,0:T(8,1...) custom-call(f32[136,256]{1,0:T(8,128)} %constant.2.clone.table_in, ...), custom_call_target="tpu_custom_call" | custom-call | tf_op jit(solution)/shard_map/pallas_call | solution.py:44
  9.1 1.9 %collective-permute-done.1.got = f32[208,128]{1,0:T(8,128)S(1)} collective-permute-done((f32[208,128]{1,0:T(8,128)S(1)}, f32[208,128]{1,0:T(8,128)S(1)}, u32[]{:S(2)}, u32[]{:S(2)}) %collective-permute-start.1) | collective-permute-done | bytes 106528 | tf_op jit(solution)/shard_map/ppermute | solution.py:69
  11.0 0.7 %collective-permute-done.got = f32[184,128]{1,0:T(8,128)S(1)} collective-permute-done((f32[184,128]{1,0:T(8,128)S(1)}, f32[184,128]{1,0:T(8,128)S(1)}, u32[]{:S(2)}, u32[]{:S(2)}) %collective-permute-start) | collective-permute-done | bytes 94240 | tf_op jit(solution)/shard_map/ppermute | solution.py:69
  11.7 0.3 %shard_map.115 = (f32[576,128]{1,0:T(8,128)S(1)}, f32[576,128]{1,0:T(8,128)S(1)}, f32[96,128]{1,0:T(8,128)S(1)}, f32[24,128]{1,0:T(8,128)S(1)}, f32[192,128]{1,0...) custom-call(f32[184,128]{1,0:T(8,128)S(1)} %collective-permute-done., ...), custom_call_target="tpu_custom_call", output_to_operand_aliasing={{0}: (1, {}), {1}: (2, {}), {2}: (3, {}), {3}: (4, {}), {4}... | custom-call | tf_op jit(solution)/shard_map/pallas_call | solution.py:44
  12.0 0.1 collective-permute-start.3
  12.1 0.5 %collective-permute-start.4 = (f32[48,128]{1,0:T(8,128)S(1)}, f32[48,128]{1,0:T(8,128)S(1)}, u32[]{:S(2)}, u32[]{:S(2)}) collective-permute-start(f32[48,128]{1,0:T(8,128)S(1)} %get-tuple-element.70), channel_id=1, source_target_pairs={{0,1},{1,2},{2,3},{3,0},{4,5},{5,6},{6,7},{7,4},{8,9},{9,10},{10,1... | collective-permute-start | bytes 73736 | tf_op jit(solution)/shard_map/ppermute | solution.py:69
  12.6 1.5 %collective-permute-start.2 = (f32[8,128]{1,0:T(8,128)S(1)}, f32[8,128]{1,0:T(8,128)S(1)}, u32[]{:S(2)}, u32[]{:S(2)}) collective-permute-start(f32[8,128]{1,0:T(8,128)S(1)} %get-tuple-element.67), channel_id=1, source_target_pairs={{0,2},{1,3},{2,0},{3,1},{4,6},{5,7},{6,4},{7,5},{8,10},{9,11},{10,... | collective-permute-start | bytes 12296 | tf_op jit(solution)/shard_map/ppermute | solution.py:69
  14.1 0.2 %shard_map.117 = (f32[576,128]{1,0:T(8,128)S(1)}, f32[96,256]{1,0:T(8,128)S(1)}) custom-call(f32[192,128]{1,0:T(8,128)S(1)} %get-tuple-element.81.m_all, f32[96,128]{1,0:T(8,128)S(1)} %get-tuple-element.79.d_all.refs_7_, f32[3,4]{1,0:T(4,128)S(1)} %get-tuple-element.73.mtable, ...), custom_call_target="tpu_custom_call", output_to_operand_aliasing={{1}: (4, {})} | custom-call | tf_op jit(solution)/shard_map/pallas_call | solution.py:44
  14.3 0.0 copy-start
  14.3 0.0 collective-permute-done.3.from_right
  14.3 1.3 %collective-permute-done.4.from_left = f32[48,128]{1,0:T(8,128)S(1)} collective-permute-done((f32[48,128]{1,0:T(8,128)S(1)}, f32[48,128]{1,0:T(8,128)S(1)}, u32[]{:S(2)}, u32[]{:S(2)}) %collective-permute-start.4) | collective-permute-done | bytes 24608 | tf_op jit(solution)/shard_map/ppermute | solution.py:69
  15.6 0.5 %shard_map.116 = (f32[576,128]{1,0:T(8,128)S(1)}, f32[72,128]{1,0:T(8,128)S(1)}, f32[72,128]{1,0:T(8,128)S(1)}, f32[120,128]{1,0:T(8,128)S(1)}, f32[24,128]{1,0:T(8,128)S(1)}) custom-call(f32[48,128]{1,0:T(8,128)S(1)} %collective-permute-done.3.from_right, f32[48,128]{1,0:T(8,128)S(1)} %collective-permute-done.4.from_left, ...), custom_call_target="tpu_custom_call", output_to_operand_aliasing={{0}: (4, {})} | custom-call | tf_op jit(solution)/shard_map/pallas_call | solution.py:44
  16.1 0.1 collective-permute-done.2.refs_0_
  16.2 0.0 copy-done
  16.2 2.4 %shard_map.118 = (f32[384,128]{1,0:T(8,128)}, f32[384,128]{1,0:T(8,128)}, f32[64,128]{1,0:T(8,128)}, f32[576,128]{1,0:T(8,128)S(1)}, f32[576,128]{1,0:T(8,128)S(...) custom-call(f32[8,128]{1,0:T(8,128)S(1)} %collective-permute-done.2., ...), custom_call_target="tpu_custom_call", output_to_operand_aliasing={{3}: (1, {}), {4}: (2, {}), {5}: (3, {}), {6}: (4, {})} | custom-call | tf_op jit(solution)/shard_map/pallas_call | solution.py:44
  (1 shorter events, 0.0 us)
Async XLA Ops:
  1.8 9.1 %collective-permute-start.1 = (f32[208,128]{1,0:T(8,128)S(1)}, f32[208,128]{1,0:T(8,128)S(1)}, u32[]{:S(2)}, u32[]{:S(2)}) collective-permute-start(f32[208,128]{1,0:T(8,128)S(1)} %get-tuple-element.47), channel_id=1, source_target_pairs={{0,4},{4,8},{8,12},{12,16},{16,20},{20,24},{24,28},{28,0},{1,5},{5... | collective-permute-start | bytes 319496 | tf_op jit(solution)/shard_map/ppermute | solution.py:69
  4.8 6.9 %collective-permute-start = (f32[184,128]{1,0:T(8,128)S(1)}, f32[184,128]{1,0:T(8,128)S(1)}, u32[]{:S(2)}, u32[]{:S(2)}) collective-permute-start(f32[184,128]{1,0:T(8,128)S(1)} %get-tuple-element.46), channel_id=1, source_target_pairs={{0,28},{4,0},{8,4},{12,8},{16,12},{20,16},{24,20},{28,24},{1,29},{... | collective-permute-start | bytes 282632 | tf_op jit(solution)/shard_map/ppermute | solution.py:69
  12.0 2.3 %collective-permute-start.3 = (f32[48,128]{1,0:T(8,128)S(1)}, f32[48,128]{1,0:T(8,128)S(1)}, u32[]{:S(2)}, u32[]{:S(2)}) collective-permute-start(f32[48,128]{1,0:T(8,128)S(1)} %get-tuple-element.69), channel_id=1, source_target_pairs={{0,3},{1,0},{2,1},{3,2},{4,7},{5,4},{6,5},{7,6},{8,11},{9,8},{10,9... | collective-permute-start | bytes 73736 | tf_op jit(solution)/shard_map/ppermute | solution.py:69
  12.1 3.5 %collective-permute-start.4 = (f32[48,128]{1,0:T(8,128)S(1)}, f32[48,128]{1,0:T(8,128)S(1)}, u32[]{:S(2)}, u32[]{:S(2)}) collective-permute-start(f32[48,128]{1,0:T(8,128)S(1)} %get-tuple-element.70), channel_id=1, source_target_pairs={{0,1},{1,2},{2,3},{3,0},{4,5},{5,6},{6,7},{7,4},{8,9},{9,10},{10,1... | collective-permute-start | bytes 73736 | tf_op jit(solution)/shard_map/ppermute | solution.py:69
  12.6 3.6 %collective-permute-start.2 = (f32[8,128]{1,0:T(8,128)S(1)}, f32[8,128]{1,0:T(8,128)S(1)}, u32[]{:S(2)}, u32[]{:S(2)}) collective-permute-start(f32[8,128]{1,0:T(8,128)S(1)} %get-tuple-element.67), channel_id=1, source_target_pairs={{0,2},{1,3},{2,0},{3,1},{4,6},{5,7},{6,4},{7,5},{8,10},{9,11},{10,... | collective-permute-start | bytes 12296 | tf_op jit(solution)/shard_map/ppermute | solution.py:69
  14.3 1.9 %copy-start = (bf16[4,3,8,16,128]{4,3,2,1,0:T(8,128)(2,1)S(1)}, bf16[4,3,8,16,128]{4,3,2,1,0:T(8,128)(2,1)}, u32[]{:S(2)}) copy-start(bf16[4,3,8,16,128]{4,3,2,1,0:T(8,128)(2,1)} %param.16) | copy-start | bytes 1179652

commit v7 on v6

--- a/solution.py
+++ b/solution.py
@@ -317,7 +317,12 @@
     sums_out[...] = jnp.where(place > 13, roll(left_in[ROWS + 8 : ROWS + OWN, :], 2), packed)
 
 
-def background_kernel(m_all, d_all, mtable, table, local_in, background, local):
+def background_kernel(
+    forward_in, contrast_in, m_all, d_all, mtable, table, local_in,
+    background, local, forward, fetched, sem,
+):
+    copy = pltpu.make_async_copy(forward_in, fetched, sem)
+    copy.start()
     smooth = jnp.dot(
         jnp.concatenate([d_all[l * ROWS + OWN : (l + 1) * ROWS, :] for l in range(DZ)], 0),
         table[0:128, :], precision=lax.Precision.HIGHEST, preferred_element_type=jnp.float32,
@@ -330,6 +335,15 @@
         for channel in range(3):
             p = channel * Z + z
             background[p * ROWS : (p + 1) * ROWS, :] = looked_up(kind, entries, channel)
+    contrast = [contrast_in[0:1, c : c + 1] for c in range(3)]
+    copy.wait()
+
+    def scale(t, carry):
+        for p in range(PLANES):
+            forward[t, p] = contrast[p // Z] * fetched[t, p].astype(jnp.float32)
+        return carry
+
+    lax.fori_loop(0, STEPS, scale, 0)
 
 
 def looked_up(kind, entries, channel):
@@ -418,7 +432,7 @@
             h_out[p * ROWS : (p + 1) * ROWS, :] = (old if scale == 1.0 else scale * old) - curl
 
 
-def planes_electric(e_all, h_all, inverse, strip_h, stored_at, contrast, gained, e_out, stride):
+def planes_electric(e_all, h_all, inverse, strip_h, stored_at, gained, e_out, stride):
     lane = lanes(ROWS)
     last, first = lane == 127, lane == 0
     mixed = jnp.where((lane & 15) == 3, strip_h[2], roll(strip_h[0], -1))
@@ -441,7 +455,7 @@
                 + plane_of(inverse, channel, z, stride) * curl[:stride]
             )
             e_out[p * stride : (p + 1) * stride, :] = value
-            total = total + contrast[channel] * (value[:OWN] * stored_at(p).astype(jnp.float32))
+            total = total + value[:OWN] * stored_at(p)
         l = z // 2
         gained[l * OWN : (l + 1) * OWN, :] = gained[l * OWN : (l + 1) * OWN, :] + total
 
@@ -569,16 +583,16 @@
 
         def step(t, carry):
             strip_h = [strip_of(sh, c) for c in range(3)]
+            planes_electric(
+                e_all, h_all, inverse, strip_h, lambda p: forward[t, p], gained,
+                e_all, ROWS,
+            )
             strip_e = strip_electric(
                 [strip_of(se, c) for c in range(3)], strip_h, [strip_of(si, c) for c in range(3)]
             )
             keep(se, strip_e)
+            planes_magnetic(e_all, h_all, h_all, strip_e)
             keep(sh, strip_magnetic(strip_h, strip_e))
-            planes_electric(
-                e_all, h_all, inverse, strip_h, lambda p: forward[t, p], contrast, gained,
-                e_all, ROWS,
-            )
-            planes_magnetic(e_all, h_all, h_all, strip_e)
             return carry
 
         lax.fori_loop(0, STEPS - 1, step, 0)
@@ -586,7 +600,7 @@
             h_final[p * OWN : (p + 1) * OWN, :] = courant * h_all[p * ROWS : p * ROWS + OWN, :]
         planes_electric(
             e_all, h_all, inverse, [strip_of(sh, c) for c in range(3)],
-            lambda p: forward[STEPS - 1, p], contrast, gained, e_final, OWN,
+            lambda p: forward[STEPS - 1, p], gained, e_final, OWN,
         )
         gradient[...] = gradient[...] * gained[...]
 
@@ -639,9 +653,14 @@
     from_left = sent(right, "gy", 1)
     from_right = sent(left, "gy", -1)
     rest = [sent(sums, "gy", m) for m in range(2, devices - 1)]
-    background, local = call(
-        background_kernel, [vmem(PLANES * ROWS, 128), vmem(DZ * ROWS, 256)],
-        [m_all, d_all, mtable, table, local], aliases={4: 1},
+    background, local, forward = call(
+        background_kernel,
+        [vmem(PLANES * ROWS, 128), vmem(DZ * ROWS, 256), vmem(STEPS, PLANES, OWN, 128)],
+        [forward_fields.reshape(STEPS, PLANES, OWN, 128), contrasts, m_all, d_all, mtable, table,
+         local],
+        aliases={6: 1},
+        scratch=[vmem(STEPS, PLANES, OWN, 128, dtype=jnp.bfloat16), pltpu.SemaphoreType.DMA],
+        in_specs=[ANY] + [VM] * 6,
     )
     h_all, se, sh, traits, sums = call(
         first_kernel(count, reach),
@@ -653,7 +672,7 @@
     at = len(rest)
     operands = rest + [
         e_all, h_all, se, sh, traits, sums, d_all, c_all, background, local, table,
-        contrasts, forward_fields.reshape(STEPS, PLANES, OWN, 128),
+        contrasts, forward,
     ]
     outs = call(
         step_kernel(count, reach, at),

time: 18.7 us -> 18.7 us (level)
  waiting for transfers between devices: 4.01 us -> 2.88 us
  Pallas kernels: 5.67 us -> 6.75 us
    ppermute x5, waiting for transfers between devices: 4.01 us -> 2.88 us  [sent(): return lax.ppermute(x, axis, [(i, (i + by) % size) for i in range(size)])]
    pallas_call x7, Pallas kernels: 5.67 us -> 6.75 us  [call(): pl.pallas_call(kernel, out_shape=outs, in_specs=in_specs, out_specs=out_s...]
  transfers between devices with their start and end apart: 5 -> 5, of which waited for: 4 -> 4; matrix products, arithmetic and copies ran while one was open for 0% -> 0% of each run, Pallas kernels for 10% -> 16%
where the time goes in v7:
time: 18.7 us; the launch traced here: 18.5 us
  starting transfers between devices  8.17 us (44%)
  Pallas kernels  6.75 us (36%)
  waiting for transfers between devices  2.88 us (15%)
  between operations  0.69 us (4%)
    ppermute x5, starting transfers between devices, sent(): return lax.ppermute(x, axis, [(i, (i + by) % size) for i in range(size)])  8.17 us
    pallas_call x7, Pallas kernels, call(): pl.pallas_call(kernel, out_shape=outs, in_specs=in_specs, out_specs=out_s...  6.75 us
    ppermute x5, waiting for transfers between devices, sent(): return lax.ppermute(x, axis, [(i, (i + by) % size) for i in range(size)])  2.88 us
  transfers between devices with their start and end apart: 5, of which 4 were waited for; matrix products, arithmetic and copies ran while one was open for 0% of the time, Pallas kernels for 16%

profile of v7, /device:TPU:0, one launch (start us, length us, event | category | flops | bytes accessed | tf_op | source)
XLA Modules:
  0.0 18.5 jit_solution(5248660788428654288)
XLA Ops:
  0.6 1.2 %shard_map.112 = (f32[184,128]{1,0:T(8,128)S(1)}, f32[208,128]{1,0:T(8,128)S(1)}, f32[384,128]{1,0:T(8,128)S(1)}, f32[384,128]{1,0:T(8,128)S(1)}, f32[64,128]{1,...) custom-call(f32[384,128]{1,0:T(8,128)} %bitcast.10, f32[384,128]{1,0:T(8,128)} %bitcast.11, ...), custom_call_target="tpu_custom_call" | custom-call | tf_op jit(solution)/shard_map/pallas_call | solution.py:44
  1.8 3.0 %collective-permute-start.1 = (f32[208,128]{1,0:T(8,128)S(1)}, f32[208,128]{1,0:T(8,128)S(1)}, u32[]{:S(2)}, u32[]{:S(2)}) collective-permute-start(f32[208,128]{1,0:T(8,128)S(1)} %get-tuple-element.48), channel_id=1, source_target_pairs={{0,4},{4,8},{8,12},{12,16},{16,20},{20,24},{24,28},{28,0},{1,5},{5... | collective-permute-start | bytes 319496 | tf_op jit(solution)/shard_map/ppermute | solution.py:69
  4.8 3.1 %collective-permute-start = (f32[184,128]{1,0:T(8,128)S(1)}, f32[184,128]{1,0:T(8,128)S(1)}, u32[]{:S(2)}, u32[]{:S(2)}) collective-permute-start(f32[184,128]{1,0:T(8,128)S(1)} %get-tuple-element.47), channel_id=1, source_target_pairs={{0,28},{4,0},{8,4},{12,8},{16,12},{20,16},{24,20},{28,24},{1,29},{... | collective-permute-start | bytes 282632 | tf_op jit(solution)/shard_map/ppermute | solution.py:69
  7.9 1.1 %shard_map.113 = (f32[136,256]{1,0:T(8,128)S(1)}, f32[3,4]{1,0:T(4,128)S(1)}, f32[1,3]{1,0:T(1,128)S(1)}, f32[576,128]{1,0:T(8,128)S(1)}, f32[576,128]{1,0:T(8,1...) custom-call(f32[136,256]{1,0:T(8,128)} %constant.2.clone.table_in, ...), custom_call_target="tpu_custom_call" | custom-call | tf_op jit(solution)/shard_map/pallas_call | solution.py:44
  9.1 1.9 %collective-permute-done.1.got = f32[208,128]{1,0:T(8,128)S(1)} collective-permute-done((f32[208,128]{1,0:T(8,128)S(1)}, f32[208,128]{1,0:T(8,128)S(1)}, u32[]{:S(2)}, u32[]{:S(2)}) %collective-permute-start.1) | collective-permute-done | bytes 106528 | tf_op jit(solution)/shard_map/ppermute | solution.py:69
  11.0 0.7 %collective-permute-done.got = f32[184,128]{1,0:T(8,128)S(1)} collective-permute-done((f32[184,128]{1,0:T(8,128)S(1)}, f32[184,128]{1,0:T(8,128)S(1)}, u32[]{:S(2)}, u32[]{:S(2)}) %collective-permute-start) | collective-permute-done | bytes 94240 | tf_op jit(solution)/shard_map/ppermute | solution.py:69
  11.7 0.3 %shard_map.115 = (f32[576,128]{1,0:T(8,128)S(1)}, f32[576,128]{1,0:T(8,128)S(1)}, f32[96,128]{1,0:T(8,128)S(1)}, f32[24,128]{1,0:T(8,128)S(1)}, f32[192,128]{1,0...) custom-call(f32[184,128]{1,0:T(8,128)S(1)} %collective-permute-done., ...), custom_call_target="tpu_custom_call", output_to_operand_aliasing={{0}: (1, {}), {1}: (2, {}), {2}: (3, {}), {3}: (4, {}), {4}... | custom-call | tf_op jit(solution)/shard_map/pallas_call | solution.py:44
  12.0 0.1 collective-permute-start.3
  12.1 0.5 %collective-permute-start.4 = (f32[48,128]{1,0:T(8,128)S(1)}, f32[48,128]{1,0:T(8,128)S(1)}, u32[]{:S(2)}, u32[]{:S(2)}) collective-permute-start(f32[48,128]{1,0:T(8,128)S(1)} %get-tuple-element.71), channel_id=1, source_target_pairs={{0,1},{1,2},{2,3},{3,0},{4,5},{5,6},{6,7},{7,4},{8,9},{9,10},{10,1... | collective-permute-start | bytes 73736 | tf_op jit(solution)/shard_map/ppermute | solution.py:69
  12.6 1.5 %collective-permute-start.2 = (f32[8,128]{1,0:T(8,128)S(1)}, f32[8,128]{1,0:T(8,128)S(1)}, u32[]{:S(2)}, u32[]{:S(2)}) collective-permute-start(f32[8,128]{1,0:T(8,128)S(1)} %get-tuple-element.68), channel_id=1, source_target_pairs={{0,2},{1,3},{2,0},{3,1},{4,6},{5,7},{6,4},{7,5},{8,10},{9,11},{10,... | collective-permute-start | bytes 12296 | tf_op jit(solution)/shard_map/ppermute | solution.py:69
  14.1 1.3 %shard_map.117 = (f32[576,128]{1,0:T(8,128)S(1)}, f32[96,256]{1,0:T(8,128)S(1)}, f32[4,24,16,128]{3,2,1,0:T(8,128)S(1)}) custom-call(bf16[4,24,16,128]{3,2,1,0:T(8,128)(2,1)} %bitcast.9, f32[1,3]{1,0:T(1,128)S(1)} %get-tuple-element.82.contrast_in.refs_12_, f32[192,128]{1,0:T(8,128)S(1)} %get-tuple-element.83.m_all, ...), custom_call_target="tpu_custom_call", output_to_operand_aliasing={{1}: (6, {})} | custom-call | tf_op jit(solution)/shard_map/pallas_call | solution.py:44
  15.4 0.0 collective-permute-done.3.from_right
  15.4 0.2 %collective-permute-done.4.from_left = f32[48,128]{1,0:T(8,128)S(1)} collective-permute-done((f32[48,128]{1,0:T(8,128)S(1)}, f32[48,128]{1,0:T(8,128)S(1)}, u32[]{:S(2)}, u32[]{:S(2)}) %collective-permute-start.4) | collective-permute-done | bytes 24608 | tf_op jit(solution)/shard_map/ppermute | solution.py:69
  15.6 0.5 %shard_map.116 = (f32[576,128]{1,0:T(8,128)S(1)}, f32[72,128]{1,0:T(8,128)S(1)}, f32[72,128]{1,0:T(8,128)S(1)}, f32[120,128]{1,0:T(8,128)S(1)}, f32[24,128]{1,0:T(8,128)S(1)}) custom-call(f32[48,128]{1,0:T(8,128)S(1)} %collective-permute-done.3.from_right, f32[48,128]{1,0:T(8,128)S(1)} %collective-permute-done.4.from_left, ...), custom_call_target="tpu_custom_call", output_to_operand_aliasing={{0}: (4, {})} | custom-call | tf_op jit(solution)/shard_map/pallas_call | solution.py:44
  16.1 0.1 collective-permute-done.2.refs_0_
  16.2 2.3 %shard_map.118 = (f32[384,128]{1,0:T(8,128)}, f32[384,128]{1,0:T(8,128)}, f32[64,128]{1,0:T(8,128)}, f32[576,128]{1,0:T(8,128)S(1)}, f32[576,128]{1,0:T(8,128)S(...) custom-call(f32[8,128]{1,0:T(8,128)S(1)} %collective-permute-done.2., ...), custom_call_target="tpu_custom_call", output_to_operand_aliasing={{3}: (1, {}), {4}: (2, {}), {5}: (3, {}), {6}: (4, {})} | custom-call | tf_op jit(solution)/shard_map/pallas_call | solution.py:44
  (1 shorter events, 0.0 us)
Async XLA Ops:
  1.8 9.1 %collective-permute-start.1 = (f32[208,128]{1,0:T(8,128)S(1)}, f32[208,128]{1,0:T(8,128)S(1)}, u32[]{:S(2)}, u32[]{:S(2)}) collective-permute-start(f32[208,128]{1,0:T(8,128)S(1)} %get-tuple-element.48), channel_id=1, source_target_pairs={{0,4},{4,8},{8,12},{12,16},{16,20},{20,24},{24,28},{28,0},{1,5},{5... | collective-permute-start | bytes 319496 | tf_op jit(solution)/shard_map/ppermute | solution.py:69
  4.8 6.9 %collective-permute-start = (f32[184,128]{1,0:T(8,128)S(1)}, f32[184,128]{1,0:T(8,128)S(1)}, u32[]{:S(2)}, u32[]{:S(2)}) collective-permute-start(f32[184,128]{1,0:T(8,128)S(1)} %get-tuple-element.47), channel_id=1, source_target_pairs={{0,28},{4,0},{8,4},{12,8},{16,12},{20,16},{24,20},{28,24},{1,29},{... | collective-permute-start | bytes 282632 | tf_op jit(solution)/shard_map/ppermute | solution.py:69
  12.0 3.4 %collective-permute-start.3 = (f32[48,128]{1,0:T(8,128)S(1)}, f32[48,128]{1,0:T(8,128)S(1)}, u32[]{:S(2)}, u32[]{:S(2)}) collective-permute-start(f32[48,128]{1,0:T(8,128)S(1)} %get-tuple-element.70), channel_id=1, source_target_pairs={{0,3},{1,0},{2,1},{3,2},{4,7},{5,4},{6,5},{7,6},{8,11},{9,8},{10,9... | collective-permute-start | bytes 73736 | tf_op jit(solution)/shard_map/ppermute | solution.py:69
  12.1 3.5 %collective-permute-start.4 = (f32[48,128]{1,0:T(8,128)S(1)}, f32[48,128]{1,0:T(8,128)S(1)}, u32[]{:S(2)}, u32[]{:S(2)}) collective-permute-start(f32[48,128]{1,0:T(8,128)S(1)} %get-tuple-element.71), channel_id=1, source_target_pairs={{0,1},{1,2},{2,3},{3,0},{4,5},{5,6},{6,7},{7,4},{8,9},{9,10},{10,1... | collective-permute-start | bytes 73736 | tf_op jit(solution)/shard_map/ppermute | solution.py:69
  12.6 3.6 %collective-permute-start.2 = (f32[8,128]{1,0:T(8,128)S(1)}, f32[8,128]{1,0:T(8,128)S(1)}, u32[]{:S(2)}, u32[]{:S(2)}) collective-permute-start(f32[8,128]{1,0:T(8,128)S(1)} %get-tuple-element.68), channel_id=1, source_target_pairs={{0,2},{1,3},{2,0},{3,1},{4,6},{5,7},{6,4},{7,5},{8,10},{9,11},{10,... | collective-permute-start | bytes 12296 | tf_op jit(solution)/shard_map/ppermute | solution.py:69

commit v8 on v6

--- a/solution.py
+++ b/solution.py
@@ -569,16 +569,16 @@
 
         def step(t, carry):
             strip_h = [strip_of(sh, c) for c in range(3)]
-            strip_e = strip_electric(
-                [strip_of(se, c) for c in range(3)], strip_h, [strip_of(si, c) for c in range(3)]
-            )
-            keep(se, strip_e)
-            keep(sh, strip_magnetic(strip_h, strip_e))
             planes_electric(
                 e_all, h_all, inverse, strip_h, lambda p: forward[t, p], contrast, gained,
                 e_all, ROWS,
             )
+            strip_e = strip_electric(
+                [strip_of(se, c) for c in range(3)], strip_h, [strip_of(si, c) for c in range(3)]
+            )
+            keep(se, strip_e)
             planes_magnetic(e_all, h_all, h_all, strip_e)
+            keep(sh, strip_magnetic(strip_h, strip_e))
             return carry
 
         lax.fori_loop(0, STEPS - 1, step, 0)

time: 18.7 us -> 18.7 us (level)
  no operation moved by 1% of the time
where the time goes in v8:
time: 18.7 us; the launch traced here: 18.5 us
  starting transfers between devices  8.17 us (44%)
  Pallas kernels  5.63 us (30%)
  waiting for transfers between devices  4.01 us (21%)
  between operations  0.7 us (4%)
    ppermute x5, starting transfers between devices, sent(): return lax.ppermute(x, axis, [(i, (i + by) % size) for i in range(size)])  8.17 us
    pallas_call x7, Pallas kernels, call(): pl.pallas_call(kernel, out_shape=outs, in_specs=in_specs, out_specs=out_s...  5.63 us
    ppermute x5, waiting for transfers between devices, sent(): return lax.ppermute(x, axis, [(i, (i + by) % size) for i in range(size)])  4.01 us
  transfers between devices with their start and end apart: 5, of which 4 were waited for; matrix products, arithmetic and copies ran while one was open for 0% of the time, Pallas kernels for 10%

profile of v8, /device:TPU:0, one launch (start us, length us, event | category | flops | bytes accessed | tf_op | source)
XLA Modules:
  0.0 18.5 jit_solution(10707144290019779053)
XLA Ops:
  0.6 1.2 %shard_map.112 = (f32[184,128]{1,0:T(8,128)S(1)}, f32[208,128]{1,0:T(8,128)S(1)}, f32[384,128]{1,0:T(8,128)S(1)}, f32[384,128]{1,0:T(8,128)S(1)}, f32[64,128]{1,...) custom-call(f32[384,128]{1,0:T(8,128)} %bitcast.10, f32[384,128]{1,0:T(8,128)} %bitcast.11, ...), custom_call_target="tpu_custom_call" | custom-call | tf_op jit(solution)/shard_map/pallas_call | solution.py:44
  1.8 3.0 %collective-permute-start.1 = (f32[208,128]{1,0:T(8,128)S(1)}, f32[208,128]{1,0:T(8,128)S(1)}, u32[]{:S(2)}, u32[]{:S(2)}) collective-permute-start(f32[208,128]{1,0:T(8,128)S(1)} %get-tuple-element.47), channel_id=1, source_target_pairs={{0,4},{4,8},{8,12},{12,16},{16,20},{20,24},{24,28},{28,0},{1,5},{5... | collective-permute-start | bytes 319496 | tf_op jit(solution)/shard_map/ppermute | solution.py:69
  4.8 3.1 %collective-permute-start = (f32[184,128]{1,0:T(8,128)S(1)}, f32[184,128]{1,0:T(8,128)S(1)}, u32[]{:S(2)}, u32[]{:S(2)}) collective-permute-start(f32[184,128]{1,0:T(8,128)S(1)} %get-tuple-element.46), channel_id=1, source_target_pairs={{0,28},{4,0},{8,4},{12,8},{16,12},{20,16},{24,20},{28,24},{1,29},{... | collective-permute-start | bytes 282632 | tf_op jit(solution)/shard_map/ppermute | solution.py:69
  7.9 1.1 %shard_map.113 = (f32[136,256]{1,0:T(8,128)S(1)}, f32[3,4]{1,0:T(4,128)S(1)}, f32[1,3]{1,0:T(1,128)S(1)}, f32[576,128]{1,0:T(8,128)S(1)}, f32[576,128]{1,0:T(8,1...) custom-call(f32[136,256]{1,0:T(8,128)} %constant.2.clone.table_in, ...), custom_call_target="tpu_custom_call" | custom-call | tf_op jit(solution)/shard_map/pallas_call | solution.py:44
  9.1 1.9 %collective-permute-done.1.got = f32[208,128]{1,0:T(8,128)S(1)} collective-permute-done((f32[208,128]{1,0:T(8,128)S(1)}, f32[208,128]{1,0:T(8,128)S(1)}, u32[]{:S(2)}, u32[]{:S(2)}) %collective-permute-start.1) | collective-permute-done | bytes 106528 | tf_op jit(solution)/shard_map/ppermute | solution.py:69
  11.0 0.7 %collective-permute-done.got = f32[184,128]{1,0:T(8,128)S(1)} collective-permute-done((f32[184,128]{1,0:T(8,128)S(1)}, f32[184,128]{1,0:T(8,128)S(1)}, u32[]{:S(2)}, u32[]{:S(2)}) %collective-permute-start) | collective-permute-done | bytes 94240 | tf_op jit(solution)/shard_map/ppermute | solution.py:69
  11.7 0.3 %shard_map.115 = (f32[576,128]{1,0:T(8,128)S(1)}, f32[576,128]{1,0:T(8,128)S(1)}, f32[96,128]{1,0:T(8,128)S(1)}, f32[24,128]{1,0:T(8,128)S(1)}, f32[192,128]{1,0...) custom-call(f32[184,128]{1,0:T(8,128)S(1)} %collective-permute-done., ...), custom_call_target="tpu_custom_call", output_to_operand_aliasing={{0}: (1, {}), {1}: (2, {}), {2}: (3, {}), {3}: (4, {}), {4}... | custom-call | tf_op jit(solution)/shard_map/pallas_call | solution.py:44
  12.0 0.1 collective-permute-start.3
  12.1 0.5 %collective-permute-start.4 = (f32[48,128]{1,0:T(8,128)S(1)}, f32[48,128]{1,0:T(8,128)S(1)}, u32[]{:S(2)}, u32[]{:S(2)}) collective-permute-start(f32[48,128]{1,0:T(8,128)S(1)} %get-tuple-element.70), channel_id=1, source_target_pairs={{0,1},{1,2},{2,3},{3,0},{4,5},{5,6},{6,7},{7,4},{8,9},{9,10},{10,1... | collective-permute-start | bytes 73736 | tf_op jit(solution)/shard_map/ppermute | solution.py:69
  12.6 1.5 %collective-permute-start.2 = (f32[8,128]{1,0:T(8,128)S(1)}, f32[8,128]{1,0:T(8,128)S(1)}, u32[]{:S(2)}, u32[]{:S(2)}) collective-permute-start(f32[8,128]{1,0:T(8,128)S(1)} %get-tuple-element.67), channel_id=1, source_target_pairs={{0,2},{1,3},{2,0},{3,1},{4,6},{5,7},{6,4},{7,5},{8,10},{9,11},{10,... | collective-permute-start | bytes 12296 | tf_op jit(solution)/shard_map/ppermute | solution.py:69
  14.1 0.2 %shard_map.117 = (f32[576,128]{1,0:T(8,128)S(1)}, f32[96,256]{1,0:T(8,128)S(1)}) custom-call(f32[192,128]{1,0:T(8,128)S(1)} %get-tuple-element.81.m_all, f32[96,128]{1,0:T(8,128)S(1)} %get-tuple-element.79.d_all.refs_7_, f32[3,4]{1,0:T(4,128)S(1)} %get-tuple-element.73.mtable, ...), custom_call_target="tpu_custom_call", output_to_operand_aliasing={{1}: (4, {})} | custom-call | tf_op jit(solution)/shard_map/pallas_call | solution.py:44
  14.3 0.0 copy-start
  14.3 0.0 collective-permute-done.3.from_right
  14.3 1.3 %collective-permute-done.4.from_left = f32[48,128]{1,0:T(8,128)S(1)} collective-permute-done((f32[48,128]{1,0:T(8,128)S(1)}, f32[48,128]{1,0:T(8,128)S(1)}, u32[]{:S(2)}, u32[]{:S(2)}) %collective-permute-start.4) | collective-permute-done | bytes 24608 | tf_op jit(solution)/shard_map/ppermute | solution.py:69
  15.6 0.5 %shard_map.116 = (f32[576,128]{1,0:T(8,128)S(1)}, f32[72,128]{1,0:T(8,128)S(1)}, f32[72,128]{1,0:T(8,128)S(1)}, f32[120,128]{1,0:T(8,128)S(1)}, f32[24,128]{1,0:T(8,128)S(1)}) custom-call(f32[48,128]{1,0:T(8,128)S(1)} %collective-permute-done.3.from_right, f32[48,128]{1,0:T(8,128)S(1)} %collective-permute-done.4.from_left, ...), custom_call_target="tpu_custom_call", output_to_operand_aliasing={{0}: (4, {})} | custom-call | tf_op jit(solution)/shard_map/pallas_call | solution.py:44
  16.1 0.1 collective-permute-done.2.refs_0_
  16.2 0.0 copy-done
  16.2 2.3 %shard_map.118 = (f32[384,128]{1,0:T(8,128)}, f32[384,128]{1,0:T(8,128)}, f32[64,128]{1,0:T(8,128)}, f32[576,128]{1,0:T(8,128)S(1)}, f32[576,128]{1,0:T(8,128)S(...) custom-call(f32[8,128]{1,0:T(8,128)S(1)} %collective-permute-done.2., ...), custom_call_target="tpu_custom_call", output_to_operand_aliasing={{3}: (1, {}), {4}: (2, {}), {5}: (3, {}), {6}: (4, {})} | custom-call | tf_op jit(solution)/shard_map/pallas_call | solution.py:44
  (1 shorter events, 0.0 us)
Async XLA Ops:
  1.8 9.1 %collective-permute-start.1 = (f32[208,128]{1,0:T(8,128)S(1)}, f32[208,128]{1,0:T(8,128)S(1)}, u32[]{:S(2)}, u32[]{:S(2)}) collective-permute-start(f32[208,128]{1,0:T(8,128)S(1)} %get-tuple-element.47), channel_id=1, source_target_pairs={{0,4},{4,8},{8,12},{12,16},{16,20},{20,24},{24,28},{28,0},{1,5},{5... | collective-permute-start | bytes 319496 | tf_op jit(solution)/shard_map/ppermute | solution.py:69
  4.8 6.9 %collective-permute-start = (f32[184,128]{1,0:T(8,128)S(1)}, f32[184,128]{1,0:T(8,128)S(1)}, u32[]{:S(2)}, u32[]{:S(2)}) collective-permute-start(f32[184,128]{1,0:T(8,128)S(1)} %get-tuple-element.46), channel_id=1, source_target_pairs={{0,28},{4,0},{8,4},{12,8},{16,12},{20,16},{24,20},{28,24},{1,29},{... | collective-permute-start | bytes 282632 | tf_op jit(solution)/shard_map/ppermute | solution.py:69
  12.0 2.3 %collective-permute-start.3 = (f32[48,128]{1,0:T(8,128)S(1)}, f32[48,128]{1,0:T(8,128)S(1)}, u32[]{:S(2)}, u32[]{:S(2)}) collective-permute-start(f32[48,128]{1,0:T(8,128)S(1)} %get-tuple-element.69), channel_id=1, source_target_pairs={{0,3},{1,0},{2,1},{3,2},{4,7},{5,4},{6,5},{7,6},{8,11},{9,8},{10,9... | collective-permute-start | bytes 73736 | tf_op jit(solution)/shard_map/ppermute | solution.py:69
  12.1 3.5 %collective-permute-start.4 = (f32[48,128]{1,0:T(8,128)S(1)}, f32[48,128]{1,0:T(8,128)S(1)}, u32[]{:S(2)}, u32[]{:S(2)}) collective-permute-start(f32[48,128]{1,0:T(8,128)S(1)} %get-tuple-element.70), channel_id=1, source_target_pairs={{0,1},{1,2},{2,3},{3,0},{4,5},{5,6},{6,7},{7,4},{8,9},{9,10},{10,1... | collective-permute-start | bytes 73736 | tf_op jit(solution)/shard_map/ppermute | solution.py:69
  12.6 3.6 %collective-permute-start.2 = (f32[8,128]{1,0:T(8,128)S(1)}, f32[8,128]{1,0:T(8,128)S(1)}, u32[]{:S(2)}, u32[]{:S(2)}) collective-permute-start(f32[8,128]{1,0:T(8,128)S(1)} %get-tuple-element.67), channel_id=1, source_target_pairs={{0,2},{1,3},{2,0},{3,1},{4,6},{5,7},{6,4},{7,5},{8,10},{9,11},{10,... | collective-permute-start | bytes 12296 | tf_op jit(solution)/shard_map/ppermute | solution.py:69
  14.3 1.9 %copy-start = (bf16[4,3,8,16,128]{4,3,2,1,0:T(8,128)(2,1)S(1)}, bf16[4,3,8,16,128]{4,3,2,1,0:T(8,128)(2,1)}, u32[]{:S(2)}) copy-start(bf16[4,3,8,16,128]{4,3,2,1,0:T(8,128)(2,1)} %param.16) | copy-start | bytes 1179652
